TPU v7x, 32 devices: a whole 2x2x4 slice. The times are simulated.
32 devices in a mesh: section: 4 (over y, x), coil: 2 (over core), space: 4 (over z).
Axes of the slice: x: 2, y: 2, z: 4, core: 2. Of those that a mesh axis runs over, the one named last changes fastest.
Arguments:
- image: float32 [4, 2, 2, 256, 256], P(None, None, 'coil', 'space'), may hold values from -6 to 6
- sens: bfloat16 [4, 2, 2, 256, 512], P('coil', None, None, 'space'), may hold values from -2 to 2
- adjoint: float32 [4, 2, 2, 256, 256], P(None, None, 'coil', 'space'), may hold values from -6 to 6
- mask_bits: int32 [2, 256, 9], replicated, may hold values from 0 to 1073741823, as said below
- step_size: float32 [4], P('section'), may hold values from 0.3 to 1
- conv1_w: bfloat16 [4, 32, 108], P('section'), may hold values from -0.625 to 0.625
- conv1_b: float32 [4, 32], P('section'), may hold values from -1 to 1
- conv2_w: bfloat16 [4, 32, 108], P('section'), may hold values from -0.125 to 0.125
Outputs:
- cascade_images: float32 [4, 4, 2, 2, 256, 256], P('section', None, None, 'coil', 'space')
Inputs may be any that keep to these rules, and one draw needn't show every extreme that they name: `mask_bits`: bit b of word w in row (p, ky) is 1 where k-space point (ky, 30 w + b) is sampled in phase p; bits for points at or beyond 256 are 0.
All inputs are finite; a program needn't handle non-finite values.
Results may differ from a plain program's by a relative error of at most 0.01.
Values may be sent and summed in bfloat16 or wider, within the bound.
No kernel may reach another device: no remote copies, remote signals or barrier semaphores. Data moves between devices by JAX's collectives and lax.ppermute only.
A program may use at most 128 MiB of HBM per device.

v0:
```python
import math

import jax
import jax.numpy as jnp
from jax import lax
from jax.sharding import PartitionSpec as P


def extended(cells, sides, width):
    for axis, dim in sides:
        count = lax.axis_size(axis)
        ends = count - 1
        head = lax.slice_in_dim(cells, 0, width, axis=dim)
        tail = lax.slice_in_dim(cells, cells.shape[dim] - width, cells.shape[dim], axis=dim)
        cells = jnp.concatenate(
            [
                lax.ppermute(tail, axis, [(i, (i + 1) % count) for i in range(ends)]),
                cells,
                lax.ppermute(head, axis, [((i + 1) % count, i) for i in range(ends)]),
            ],
            axis=dim,
        )
    return cells


def passed_along(value, axis, steps):
    count = lax.axis_size(axis)
    leading, last = (max(0, -steps), min(count, count - steps))
    return lax.ppermute(value, axis, [(source, source + steps) for source in range(leading, last)])


def dft_tables(length):
    index = jnp.arange(length, dtype=jnp.int32)
    product = index[:, None] * index[None, :] % length
    angle = product.astype(jnp.float32) * (2.0 * math.pi / length)
    scale = 1.0 / math.sqrt(length)
    return (
        (jnp.cos(angle) * scale).astype(jnp.bfloat16),
        (jnp.sin(angle) * scale).astype(jnp.bfloat16),
    )


def unpack_mask(mask_bits, length_z):
    column = jnp.arange(length_z, dtype=jnp.int32)
    word_count = mask_bits.shape[2]
    select = (column[:, None] // 30 == jnp.arange(word_count, dtype=jnp.int32)[None, :]).astype(
        jnp.int32
    )
    chosen = jnp.sum(mask_bits[:, :, None, :] * select[None, None], axis=3)
    return (jnp.right_shift(chosen, column % 30) & 1).astype(jnp.float32)


def mult_last(values, table):
    return jnp.einsum("...n,nk->...k", values, table, preferred_element_type=jnp.float32)


def mult_rows(values, table):
    return jnp.einsum("kn,...nz->...kz", table, values, preferred_element_type=jnp.float32)


def along_last(real_part, imag_part, cos_table, sin_table, direction):
    first = mult_last(real_part, cos_table) + direction * mult_last(imag_part, sin_table)
    second = mult_last(imag_part, cos_table) - direction * mult_last(real_part, sin_table)
    return (first, second)


def along_rows(real_part, imag_part, cos_table, sin_table, direction):
    first = mult_rows(real_part, cos_table) + direction * mult_rows(imag_part, sin_table)
    second = mult_rows(imag_part, cos_table) - direction * mult_rows(real_part, sin_table)
    return (first, second)


def correlate(source, weights):
    channels = source.shape[0]
    out_x = source.shape[1] - 2
    out_y = source.shape[2] - 2
    length_z = source.shape[3]
    padded = jnp.pad(source, ((0, 0), (0, 0), (0, 0), (1, 1)))
    result = jnp.zeros((weights.shape[0], out_x, out_y, length_z), jnp.float32)
    for offset_x in range(3):
        pieces = []
        for offset_y in range(3):
            for offset_z in range(3):
                pieces.append(
                    padded[
                        :,
                        offset_x : offset_x + out_x,
                        offset_y : offset_y + out_y,
                        offset_z : offset_z + length_z,
                    ]
                )
        patches = jnp.stack(pieces, axis=0).reshape(9 * channels, out_x, out_y, length_z)
        weight_block = weights[:, offset_x * 9 * channels : (offset_x + 1) * 9 * channels]
        result = result + jnp.einsum(
            "ok,kxyz->oxyz", weight_block, patches, preferred_element_type=jnp.float32
        )
    return result


def per_device(image, sens, adjoint, mask_bits, step_size, conv1_w, conv1_b, conv2_w):
    channels = image.shape[0]
    slab_count = image.shape[1]
    row_count = image.shape[3]
    length_z = image.shape[4]
    phases = mask_bits.shape[0]
    length_y = mask_bits.shape[1]
    planes = lax.axis_size("coil")
    spaces = lax.axis_size("space")
    coil_local = sens.shape[0]
    item_count = coil_local * planes * phases
    item_local = item_count // spaces
    hidden_width = conv1_w.shape[1]
    section_index = lax.axis_index("section")
    space_index = lax.axis_index("space")
    sampled = unpack_mask(mask_bits, length_z)
    cos_z, sin_z = dft_tables(length_z)
    cos_y, sin_y = dft_tables(length_y)
    step_rate = step_size[0]
    first_w = conv1_w[0]
    bias_one = conv1_b[0]
    second_w = (
        conv2_w[0]
        .reshape(hidden_width, 27, channels)
        .transpose(2, 1, 0)
        .reshape(channels, 27 * hidden_width)
    )
    item_ids = space_index * item_local + jnp.arange(item_local, dtype=jnp.int32)
    phase_pick = (
        item_ids[:, None] % phases == jnp.arange(phases, dtype=jnp.int32)[None, :]
    ).astype(jnp.float32)
    item_mask = jnp.einsum("kp,pyz->kyz", phase_pick, sampled)

    def cascade(current, slab_index):
        coil_maps = lax.dynamic_index_in_dim(sens, slab_index, 1, keepdims=False)
        coil_maps = coil_maps.reshape(coil_local, planes, row_count, 2, length_z)
        map_re = coil_maps[:, :, :, 0].astype(jnp.float32)[:, :, None]
        map_im = coil_maps[:, :, :, 1].astype(jnp.float32)[:, :, None]
        adjoint_slab = lax.dynamic_index_in_dim(adjoint, slab_index, 1, keepdims=False)
        gathered = lax.all_gather(current.astype(jnp.bfloat16), "coil", axis=1, tiled=True)
        planar = (
            gathered.reshape(phases, 2, planes, row_count, length_z)
            .transpose(2, 0, 1, 3, 4)
            .astype(jnp.float32)
        )
        image_re = planar[:, :, 0][None]
        image_im = planar[:, :, 1][None]
        coil_re = (map_re * image_re - map_im * image_im).astype(jnp.bfloat16)
        coil_im = (map_re * image_im + map_im * image_re).astype(jnp.bfloat16)
        coil_img = jnp.stack([coil_re, coil_im], axis=3).reshape(item_count, 2, row_count, length_z)
        exchanged = lax.all_to_all(coil_img, "space", split_axis=0, concat_axis=2, tiled=True)
        fwd_re, fwd_im = along_last(exchanged[:, 0], exchanged[:, 1], cos_z, sin_z, 1.0)
        spec_re, spec_im = along_rows(
            fwd_re.astype(jnp.bfloat16), fwd_im.astype(jnp.bfloat16), cos_y, sin_y, 1.0
        )
        spec_re = (spec_re * item_mask).astype(jnp.bfloat16)
        spec_im = (spec_im * item_mask).astype(jnp.bfloat16)
        inv_re, inv_im = along_rows(spec_re, spec_im, cos_y, sin_y, -1.0)
        out_re, out_im = along_last(
            inv_re.astype(jnp.bfloat16), inv_im.astype(jnp.bfloat16), cos_z, sin_z, -1.0
        )
        outgoing = jnp.stack([out_re.astype(jnp.bfloat16), out_im.astype(jnp.bfloat16)], axis=1)
        returned_img = lax.all_to_all(outgoing, "space", split_axis=2, concat_axis=0, tiled=True)
        returned_img = returned_img.reshape(
            coil_local, planes, phases, 2, row_count, length_z
        ).astype(jnp.float32)
        back_re = returned_img[:, :, :, 0]
        back_im = returned_img[:, :, :, 1]
        part_re = jnp.sum(map_re * back_re + map_im * back_im, axis=0)
        part_im = jnp.sum(map_re * back_im - map_im * back_re, axis=0)
        partial_value = (
            jnp.stack([part_re, part_im], axis=2)
            .transpose(1, 2, 0, 3, 4)
            .reshape(channels, planes, row_count, length_z)
        )
        shares = lax.psum_scatter(
            partial_value.astype(jnp.bfloat16), "coil", scatter_dimension=1, tiled=True
        ).astype(jnp.float32)
        updated = current - step_rate * (shares - adjoint_slab)
        lifted = updated.astype(jnp.bfloat16)
        widened = extended(lifted, (("coil", 1), ("space", 2)), 1)
        hidden = jnp.maximum(
            correlate(widened, first_w) + bias_one[:, None, None, None], 0.0
        ).astype(jnp.bfloat16)
        hidden_wide = extended(hidden, (("coil", 1), ("space", 2)), 1)
        return updated + correlate(hidden_wide, second_w)

    tick_count = slab_count + lax.axis_size("section") - 1

    def advance(tick_index, loop_state):
        incoming, outputs = loop_state
        offset = tick_index - section_index
        slab_index = jnp.clip(offset, 0, slab_count - 1)
        entering = lax.dynamic_index_in_dim(image, slab_index, 1, keepdims=False)
        current = jnp.where(section_index == 0, entering, incoming)
        finished = cascade(current, slab_index)
        active = (offset >= 0) & (offset < slab_count)
        previous = lax.dynamic_index_in_dim(outputs, slab_index, 1, keepdims=True)
        stored = jnp.where(active, finished[:, None], previous)
        outputs = lax.dynamic_update_slice_in_dim(outputs, stored, slab_index, 1)
        passed = passed_along(finished.astype(jnp.bfloat16), "section", 1).astype(finished.dtype)
        return (passed, outputs)

    initial = (jnp.zeros_like(image[:, 0]), jnp.zeros_like(image))
    last_in, outputs = lax.fori_loop(0, tick_count, advance, initial)
    return outputs[None]


def solution(mesh):
    in_specs = (
        P(None, None, "coil", "space", None),
        P("coil", None, None, "space", None),
        P(None, None, "coil", "space", None),
        P(),
        P("section"),
        P("section", None, None),
        P("section", None),
        P("section", None, None),
    )
    out_specs = P("section", None, None, "coil", "space", None)
    return jax.shard_map(
        per_device, mesh=mesh, in_specs=in_specs, out_specs=out_specs, check_vma=False
    )
```

profile of v0, /device:TPU:0, one launch (start us, length us, event | category | flops | bytes accessed | tf_op | source)
XLA Modules:
  0.0 1036.5 jit_solution(15423953089467877045)
XLA Ops:
  10.2 1019.5 %while.20 = (s32[]{:T(128)}, f32[4,1,64,256]{3,0,2,1:T(4,128)S(1)}, f32[4,2,1,64,256]{4,3,1,0,2:T(8,128)}, pred[]{:T(512)}, s32[]{:T(128)}, /*index=5*/f32[4,2,1...) while((s32[]{:T(128)}, f32[4,1,64,256]{3,0,2,1:T(4,128)S(1)}, ...), condition=%wide.region_5.6_spmd.clone.clone, body=%wide.region_1.5_spmd.clone.clone.sunk | while | flops 1387907712 | bytes 364505152 | solution.py:204
  15.5 20.8 %all_to_all.86 = bf16[8,2,64,256]{3,2,1,0:T(8,128)(2,1)S(1)} all-to-all(bf16[8,2,64,256]{3,2,1,0:T(8,128)(2,1)S(1)} %copy.304), channel_id=1, replica_groups=mesh['section'=4,'coil'=2,'space'=4] {'space'}, dimensions={0} | all-to-all | bytes 1048576 | tf_op jit(solution)/shard_map/while/body/eval_jaxpr/all_to_all | solution.py:150
  56.6 16.6 %all_to_all.87 = bf16[2,2,256,256]{3,0,1,2:T(2,128)(2,1)S(1)} all-to-all(bf16[2,2,256,256]{3,0,1,2:T(2,128)(2,1)S(1)} %copy.306), channel_id=1, replica_groups=mesh['section'=4,'coil'=2,'space'=4] {'space'}, dimensions={2} | all-to-all | bytes 1048576 | tf_op jit(solution)/shard_map/while/body/eval_jaxpr/all_to_all | solution.py:162
  75.3 6.0 reduce-scatter.2.cloned.1.call-done
  90.6 4.5 collective-permute-start.3
  111.5 4.8 collective-permute-start.7
  118.4 5.2 select_maximum_fusion.7
  144.1 13.3 %copy.313 = bf16[9,32,1,64,256]{4,3,1,0,2:T(8,128)(2,1)} copy(bf16[9,32,1,64,256]{4,1,3,2,0:T(8,128)(2,1)} %fusion.424) | data formatting | bytes 18874368 | tf_op jit(solution)/shard_map/while/body/eval_jaxpr/stack | solution.py:92
  157.3 13.5 %copy.314 = bf16[9,32,1,64,256]{4,3,1,0,2:T(8,128)(2,1)} copy(bf16[9,32,1,64,256]{4,1,3,2,0:T(8,128)(2,1)} %copy-done.1) | data formatting | bytes 18874368 | tf_op jit(solution)/shard_map/while/body/eval_jaxpr/stack | solution.py:92
  170.8 8.9 fusion.425
  179.7 5.4 fusion.426
  185.1 13.3 %copy.315 = bf16[9,32,1,64,256]{4,3,1,0,2:T(8,128)(2,1)} copy(bf16[9,32,1,64,256]{4,1,3,2,0:T(8,128)(2,1)} %copy-done) | data formatting | bytes 18874368 | tf_op jit(solution)/shard_map/while/body/eval_jaxpr/stack | solution.py:92
  198.3 8.9 fusion.427
  207.3 3.6 collective-permute-start.8
  218.9 20.5 %all_to_all.86 = bf16[8,2,64,256]{3,2,1,0:T(8,128)(2,1)S(1)} all-to-all(bf16[8,2,64,256]{3,2,1,0:T(8,128)(2,1)S(1)} %copy.304), channel_id=1, replica_groups=mesh['section'=4,'coil'=2,'space'=4] {'space'}, dimensions={0} | all-to-all | bytes 1048576 | tf_op jit(solution)/shard_map/while/body/eval_jaxpr/all_to_all | solution.py:150
  259.5 16.6 %all_to_all.87 = bf16[2,2,256,256]{3,0,1,2:T(2,128)(2,1)S(1)} all-to-all(bf16[2,2,256,256]{3,0,1,2:T(2,128)(2,1)S(1)} %copy.306), channel_id=1, replica_groups=mesh['section'=4,'coil'=2,'space'=4] {'space'}, dimensions={2} | all-to-all | bytes 1048576 | tf_op jit(solution)/shard_map/while/body/eval_jaxpr/all_to_all | solution.py:162
  278.2 6.9 reduce-scatter.2.cloned.1.call-done
  294.4 4.5 collective-permute-start.3
  315.3 4.8 collective-permute-start.7
  322.2 5.2 select_maximum_fusion.7
  347.9 13.3 %copy.313 = bf16[9,32,1,64,256]{4,3,1,0,2:T(8,128)(2,1)} copy(bf16[9,32,1,64,256]{4,1,3,2,0:T(8,128)(2,1)} %fusion.424) | data formatting | bytes 18874368 | tf_op jit(solution)/shard_map/while/body/eval_jaxpr/stack | solution.py:92
  361.1 13.5 %copy.314 = bf16[9,32,1,64,256]{4,3,1,0,2:T(8,128)(2,1)} copy(bf16[9,32,1,64,256]{4,1,3,2,0:T(8,128)(2,1)} %copy-done.1) | data formatting | bytes 18874368 | tf_op jit(solution)/shard_map/while/body/eval_jaxpr/stack | solution.py:92
  374.6 8.9 fusion.425
  383.5 5.4 fusion.426
  388.9 13.3 %copy.315 = bf16[9,32,1,64,256]{4,3,1,0,2:T(8,128)(2,1)} copy(bf16[9,32,1,64,256]{4,1,3,2,0:T(8,128)(2,1)} %copy-done) | data formatting | bytes 18874368 | tf_op jit(solution)/shard_map/while/body/eval_jaxpr/stack | solution.py:92
  402.1 8.9 fusion.427
  422.7 20.5 %all_to_all.86 = bf16[8,2,64,256]{3,2,1,0:T(8,128)(2,1)S(1)} all-to-all(bf16[8,2,64,256]{3,2,1,0:T(8,128)(2,1)S(1)} %copy.304), channel_id=1, replica_groups=mesh['section'=4,'coil'=2,'space'=4] {'space'}, dimensions={0} | all-to-all | bytes 1048576 | tf_op jit(solution)/shard_map/while/body/eval_jaxpr/all_to_all | solution.py:150
  463.3 16.6 %all_to_all.87 = bf16[2,2,256,256]{3,0,1,2:T(2,128)(2,1)S(1)} all-to-all(bf16[2,2,256,256]{3,0,1,2:T(2,128)(2,1)S(1)} %copy.306), channel_id=1, replica_groups=mesh['section'=4,'coil'=2,'space'=4] {'space'}, dimensions={2} | all-to-all | bytes 1048576 | tf_op jit(solution)/shard_map/while/body/eval_jaxpr/all_to_all | solution.py:162
  481.9 6.9 reduce-scatter.2.cloned.1.call-done
  498.2 4.5 collective-permute-start.3
  519.1 4.8 collective-permute-start.7
  526.0 5.2 select_maximum_fusion.7
  551.6 13.3 %copy.313 = bf16[9,32,1,64,256]{4,3,1,0,2:T(8,128)(2,1)} copy(bf16[9,32,1,64,256]{4,1,3,2,0:T(8,128)(2,1)} %fusion.424) | data formatting | bytes 18874368 | tf_op jit(solution)/shard_map/while/body/eval_jaxpr/stack | solution.py:92
  564.9 13.5 %copy.314 = bf16[9,32,1,64,256]{4,3,1,0,2:T(8,128)(2,1)} copy(bf16[9,32,1,64,256]{4,1,3,2,0:T(8,128)(2,1)} %copy-done.1) | data formatting | bytes 18874368 | tf_op jit(solution)/shard_map/while/body/eval_jaxpr/stack | solution.py:92
  578.4 8.9 fusion.425
  587.3 5.4 fusion.426
  592.7 13.3 %copy.315 = bf16[9,32,1,64,256]{4,3,1,0,2:T(8,128)(2,1)} copy(bf16[9,32,1,64,256]{4,1,3,2,0:T(8,128)(2,1)} %copy-done) | data formatting | bytes 18874368 | tf_op jit(solution)/shard_map/while/body/eval_jaxpr/stack | solution.py:92
  605.9 8.9 fusion.427
  614.9 3.6 collective-permute-start.8
  626.5 20.5 %all_to_all.86 = bf16[8,2,64,256]{3,2,1,0:T(8,128)(2,1)S(1)} all-to-all(bf16[8,2,64,256]{3,2,1,0:T(8,128)(2,1)S(1)} %copy.304), channel_id=1, replica_groups=mesh['section'=4,'coil'=2,'space'=4] {'space'}, dimensions={0} | all-to-all | bytes 1048576 | tf_op jit(solution)/shard_map/while/body/eval_jaxpr/all_to_all | solution.py:150
  667.0 16.6 %all_to_all.87 = bf16[2,2,256,256]{3,0,1,2:T(2,128)(2,1)S(1)} all-to-all(bf16[2,2,256,256]{3,0,1,2:T(2,128)(2,1)S(1)} %copy.306), channel_id=1, replica_groups=mesh['section'=4,'coil'=2,'space'=4] {'space'}, dimensions={2} | all-to-all | bytes 1048576 | tf_op jit(solution)/shard_map/while/body/eval_jaxpr/all_to_all | solution.py:162
  685.7 6.9 reduce-scatter.2.cloned.1.call-done
  702.0 4.5 collective-permute-start.3
  722.9 4.8 collective-permute-start.7
  729.8 5.2 select_maximum_fusion.7
  755.4 13.3 %copy.313 = bf16[9,32,1,64,256]{4,3,1,0,2:T(8,128)(2,1)} copy(bf16[9,32,1,64,256]{4,1,3,2,0:T(8,128)(2,1)} %fusion.424) | data formatting | bytes 18874368 | tf_op jit(solution)/shard_map/while/body/eval_jaxpr/stack | solution.py:92
  768.7 13.5 %copy.314 = bf16[9,32,1,64,256]{4,3,1,0,2:T(8,128)(2,1)} copy(bf16[9,32,1,64,256]{4,1,3,2,0:T(8,128)(2,1)} %copy-done.1) | data formatting | bytes 18874368 | tf_op jit(solution)/shard_map/while/body/eval_jaxpr/stack | solution.py:92
  782.1 8.9 fusion.425
  791.0 5.4 fusion.426
  796.4 13.3 %copy.315 = bf16[9,32,1,64,256]{4,3,1,0,2:T(8,128)(2,1)} copy(bf16[9,32,1,64,256]{4,1,3,2,0:T(8,128)(2,1)} %copy-done) | data formatting | bytes 18874368 | tf_op jit(solution)/shard_map/while/body/eval_jaxpr/stack | solution.py:92
  809.7 8.9 fusion.427
  830.2 20.5 %all_to_all.86 = bf16[8,2,64,256]{3,2,1,0:T(8,128)(2,1)S(1)} all-to-all(bf16[8,2,64,256]{3,2,1,0:T(8,128)(2,1)S(1)} %copy.304), channel_id=1, replica_groups=mesh['section'=4,'coil'=2,'space'=4] {'space'}, dimensions={0} | all-to-all | bytes 1048576 | tf_op jit(solution)/shard_map/while/body/eval_jaxpr/all_to_all | solution.py:150
  870.8 16.6 %all_to_all.87 = bf16[2,2,256,256]{3,0,1,2:T(2,128)(2,1)S(1)} all-to-all(bf16[2,2,256,256]{3,0,1,2:T(2,128)(2,1)S(1)} %copy.306), channel_id=1, replica_groups=mesh['section'=4,'coil'=2,'space'=4] {'space'}, dimensions={2} | all-to-all | bytes 1048576 | tf_op jit(solution)/shard_map/while/body/eval_jaxpr/all_to_all | solution.py:162
  889.5 6.9 reduce-scatter.2.cloned.1.call-done
  905.7 4.5 collective-permute-start.3
  926.7 4.8 collective-permute-start.7
  933.6 5.2 select_maximum_fusion.7
  959.2 13.3 %copy.313 = bf16[9,32,1,64,256]{4,3,1,0,2:T(8,128)(2,1)} copy(bf16[9,32,1,64,256]{4,1,3,2,0:T(8,128)(2,1)} %fusion.424) | data formatting | bytes 18874368 | tf_op jit(solution)/shard_map/while/body/eval_jaxpr/stack | solution.py:92
  972.5 13.5 %copy.314 = bf16[9,32,1,64,256]{4,3,1,0,2:T(8,128)(2,1)} copy(bf16[9,32,1,64,256]{4,1,3,2,0:T(8,128)(2,1)} %copy-done.1) | data formatting | bytes 18874368 | tf_op jit(solution)/shard_map/while/body/eval_jaxpr/stack | solution.py:92
  985.9 8.9 fusion.425
  994.8 5.4 fusion.426
  1000.2 13.3 %copy.315 = bf16[9,32,1,64,256]{4,3,1,0,2:T(8,128)(2,1)} copy(bf16[9,32,1,64,256]{4,1,3,2,0:T(8,128)(2,1)} %copy-done) | data formatting | bytes 18874368 | tf_op jit(solution)/shard_map/while/body/eval_jaxpr/stack | solution.py:92
  1013.5 8.9 fusion.427
  1022.4 3.6 collective-permute-start.8
  (583 shorter events, 399.1 us)
Async XLA Ops:
  10.2 35.7 %copy-start.8 = (f32[2,256,256]{1,2,0:T(8,128)}, f32[2,256,256]{1,2,0:T(8,128)S(1)}, u32[]{:S(2)}) copy-start(f32[2,256,256]{1,2,0:T(8,128)S(1)} %get-tuple-element.995) | copy-start | bytes 1572868 | tf_op jit(solution)/shard_map/while
  10.2 71.1 %reduce-scatter.2.cloned.1.call-start = ((), (), s32[]{:S(2)}) async-start(), calls=%async_computation.3 | async-start | bytes 393216 | tf_op jit(solution)/shard_map/while/body/eval_jaxpr/reduce_scatter | solution.py:175
  84.0 4.3 collective-permute-start
  85.3 4.0 collective-permute-start.1
  89.3 5.9 collective-permute-start.2
  90.6 5.9 collective-permute-start.3
  102.8 13.6 %copy-start.4 = (f32[4,2,1,64,256]{4,3,1,0,2:T(8,128)S(1)}, f32[4,2,1,64,256]{4,3,1,0,2:T(8,128)}, u32[]{:S(2)}) copy-start(f32[4,2,1,64,256]{4,3,1,0,2:T(8,128)} %get-tuple-element.973) | copy-start | bytes 1572868 | tf_op jit(solution)/shard_map/while
  102.8 4.7 collective-permute-start.4
  104.2 5.4 collective-permute-start.5
  110.3 6.7 collective-permute-start.6
  111.5 6.9 collective-permute-start.7
  198.3 15.1 %copy-start.9 = (f32[2,256,256]{1,2,0:T(8,128)S(1)}, f32[2,256,256]{1,2,0:T(8,128)}, u32[]{:S(2)}) copy-start(f32[2,256,256]{1,2,0:T(8,128)} %copy-done.8) | copy-start | bytes 1572868 | tf_op jit(solution)/shard_map/while
  207.3 6.1 collective-permute-start.8
  213.7 35.2 %copy-start.8 = (f32[2,256,256]{1,2,0:T(8,128)}, f32[2,256,256]{1,2,0:T(8,128)S(1)}, u32[]{:S(2)}) copy-start(f32[2,256,256]{1,2,0:T(8,128)S(1)} %get-tuple-element.995) | copy-start | bytes 1572868 | tf_op jit(solution)/shard_map/while
  213.7 71.4 %reduce-scatter.2.cloned.1.call-start = ((), (), s32[]{:S(2)}) async-start(), calls=%async_computation.3 | async-start | bytes 393216 | tf_op jit(solution)/shard_map/while/body/eval_jaxpr/reduce_scatter | solution.py:175
  287.8 4.3 collective-permute-start
  289.1 4.0 collective-permute-start.1
  293.1 5.9 collective-permute-start.2
  294.4 5.9 collective-permute-start.3
  306.6 13.6 %copy-start.4 = (f32[4,2,1,64,256]{4,3,1,0,2:T(8,128)S(1)}, f32[4,2,1,64,256]{4,3,1,0,2:T(8,128)}, u32[]{:S(2)}) copy-start(f32[4,2,1,64,256]{4,3,1,0,2:T(8,128)} %get-tuple-element.973) | copy-start | bytes 1572868 | tf_op jit(solution)/shard_map/while
  306.6 4.7 collective-permute-start.4
  308.0 5.4 collective-permute-start.5
  314.1 6.7 collective-permute-start.6
  315.3 6.9 collective-permute-start.7
  402.1 15.1 %copy-start.9 = (f32[2,256,256]{1,2,0:T(8,128)S(1)}, f32[2,256,256]{1,2,0:T(8,128)}, u32[]{:S(2)}) copy-start(f32[2,256,256]{1,2,0:T(8,128)} %copy-done.8) | copy-start | bytes 1572868 | tf_op jit(solution)/shard_map/while
  411.1 6.1 collective-permute-start.8
  417.4 35.2 %copy-start.8 = (f32[2,256,256]{1,2,0:T(8,128)}, f32[2,256,256]{1,2,0:T(8,128)S(1)}, u32[]{:S(2)}) copy-start(f32[2,256,256]{1,2,0:T(8,128)S(1)} %get-tuple-element.995) | copy-start | bytes 1572868 | tf_op jit(solution)/shard_map/while
  417.4 71.4 %reduce-scatter.2.cloned.1.call-start = ((), (), s32[]{:S(2)}) async-start(), calls=%async_computation.3 | async-start | bytes 393216 | tf_op jit(solution)/shard_map/while/body/eval_jaxpr/reduce_scatter | solution.py:175
  491.6 4.3 collective-permute-start
  492.9 4.0 collective-permute-start.1
  496.9 5.9 collective-permute-start.2
  498.2 5.9 collective-permute-start.3
  510.4 4.7 collective-permute-start.4
  511.8 5.4 collective-permute-start.5
  517.8 6.7 collective-permute-start.6
  519.1 6.9 collective-permute-start.7
  605.9 15.1 %copy-start.9 = (f32[2,256,256]{1,2,0:T(8,128)S(1)}, f32[2,256,256]{1,2,0:T(8,128)}, u32[]{:S(2)}) copy-start(f32[2,256,256]{1,2,0:T(8,128)} %copy-done.8) | copy-start | bytes 1572868 | tf_op jit(solution)/shard_map/while
  614.9 6.1 collective-permute-start.8
  621.2 35.2 %copy-start.8 = (f32[2,256,256]{1,2,0:T(8,128)}, f32[2,256,256]{1,2,0:T(8,128)S(1)}, u32[]{:S(2)}) copy-start(f32[2,256,256]{1,2,0:T(8,128)S(1)} %get-tuple-element.995) | copy-start | bytes 1572868 | tf_op jit(solution)/shard_map/while
  621.2 71.4 %reduce-scatter.2.cloned.1.call-start = ((), (), s32[]{:S(2)}) async-start(), calls=%async_computation.3 | async-start | bytes 393216 | tf_op jit(solution)/shard_map/while/body/eval_jaxpr/reduce_scatter | solution.py:175
  695.3 4.3 collective-permute-start
  696.6 4.0 collective-permute-start.1
  700.7 5.9 collective-permute-start.2
  702.0 5.9 collective-permute-start.3
  714.2 13.6 %copy-start.4 = (f32[4,2,1,64,256]{4,3,1,0,2:T(8,128)S(1)}, f32[4,2,1,64,256]{4,3,1,0,2:T(8,128)}, u32[]{:S(2)}) copy-start(f32[4,2,1,64,256]{4,3,1,0,2:T(8,128)} %get-tuple-element.973) | copy-start | bytes 1572868 | tf_op jit(solution)/shard_map/while
  714.2 4.7 collective-permute-start.4
  715.6 5.4 collective-permute-start.5
  721.6 6.7 collective-permute-start.6
  722.9 6.9 collective-permute-start.7
  809.7 15.1 %copy-start.9 = (f32[2,256,256]{1,2,0:T(8,128)S(1)}, f32[2,256,256]{1,2,0:T(8,128)}, u32[]{:S(2)}) copy-start(f32[2,256,256]{1,2,0:T(8,128)} %copy-done.8) | copy-start | bytes 1572868 | tf_op jit(solution)/shard_map/while
  818.6 6.1 collective-permute-start.8
  825.0 35.2 %copy-start.8 = (f32[2,256,256]{1,2,0:T(8,128)}, f32[2,256,256]{1,2,0:T(8,128)S(1)}, u32[]{:S(2)}) copy-start(f32[2,256,256]{1,2,0:T(8,128)S(1)} %get-tuple-element.995) | copy-start | bytes 1572868 | tf_op jit(solution)/shard_map/while
  825.0 71.4 %reduce-scatter.2.cloned.1.call-start = ((), (), s32[]{:S(2)}) async-start(), calls=%async_computation.3 | async-start | bytes 393216 | tf_op jit(solution)/shard_map/while/body/eval_jaxpr/reduce_scatter | solution.py:175
  899.1 4.3 collective-permute-start
  900.4 4.0 collective-permute-start.1
  904.4 5.9 collective-permute-start.2
  905.7 5.9 collective-permute-start.3
  917.9 13.6 %copy-start.4 = (f32[4,2,1,64,256]{4,3,1,0,2:T(8,128)S(1)}, f32[4,2,1,64,256]{4,3,1,0,2:T(8,128)}, u32[]{:S(2)}) copy-start(f32[4,2,1,64,256]{4,3,1,0,2:T(8,128)} %get-tuple-element.973) | copy-start | bytes 1572868 | tf_op jit(solution)/shard_map/while
  918.0 4.7 collective-permute-start.4
  919.4 5.4 collective-permute-start.5
  925.4 6.7 collective-permute-start.6
  926.7 6.9 collective-permute-start.7
  1013.5 15.1 %copy-start.9 = (f32[2,256,256]{1,2,0:T(8,128)S(1)}, f32[2,256,256]{1,2,0:T(8,128)}, u32[]{:S(2)}) copy-start(f32[2,256,256]{1,2,0:T(8,128)} %copy-done.8) | copy-start | bytes 1572868 | tf_op jit(solution)/shard_map/while
  1022.4 6.1 collective-permute-start.8
  (34 other events, 262.5 us)
Sparse Core Ops, SparseCore 0:
  74.5 6.8 reduce-scatter.1
  277.3 7.7 reduce-scatter.1
  481.1 7.7 reduce-scatter.1
  684.9 7.7 reduce-scatter.1
  888.6 7.7 reduce-scatter.1
where the time goes:
time: 1040 us
  local copies, waits for them, and re-layouts  328 us (32%)
  matrix products  227 us (22%)
  blocking collectives  196 us (19%)
  starting transfers between devices  122 us (12%)
  waiting for transfers between devices  77.1 us (7%)
  other arithmetic  67.8 us (7%)
  between operations  13.4 us (1%)
    another operation x45, local copies, waits for them, and re-layouts, correlate(): jnp.stack(pieces, axis=0).reshape(9 * channels, out_x, out_y, length_z)  223 us
    dot_general x30, matrix products, correlate(): jnp.einsum('ok,kxyz->oxyz', weight_block, patches, preferred_element_type...  130 us
    all_to_all x5, blocking collectives, cascade(): lax.all_to_all(coil_img, 'space', split_axis=0, concat_axis=2, tiled=True)  103 us
    all_to_all x5, blocking collectives, cascade(): lax.all_to_all(outgoing, 'space', split_axis=2, concat_axis=0, tiled=True)  83.1 us
    while x175, local copies, waits for them, and re-layouts  79.3 us
    ppermute x20, starting transfers between devices, extended(): lax.ppermute(tail, axis, [(i, (i + 1) % count) for i in range(ends)])  77.8 us
    dot_general x40, matrix products, mult_rows(): jnp.einsum('kn,...nz->...kz', table, values, preferred_element_type=jnp.f...  49.7 us
    dot_general x40, matrix products, mult_last(): jnp.einsum('...n,nk->...k', values, table, preferred_element_type=jnp.flo...  47.4 us
  transfers between devices with their start and end apart: 50, of which 40 were waited for; matrix products, arithmetic and copies ran while one was open for 1% of the time, Pallas kernels for 0%

commit v1 on v0

v1 whole, which is shorter than its diff:
```python
import functools
import math

import jax
import jax.numpy as jnp
from jax import lax
from jax.experimental import pallas as pl
from jax.experimental.pallas import tpu as pltpu
from jax.sharding import Mesh
from jax.sharding import PartitionSpec as P

BF = jnp.bfloat16
F32 = jnp.float32
ROWS = 8
LANES = 128


def dft_tables(length):
    index = jnp.arange(length, dtype=jnp.int32)
    product = index[:, None] * index[None, :] % length
    angle = product.astype(F32) * (2.0 * math.pi / length)
    scale = 1.0 / math.sqrt(length)
    return (jnp.cos(angle) * scale).astype(BF), (jnp.sin(angle) * scale).astype(BF)


def block_tables(length):
    cos, sin = dft_tables(length)
    first = jnp.concatenate(
        [jnp.concatenate([cos, -sin], axis=1), jnp.concatenate([sin, cos], axis=1)], axis=0
    )
    second = jnp.concatenate(
        [jnp.concatenate([cos, sin], axis=1), jnp.concatenate([-sin, cos], axis=1)], axis=0
    )
    return first, second


def unpack_mask(mask_bits, length_z):
    column = jnp.arange(length_z, dtype=jnp.int32)
    word_count = mask_bits.shape[2]
    select = (column[:, None] // 30 == jnp.arange(word_count, dtype=jnp.int32)[None, :]).astype(
        jnp.int32
    )
    chosen = jnp.sum(mask_bits[:, :, None, :] * select[None, None], axis=3)
    return (jnp.right_shift(chosen, column % 30) & 1).astype(F32)


def dot(left, right):
    return jnp.dot(left, right, preferred_element_type=F32)


def shifted_lanes(values, step):
    length = values.shape[1]
    lane = lax.broadcasted_iota(jnp.int32, values.shape, 1)
    if step > 0:
        return jnp.where(lane == 0, 0.0, pltpu.roll(values, 1, 1))
    return jnp.where(lane == length - 1, 0.0, pltpu.roll(values, length - 1, 1))


def consistency_kernel(
    phases,
    neighbours,
    step_ref,
    base_ref,
    *refs,
):
    part_refs = refs[:neighbours]
    (
        sens_ref,
        adjoint_ref,
        mask_ref,
        first_z,
        second_z,
        first_y,
        second_y,
        x_ref,
        dc_ref,
        v_ref,
        total,
    ) = refs[neighbours:]
    channels, length_y, length_z = base_ref.shape
    for channel in range(channels):
        value = base_ref[channel].astype(F32)
        for part in part_refs:
            value = value + part[channel].astype(F32)
        x_ref[channel] = value
        total[channel] = -adjoint_ref[channel].astype(F32)

    def coil(index, carry):
        maps = sens_ref[index].astype(F32)
        map_re, map_im = maps[:, :length_z], maps[:, length_z:]
        for phase in range(phases):
            image_re = x_ref[2 * phase].astype(BF).astype(F32)
            image_im = x_ref[2 * phase + 1].astype(BF).astype(F32)
            coil_img = jnp.concatenate(
                [
                    (map_re * image_re - map_im * image_im).astype(BF),
                    (map_re * image_im + map_im * image_re).astype(BF),
                ],
                axis=1,
            )
            kz = dot(coil_img, first_z[...]).astype(BF)
            kz = jnp.concatenate([kz[:, :length_z], kz[:, length_z:]], axis=0)
            spectrum = dot(second_y[...], kz)
            keep = mask_ref[phase]
            spectrum = jnp.concatenate(
                [
                    (spectrum[:length_y] * keep).astype(BF),
                    (spectrum[length_y:] * keep).astype(BF),
                ],
                axis=0,
            )
            back_y = dot(first_y[...], spectrum).astype(BF)
            back_y = jnp.concatenate([back_y[:length_y], back_y[length_y:]], axis=1)
            back = dot(back_y, second_z[...])
            back_re, back_im = back[:, :length_z], back[:, length_z:]
            total[2 * phase] += map_re * back_re + map_im * back_im
            total[2 * phase + 1] += map_re * back_im - map_im * back_re
        return carry

    lax.fori_loop(0, sens_ref.shape[0], coil, 0)
    for channel in range(channels):
        value = x_ref[channel] - step_ref[0] * total[channel]
        dc_ref[channel] = value
        v_ref[channel] = value.astype(BF)


def refine_kernel(
    neighbours,
    width,
    v_ref,
    *refs,
):
    other_refs = refs[:neighbours]
    dc_ref, w1_ref, b1_ref, w2_ref, base_ref = refs[neighbours : neighbours + 5]
    send_refs = refs[neighbours + 5 : 2 * neighbours + 5]
    mixed, hidden = refs[2 * neighbours + 5 :]
    channels, length_y, length_z = v_ref.shape
    tiles, mixed_rows, lanes = mixed.shape
    per_row = mixed_rows // (length_y + 2)
    for tile in range(tiles):
        mixed[tile, 0:per_row, :] = jnp.zeros((per_row, lanes), F32)
        mixed[tile, (length_y + 1) * per_row :, :] = jnp.zeros((per_row, lanes), F32)
    hidden[0:width, :] = jnp.zeros((width, length_z), BF)
    hidden[(length_y + 1) * width :, :] = jnp.zeros((width, length_z), BF)
    sources = [v_ref, *other_refs]
    for at in range(per_row):
        plane, channel = divmod(at, channels)
        if plane < len(sources):
            value = sources[plane][channel].astype(F32)
        else:
            value = jnp.zeros((length_y, length_z), F32)
        for tile in range(tiles):
            mixed[tile, pl.ds(per_row + at, length_y, stride=per_row), :] = value[
                :, tile * lanes : (tile + 1) * lanes
            ]

    def first(block, carry):
        for half in range(2):
            at = block * 2 + half
            start = pl.multiple_of(at * (ROWS * per_row), ROWS * per_row)
            window = jnp.concatenate(
                [mixed[tile, pl.ds(start, (ROWS + 2) * per_row), :] for tile in range(tiles)],
                axis=1,
            )
            taps = jnp.concatenate(
                [
                    shifted_lanes(window, 1).astype(BF),
                    window.astype(BF),
                    shifted_lanes(window, -1).astype(BF),
                ],
                axis=0,
            )
            value = dot(w1_ref[...], taps) + b1_ref[...]
            store = pl.multiple_of((at * ROWS + 1) * width, width)
            hidden[pl.ds(store, ROWS * width), :] = jnp.maximum(value, 0.0).astype(BF)
        return carry

    lax.fori_loop(0, length_y // (2 * ROWS), first, 0)
    block_rows = channels * ROWS

    def second(block, carry):
        results = []
        for half in range(2):
            at = block * 2 + half
            start = pl.multiple_of(at * (ROWS * width), ROWS * width)
            parts = dot(w2_ref[...], hidden[pl.ds(start, (ROWS + 2) * width), :])
            third = parts.shape[0] // 3
            results.append(
                shifted_lanes(parts[:third], 1)
                + parts[third : 2 * third]
                + shifted_lanes(parts[2 * third :], -1)
            )
        rows = pl.ds(pl.multiple_of(block * (2 * ROWS), 2 * ROWS), 2 * ROWS)
        for plane in range(neighbours + 1):
            for channel in range(channels):
                lo = plane * block_rows + channel * ROWS
                value = jnp.concatenate([piece[lo : lo + ROWS] for piece in results], axis=0)
                if plane == 0:
                    base_ref[channel, rows, :] = dc_ref[channel, rows, :] + value
                else:
                    send_refs[plane - 1][channel, rows, :] = value.astype(BF)
        return carry

    lax.fori_loop(0, length_y // (2 * ROWS), second, 0)


def gathered_rows(value, axis, dim):
    count = lax.axis_size(axis)
    index = lax.axis_index(axis)
    size = value.shape[dim]
    shape = list(value.shape)
    shape[dim] = size * count
    whole = jnp.zeros(shape, value.dtype)
    for step in range(count):
        block = value
        if step:
            block = lax.ppermute(value, axis, [(i, (i + step) % count) for i in range(count)])
        whole = lax.dynamic_update_slice_in_dim(
            whole, block, (index - step) % count * size, dim
        )
    return whole


def banded(base, rows):
    taps = base.shape[-2]
    window = rows + taps - 1
    pads = [(0, 0)] * (base.ndim - 2)
    return jnp.stack(
        [jnp.pad(base, (*pads, (row, window - taps - row), (0, 0))) for row in range(rows)], axis=0
    )


def per_device(image, sens, adjoint, mask_bits, step_size, conv1_w, conv1_b, conv2_w):
    channels, slab_count, _, row_count, length_z = image.shape
    phases, length_y = mask_bits.shape[:2]
    planes = lax.axis_size("coil")
    coil_local = sens.shape[0]
    width = conv1_w.shape[1]
    groups = lax.axis_size("group")
    members = lax.axis_size("member")
    cascades = groups * members
    group = lax.axis_index("group")
    member = lax.axis_index("member")
    plane = lax.axis_index("coil")
    section = group * members + member
    first_z, second_z = block_tables(length_z)
    first_y, second_y = (first_z, second_z) if length_y == length_z else block_tables(length_y)
    sampled = unpack_mask(mask_bits, length_z)

    packed = jnp.concatenate(
        [
            conv1_w.reshape(1, -1).astype(F32),
            conv2_w.reshape(1, -1).astype(F32),
            conv1_b.reshape(1, -1),
            step_size.reshape(1, 1),
        ],
        axis=1,
    )
    packed = gathered_rows(gathered_rows(packed, "member", 0), "group", 0)
    taps = conv1_w.shape[2]
    count_w = width * taps
    all_w1 = packed[:, :count_w].reshape(cascades, width, 3, 3, 3, channels)
    all_w2 = packed[:, count_w : 2 * count_w].reshape(cascades, width, 3, 3, 3, channels)
    all_b1 = packed[:, 2 * count_w : 2 * count_w + width]
    steps = packed[:, 2 * count_w + width]

    if planes == 1:
        sides = []
    elif planes == 2:
        sides = [None]
    else:
        sides = [-1, 1]
    neighbours = len(sides)
    involved = neighbours + 1
    per_row = -(-(involved * channels) // 8) * 8

    def tap_of(side, sign):
        if side is None:
            return jnp.where(plane == 0, 1 + sign, 1 - sign)
        return 1 + sign * side

    def weights_of(cascade):
        w1 = all_w1[cascade]
        w2 = all_w2[cascade]
        taken1 = [w1[:, 1]]
        taken2 = [w2[:, 1]]
        for side in sides:
            taken1.append(lax.dynamic_index_in_dim(w1, tap_of(side, 1), 1, keepdims=False))
            taken2.append(lax.dynamic_index_in_dim(w2, tap_of(side, -1), 1, keepdims=False))
        for _ in range(per_row // channels - involved):
            taken1.append(jnp.zeros_like(taken1[0]))
        base1 = jnp.stack(taken1, axis=3)
        base1 = base1.transpose(0, 2, 1, 3, 4).reshape(width, 3, 3, per_row)
        big1 = banded(base1, ROWS)
        big1 = big1.reshape(ROWS * width, 3 * (ROWS + 2) * per_row).astype(BF)
        base2 = jnp.stack(taken2, axis=0)
        base2 = base2.transpose(3, 0, 4, 2, 1)
        big2 = banded(base2, ROWS).transpose(1, 2, 3, 0, 4, 5)
        big2 = big2.reshape(3 * involved * channels * ROWS, (ROWS + 2) * width).astype(BF)
        bias = jnp.tile(all_b1[cascade], ROWS)[:, None]
        return big1, bias, big2

    maps = lax.dynamic_index_in_dim(sens, group, 1, keepdims=False)
    maps = lax.all_to_all(maps, "coil", split_axis=1, concat_axis=0, tiled=True)
    maps = gathered_rows(maps[:, 0], "space", 1)
    own_image = lax.dynamic_index_in_dim(image, group, 1, keepdims=False)[:, 0].astype(BF)
    own_adjoint = lax.dynamic_index_in_dim(adjoint, group, 1, keepdims=False)[:, 0].astype(BF)
    base = gathered_rows(own_image, "space", 1)
    target = gathered_rows(own_adjoint, "space", 1)

    full = jax.ShapeDtypeStruct((channels, length_y, length_z), F32)
    half = jax.ShapeDtypeStruct((channels, length_y, length_z), BF)
    vmem = pl.BlockSpec(memory_space=pltpu.VMEM)
    smem = pl.BlockSpec(memory_space=pltpu.SMEM)
    params = pltpu.CompilerParams(vmem_limit_bytes=56 * 1024 * 1024)

    def consistency(cascade, base, parts):
        return pl.pallas_call(
            functools.partial(consistency_kernel, phases, len(parts)),
            out_shape=(full, full, half),
            in_specs=[smem] + [vmem] * (8 + len(parts)),
            out_specs=(vmem, vmem, vmem),
            scratch_shapes=[pltpu.VMEM((channels, length_y, length_z), F32)],
            compiler_params=params,
        )(
            steps[cascade : cascade + 1],
            base,
            *parts,
            maps,
            target,
            sampled,
            first_z,
            second_z,
            first_y,
            second_y,
        )

    def refine(cascade, value, others, updated):
        big1, bias, big2 = weights_of(cascade)
        return pl.pallas_call(
            functools.partial(refine_kernel, neighbours, width),
            out_shape=(full,) + (half,) * neighbours,
            in_specs=[vmem] * (5 + neighbours),
            out_specs=(vmem,) * (1 + neighbours),
            scratch_shapes=[
                pltpu.VMEM((length_z // LANES, (length_y + 2) * per_row, LANES), F32),
                pltpu.VMEM(((length_y + 2) * width, length_z), BF),
            ],
            compiler_params=params,
        )(value, *others, updated, big1, bias, big2)

    def exchanged(values):
        received = []
        for value, side in zip(values, sides):
            if side is None:
                pairs = [(0, 1), (1, 0)]
            else:
                pairs = [(i, i - side) for i in range(planes) if 0 <= i - side < planes]
            received.append(lax.ppermute(value, "coil", pairs))
        return received

    row_start = lax.axis_index("space") * row_count

    def own_rows(value):
        return lax.dynamic_slice_in_dim(value, row_start, row_count, 1)

    results = []
    parts = []
    for cascade in range(cascades):
        current, updated, value = consistency(cascade, base, parts)
        if cascade:
            results.append(own_rows(current))
        others = exchanged([value] * neighbours)
        base, *sends = refine(cascade, value, others, updated)
        turned = sends[::-1] if neighbours == 2 else sends
        parts = exchanged(turned)[::-1] if neighbours == 2 else exchanged(turned)
    last = own_rows(base)
    for part in parts:
        last = last + own_rows(part).astype(F32)
    results.append(last)

    def result_of(wanted):
        chosen = results[0]
        for cascade in range(1, cascades):
            chosen = jnp.where(wanted == cascade, results[cascade], chosen)
        return chosen

    output = jnp.zeros((channels, slab_count, row_count, length_z), F32)
    for step in range(groups):
        if step == 0:
            chosen = result_of(section)
        else:
            target_group = (group - step) % groups
            chosen = result_of(target_group * members + member).astype(BF)
            chosen = lax.ppermute(
                chosen, "group", [(i, (i - step) % groups) for i in range(groups)]
            ).astype(F32)
        output = lax.dynamic_update_slice_in_dim(
            output, chosen[:, None], (group + step) % groups, 1
        )
    return output[None, :, :, None]


def solution(mesh):
    sections, coils, spaces = mesh.devices.shape
    def run(image, *args):
        groups = image.shape[1]
        fine = Mesh(
            mesh.devices.reshape(groups, sections // groups, coils, spaces),
            ("group", "member", "coil", "space"),
        )
        section = ("group", "member")
        in_specs = (
            P(None, None, "coil", "space", None),
            P("coil", None, None, "space", None),
            P(None, None, "coil", "space", None),
            P(),
            P(section),
            P(section, None, None),
            P(section, None),
            P(section, None, None),
        )
        out_specs = P(section, None, None, "coil", "space", None)
        return jax.shard_map(
            per_device, mesh=fine, in_specs=in_specs, out_specs=out_specs, check_vma=False
        )(image, *args)

    return run
```

time: 1040 us -> 258 us (0.25)
  local copies, waits for them, and re-layouts: 328 us -> 88.9 us
  matrix products: 227 us -> 0 us
  blocking collectives: 196 us -> 4.66 us
  Pallas kernels: 0 us -> 110 us
  starting transfers between devices: 122 us -> 21.7 us
  other arithmetic: 67.8 us -> 8.49 us
  waiting for transfers between devices: 77.1 us -> 19.9 us
  between operations: 13.4 us -> 1.78 us
    dot_general x111 -> x0, matrix products: 227 us -> none  [the longest x30 130 us: correlate(): jnp.einsum('ok,kxyz->oxyz', weight_block, patches, preferred_element_type...]
    another operation x56 -> x75, local copies, waits for them, and re-layouts: 226 us -> 42.5 us  [the longest x48 27.9 us: banded(): jnp.stack([jnp.pad(base, (*pads, (row, window - taps - row), (0, 0))) for...]
    all_to_all x10 -> x1, blocking collectives: 186 us -> 4.66 us  [per_device(): maps = lax.all_to_all(maps, 'coil', split_axis=1, concat_axis=0, tiled=True)]
    pallas_call x0 -> x8, Pallas kernels: none -> 110 us  [the longest x4 56.8 us: refine(): pl.pallas_call(functools.partial(refine_kernel, neighbours, width), out_s...]
    ppermute x45 -> x20, starting transfers between devices: 122 us -> 21.7 us  [the longest x11 18.1 us: gathered_rows(): lax.ppermute(value, axis, [(i, (i + step) % count) for i in range(count)])]
    while x175 -> x0, local copies, waits for them, and re-layouts: 79.3 us -> none
    reduce_scatter x5 -> x0, waiting for transfers between devices: 33.7 us -> none  [cascade(): lax.psum_scatter(partial_value.astype(jnp.bfloat16), 'coil', scatter_dime...]
    concatenate x10 -> x1, other arithmetic: 29 us -> 1.11 us  [block_tables(): jnp.concatenate([jnp.concatenate([cos, sin], axis=1), jnp.concatenate([-s...]
  transfers between devices with their start and end apart: 50 -> 20, of which waited for: 40 -> 8; matrix products, arithmetic and copies ran while one was open for 1% -> 34% of each run, Pallas kernels for 0% -> 0%
where the time goes in v1:
time: 258 us; the launch traced here: 256 us
  Pallas kernels  110 us (43%)
  local copies, waits for them, and re-layouts  88.9 us (34%)
  starting transfers between devices  21.7 us (8%)
  waiting for transfers between devices  19.9 us (8%)
  other arithmetic  8.49 us (3%)
  blocking collectives  4.66 us (2%)
    pallas_call x4, Pallas kernels, refine(): pl.pallas_call(functools.partial(refine_kernel, neighbours, width), out_s...  56.8 us
    pallas_call x4, Pallas kernels, consistency(): pl.pallas_call(functools.partial(consistency_kernel, phases, len(parts)),...  53.4 us
    another operation x48, local copies, waits for them, and re-layouts, banded(): jnp.stack([jnp.pad(base, (*pads, (row, window - taps - row), (0, 0))) for...  27.9 us
    ppermute x11, starting transfers between devices, gathered_rows(): lax.ppermute(value, axis, [(i, (i + step) % count) for i in range(count)])  18.1 us
    ppermute x11, waiting for transfers between devices, gathered_rows(): lax.ppermute(value, axis, [(i, (i + step) % count) for i in range(count)])  13.6 us
    unnamed x95, local copies, waits for them, and re-layouts  12.7 us
    dynamic_update_slice x16, local copies, waits for them, and re-layouts, gathered_rows(): lax.dynamic_update_slice_in_dim(whole, block, (index - step) % count * si...  9.83 us
    convert_element_type x8, local copies, waits for them, and re-layouts, weights_of(): big2.reshape(3 * involved * channels * ROWS, (ROWS + 2) * width).astype(BF)  7.18 us
  transfers between devices with their start and end apart: 20, of which 8 were waited for; matrix products, arithmetic and copies ran while one was open for 34% of the time, Pallas kernels for 0%

profile of v1, /device:TPU:0, one launch (start us, length us, event | category | flops | bytes accessed | tf_op | source)
XLA Modules:
  0.0 255.7 jit_solution(1775602305034148210)
XLA Ops:
  0.0 1.0 copy-done
  1.1 4.7 %all_to_all.15 = bf16[2,2,64,512]{3,2,0,1:T(8,128)(2,1)} all-to-all(bf16[2,2,64,512]{3,2,0,1:T(8,128)(2,1)S(1)} %copy.225), channel_id=1, replica_groups=mesh['group'=2,'member'=2,'coil'=2,'space'=4] {'coil'}, dimensions={1} | all-to-all | bytes 524288 | tf_op jit(solution)/shard_map/all_to_all | solution.py:304
  5.8 3.1 %collective-permute-start.5 = (bf16[4,64,512]{2,1,0:T(8,128)(2,1)}, bf16[4,64,512]{2,1,0:T(8,128)(2,1)}, u32[]{:S(2)}, u32[]{:S(2)}) collective-permute-start(bf16[4,64,512]{2,1,0:T(8,128)(2,1)} %bitcast.9), channel_id=1, source_target_pairs={{0,1},{1,2},{2,3},{3,0},{4,5},{5,6},{6,7},{7,4},{8,9},{9,10},{10,1... | collective-permute-start | bytes 786440 | tf_op jit(solution)/shard_map/ppermute | solution.py:217
  8.8 2.6 %collective-permute-start.6 = (bf16[4,64,512]{2,1,0:T(8,128)(2,1)}, bf16[4,64,512]{2,1,0:T(8,128)(2,1)}, u32[]{:S(2)}, u32[]{:S(2)}) collective-permute-start(bf16[4,64,512]{2,1,0:T(8,128)(2,1)} %bitcast.9), channel_id=1, source_target_pairs={{0,2},{1,3},{2,0},{3,1},{4,6},{5,7},{6,4},{7,5},{8,10},{9,11},{10,... | collective-permute-start | bytes 786440 | tf_op jit(solution)/shard_map/ppermute | solution.py:217
  11.4 1.3 collective-permute-start.7
  13.8 1.5 collective-permute-start
  15.3 1.6 constant_dynamic-update-slice_fusion.35
  17.7 1.1 multiply_convert_fusion
  18.8 1.0 fusion.10
  19.9 1.0 constant_dynamic-update-slice_fusion.39
  22.6 1.1 fusion.1
  23.8 1.6 constant_dynamic-update-slice_fusion.43
  26.0 1.6 collective-permute-start.1
  27.7 2.6 %collective-permute-done.1 = f32[2,6945]{1,0:T(2,128)S(1)} collective-permute-done((f32[2,6945]{1,0:T(2,128)S(1)}, f32[2,6945]{1,0:T(2,128)S(1)}, u32[]{:S(2)}, u32[]{:S(2)}) %collective-permute-start.1) | collective-permute-done | bytes 55592 | tf_op jit(solution)/shard_map/ppermute | solution.py:217
  34.3 1.0 squeeze.49
  35.2 1.0 squeeze.51
  36.4 1.0 squeeze.50
  37.4 1.9 slice_bitcast_fusion.4
  39.3 1.0 copy.232
  40.3 1.0 copy.233
  42.3 1.8 slice_bitcast_fusion.5
  44.1 1.1 copy.228
  45.1 1.0 copy.229
  50.9 1.5 fusion.24
  58.8 1.6 copy.275
  60.3 3.5 %stack.401 = bf16[8,3,2,4,10,32]{5,0,4,3,2,1:T(8,128)(2,1)} concatenate(bf16[1,3,2,4,10,32]{5,0,4,3,2,1:T(2,128)(2,1)S(1)} %copy.268, bf16[1,3,2,4,10,32]{5,0,4,3,2,1:T(2,128)(2,1)S(1)} %copy.269, bf16[1,3,2,4,10,32]{5,0,4,3,2,1:T(2,128)(2,1)S(1)} %copy.270, bf16[1,3,2,4,10,32]{5,0,4,3,2,1:T(2,128)(2,1)S(1)} %copy.271, bf16[1,3,2,4,10,32]{5,0,4,3,2,1:T(2,128)(2,1)S(1)} %copy.272, ...), dimensions={0} | concatenate | bytes 245760 | tf_op jit(solution)/shard_map/stack | solution.py:228
  63.9 1.2 copy.276
  65.1 1.1 convert_element_type.225.refs_4_
  66.2 1.0 copy.262
  67.2 1.0 copy.263
  68.3 1.6 copy.249
  70.7 0.9 copy.234
  76.3 3.5 %stack.357 = bf16[8,3,2,4,10,32]{5,0,4,3,2,1:T(8,128)(2,1)} concatenate(bf16[1,3,2,4,10,32]{5,0,4,3,2,1:T(2,128)(2,1)S(1)} %copy.234, bf16[1,3,2,4,10,32]{5,0,4,3,2,1:T(2,128)(2,1)S(1)} %copy.235, bf16[1,3,2,4,10,32]{5,0,4,3,2,1:T(2,128)(2,1)S(1)} %copy.236, bf16[1,3,2,4,10,32]{5,0,4,3,2,1:T(2,128)(2,1)S(1)} %copy.237, bf16[1,3,2,4,10,32]{5,0,4,3,2,1:T(2,128)(2,1)S(1)} %copy.238, ...), dimensions={0} | concatenate | bytes 245760 | tf_op jit(solution)/shard_map/stack | solution.py:228
  79.8 1.2 copy.242
  81.0 1.1 convert_element_type.219.refs_4_
  82.1 3.5 %collective-permute-start.9 = (bf16[4,64,256]{2,1,0:T(8,128)(2,1)}, bf16[4,64,256]{2,1,0:T(8,128)(2,1)S(1)}, u32[]{:S(2)}, u32[]{:S(2)}) collective-permute-start(bf16[4,64,256]{2,1,0:T(8,128)(2,1)} %get-tuple-element.52), channel_id=1, source_target_pairs={{0,2},{1,3},{2,0},{3,1},{4,6},{5,7},{6,4},{7,5},{8,10},{9,11},{10,... | collective-permute-start | bytes 393224 | tf_op jit(solution)/shard_map/ppermute | solution.py:217
  87.6 6.7 %collective-permute-done.9 = bf16[4,64,256]{2,1,0:T(8,128)(2,1)S(1)} collective-permute-done((bf16[4,64,256]{2,1,0:T(8,128)(2,1)}, bf16[4,64,256]{2,1,0:T(8,128)(2,1)S(1)}, u32[]{:S(2)}, u32[]{:S(2)}) %collective-permute-start.9) | collective-permute-done | bytes 131104 | tf_op jit(solution)/shard_map/ppermute | solution.py:217
  94.3 2.2 collective-permute-start.10
  97.0 1.4 collective-permute-start.4
  98.4 2.1 collective-permute-done.10
  100.5 1.7 collective-permute-done.4
  102.2 1.2 constant_dynamic-update-slice_fusion.38
  103.4 1.0 constant_dynamic-update-slice_fusion.37
  104.4 1.0 constant_dynamic-update-slice_fusion.36.refs_0_.refs_1_
  105.4 1.0 copy-done.1
  106.4 13.3 %shard_map.82 = (f32[4,256,256]{2,1,0:T(8,128)}, f32[4,256,256]{2,1,0:T(8,128)}, bf16[4,256,256]{2,1,0:T(8,128)(2,1)}) custom-call(f32[1]{0:T(128)} %bitcast.4.step_ref, bf16[4,256,256]{2,1,0:T(8,128)(2,1)} %copy-done.3, bf16[4,256,512]{2,1,0:T(8,128)(2,1)} %copy-done.1, bf16[4,256,256]{2,1,0:T(8,128)(2,1)} %copy-done.2, ...), custom_call_target="tpu_custom_call" | custom-call | tf_op jit(solution)/shard_map/pallas_call | solution.py:318
  120.9 1.2 copy.231
  125.6 14.1 %shard_map.83 = (f32[4,256,256]{2,1,0:T(8,128)}, bf16[4,256,256]{2,1,0:T(8,128)(2,1)}) custom-call(bf16[4,256,256]{2,1,0:T(8,128)(2,1)} %get-tuple-element.24.v_ref, bf16[4,256,256]{2,1,0:T(8,128)(2,1)} %copy-done.6, f32[4,256,256]{2,1,0:T(8,128)} %get-tuple-element.25.refs_1_, bf16[256,240]{1,0:T(8,128)(2,1)} %copy.243.refs_2_, ...), custom_call_target="tpu_custom_call" | custom-call | tf_op jit(solution)/shard_map/pallas_call | solution.py:340
  141.2 1.6 stack.379
  143.0 1.1 convert_element_type.222.refs_4_
  145.3 13.4 %shard_map.84 = (f32[4,256,256]{2,1,0:T(8,128)}, f32[4,256,256]{2,1,0:T(8,128)}, bf16[4,256,256]{2,1,0:T(8,128)(2,1)}) custom-call(f32[1]{0:T(128)} %bitcast.3.step_ref, f32[4,256,256]{2,1,0:T(8,128)} %get-tuple-element.26.base_ref, bf16[4,256,256]{2,1,0:T(8,128)(2,1)} %copy-done.5, bf16[4,256,512]{2,1,0:T(8,128)(2,1)} %copy-done.1, ...), custom_call_target="tpu_custom_call" | custom-call | tf_op jit(solution)/shard_map/pallas_call | solution.py:318
  161.6 14.2 %shard_map.85 = (f32[4,256,256]{2,1,0:T(8,128)}, bf16[4,256,256]{2,1,0:T(8,128)(2,1)}) custom-call(bf16[4,256,256]{2,1,0:T(8,128)(2,1)} %get-tuple-element.28.v_ref, bf16[4,256,256]{2,1,0:T(8,128)(2,1)} %copy-done.9, f32[4,256,256]{2,1,0:T(8,128)} %get-tuple-element.29.refs_1_, bf16[256,240]{1,0:T(8,128)(2,1)} %copy.260.refs_2_, ...), custom_call_target="tpu_custom_call" | custom-call | tf_op jit(solution)/shard_map/pallas_call | solution.py:340
  176.4 1.6 collective-permute-done.14.refs_0_
  178.8 13.4 %shard_map.86 = (f32[4,256,256]{2,1,0:T(8,128)}, f32[4,256,256]{2,1,0:T(8,128)}, bf16[4,256,256]{2,1,0:T(8,128)(2,1)}) custom-call(f32[1]{0:T(128)} %bitcast.2.step_ref, f32[4,256,256]{2,1,0:T(8,128)} %get-tuple-element.30.base_ref, bf16[4,256,256]{2,1,0:T(8,128)(2,1)} %copy-done.10, bf16[4,256,512]{2,1,0:T(8,128)(2,1)} %copy-done.1, ...), custom_call_target="tpu_custom_call" | custom-call | tf_op jit(solution)/shard_map/pallas_call | solution.py:318
  195.6 14.4 %shard_map.87 = (f32[4,256,256]{2,1,0:T(8,128)}, bf16[4,256,256]{2,1,0:T(8,128)(2,1)}) custom-call(bf16[4,256,256]{2,1,0:T(8,128)(2,1)} %get-tuple-element.32.v_ref, bf16[4,256,256]{2,1,0:T(8,128)(2,1)} %copy-done.7, f32[4,256,256]{2,1,0:T(8,128)} %get-tuple-element.33.refs_1_, bf16[256,240]{1,0:T(8,128)(2,1)} %copy.277.refs_2_, ...), custom_call_target="tpu_custom_call" | custom-call | tf_op jit(solution)/shard_map/pallas_call | solution.py:340
  211.0 1.6 stack.423
  212.8 1.1 convert_element_type.228.refs_4_
  215.1 13.4 %shard_map.88 = (f32[4,256,256]{2,1,0:T(8,128)}, f32[4,256,256]{2,1,0:T(8,128)}, bf16[4,256,256]{2,1,0:T(8,128)(2,1)}) custom-call(f32[1]{0:T(128)} %bitcast.1.step_ref, f32[4,256,256]{2,1,0:T(8,128)} %get-tuple-element.34.base_ref, bf16[4,256,256]{2,1,0:T(8,128)(2,1)} %copy-done.4, bf16[4,256,512]{2,1,0:T(8,128)(2,1)} %copy-done.1, ...), custom_call_target="tpu_custom_call" | custom-call | tf_op jit(solution)/shard_map/pallas_call | solution.py:318
  231.8 14.1 %shard_map.89 = (f32[4,256,256]{2,1,0:T(8,128)}, bf16[4,256,256]{2,1,0:T(8,128)(2,1)}) custom-call(bf16[4,256,256]{2,1,0:T(8,128)(2,1)} %get-tuple-element.36.v_ref, bf16[4,256,256]{2,1,0:T(8,128)(2,1)} %copy-done.8, f32[4,256,256]{2,1,0:T(8,128)} %get-tuple-element.37.refs_1_, bf16[256,240]{1,0:T(8,128)(2,1)} %copy.294.refs_2_, ...), custom_call_target="tpu_custom_call" | custom-call | tf_op jit(solution)/shard_map/pallas_call | solution.py:340
  246.1 2.0 collective-permute-done.18
  248.1 1.3 select_convert_fusion
  249.3 1.6 collective-permute-start.19
  250.9 1.3 bitcast_dynamic-update-slice_fusion
  252.2 2.7 %collective-permute-done.19 = bf16[4,64,256]{2,1,0:T(8,128)(2,1)S(1)} collective-permute-done((bf16[4,64,256]{2,1,0:T(8,128)(2,1)S(1)}, bf16[4,64,256]{2,1,0:T(8,128)(2,1)S(1)}, u32[]{:S(2)}, u32[]{:S(2)}) %collective-permute-start.19) | collective-permute-done | bytes 131104 | tf_op jit(solution)/shard_map/ppermute | solution.py:395
  (233 shorter events, 49.3 us)
Async XLA Ops:
  0.0 1.0 copy-start
  0.0 12.7 %copy-start.30 = (bf16[1,32,108]{2,1,0:T(8,128)(2,1)S(1)}, bf16[1,32,108]{2,1,0:T(8,128)(2,1)}, u32[]{:S(2)}) copy-start(bf16[1,32,108]{2,1,0:T(8,128)(2,1)} %param.13) | copy-start | bytes 20740
  0.0 12.9 %copy-start.31 = (bf16[1,32,108]{2,1,0:T(8,128)(2,1)S(1)}, bf16[1,32,108]{2,1,0:T(8,128)(2,1)}, u32[]{:S(2)}) copy-start(bf16[1,32,108]{2,1,0:T(8,128)(2,1)} %param.15) | copy-start | bytes 20740
  0.0 13.7 %copy-start.32 = (f32[1,32]{1,0:T(1,128)S(1)}, f32[1,32]{1,0:T(1,128)}, u32[]{:S(2)}) copy-start(f32[1,32]{1,0:T(1,128)} %param.14) | copy-start | bytes 388
  5.8 96.5 %collective-permute-start.5 = (bf16[4,64,512]{2,1,0:T(8,128)(2,1)}, bf16[4,64,512]{2,1,0:T(8,128)(2,1)}, u32[]{:S(2)}, u32[]{:S(2)}) collective-permute-start(bf16[4,64,512]{2,1,0:T(8,128)(2,1)} %bitcast.9), channel_id=1, source_target_pairs={{0,1},{1,2},{2,3},{3,0},{4,5},{5,6},{6,7},{7,4},{8,9},{9,10},{10,1... | collective-permute-start | bytes 786440 | tf_op jit(solution)/shard_map/ppermute | solution.py:217
  8.8 94.6 %collective-permute-start.6 = (bf16[4,64,512]{2,1,0:T(8,128)(2,1)}, bf16[4,64,512]{2,1,0:T(8,128)(2,1)}, u32[]{:S(2)}, u32[]{:S(2)}) collective-permute-start(bf16[4,64,512]{2,1,0:T(8,128)(2,1)} %bitcast.9), channel_id=1, source_target_pairs={{0,2},{1,3},{2,0},{3,1},{4,6},{5,7},{6,4},{7,5},{8,10},{9,11},{10,... | collective-permute-start | bytes 786440 | tf_op jit(solution)/shard_map/ppermute | solution.py:217
  11.4 93.0 %collective-permute-start.7 = (bf16[4,64,512]{2,1,0:T(8,128)(2,1)}, bf16[4,64,512]{2,1,0:T(8,128)(2,1)}, u32[]{:S(2)}, u32[]{:S(2)}) collective-permute-start(bf16[4,64,512]{2,1,0:T(8,128)(2,1)} %bitcast.9), channel_id=1, source_target_pairs={{0,3},{1,0},{2,1},{3,2},{4,7},{5,4},{6,5},{7,6},{8,11},{9,8},{10,9... | collective-permute-start | bytes 786440 | tf_op jit(solution)/shard_map/ppermute | solution.py:217
  13.8 12.0 %collective-permute-start = (f32[1,6945]{1,0:T(1,128)S(1)}, f32[1,6945]{1,0:T(1,128)S(1)}, u32[]{:S(2)}, u32[]{:S(2)}) collective-permute-start(f32[1,6945]{1,0:T(1,128)S(1)} %concatenate.21), channel_id=1, source_target_pairs={{0,8},{8,0},{1,9},{9,1},{2,10},{10,2},{3,11},{11,3},{4,12},{12,4},... | collective-permute-start | bytes 83348 | tf_op jit(solution)/shard_map/ppermute | solution.py:217
  17.0 3.9 %copy-start.29 = (s32[2,256,9]{1,0,2:T(2,128)S(1)}, s32[2,256,9]{1,0,2:T(2,128)}, u32[]{:S(2)}) copy-start(s32[2,256,9]{1,0,2:T(2,128)} %param.11) | copy-start | bytes 55300
  17.0 65.2 %collective-permute-start.8 = (bf16[4,64,256]{2,1,0:T(8,128)(2,1)}, bf16[4,64,256]{2,1,0:T(8,128)(2,1)}, u32[]{:S(2)}, u32[]{:S(2)}) collective-permute-start(bf16[4,64,256]{2,1,0:T(8,128)(2,1)} %get-tuple-element.52), channel_id=1, source_target_pairs={{0,1},{1,2},{2,3},{3,0},{4,5},{5,6},{6,7},{7,4},{8,9},{9,10},{10,1... | collective-permute-start | bytes 393224 | tf_op jit(solution)/shard_map/ppermute | solution.py:217
  26.0 4.2 %collective-permute-start.1 = (f32[2,6945]{1,0:T(2,128)S(1)}, f32[2,6945]{1,0:T(2,128)S(1)}, u32[]{:S(2)}, u32[]{:S(2)}) collective-permute-start(f32[2,6945]{1,0:T(2,128)S(1)} %dynamic_update_slice.57), channel_id=1, source_target_pairs={{0,16},{16,0},{1,17},{17,1},{2,18},{18,2},{3,19},{19,3},{4,20},{20... | collective-permute-start | bytes 166688 | tf_op jit(solution)/shard_map/ppermute | solution.py:217
  30.3 56.3 %collective-permute-start.2 = (bf16[4,64,256]{2,1,0:T(8,128)(2,1)}, bf16[4,64,256]{2,1,0:T(8,128)(2,1)}, u32[]{:S(2)}, u32[]{:S(2)}) collective-permute-start(bf16[4,64,256]{2,1,0:T(8,128)(2,1)} %get-tuple-element.54), channel_id=1, source_target_pairs={{0,1},{1,2},{2,3},{3,0},{4,5},{5,6},{6,7},{7,4},{8,9},{9,10},{10,1... | collective-permute-start | bytes 393224 | tf_op jit(solution)/shard_map/ppermute | solution.py:217
  30.5 0.6 copy-start.12
  44.1 8.3 %copy-start.19 = (bf16[32,1,3,3,4]{4,3,2,1,0:T(4,128)(2,1)S(1)}, bf16[32,1,3,3,4]{4,3,2,1,0:T(4,128)(2,1)}, u32[]{:S(2)}) copy-start(bf16[32,1,3,3,4]{4,3,2,1,0:T(4,128)(2,1)} %get-tuple-element.58) | copy-start | bytes 6916
  44.1 9.1 %copy-start.18 = (bf16[1,32,3,3,4]{4,3,2,1,0:T(4,128)(2,1)S(1)}, bf16[1,32,3,3,4]{4,3,2,1,0:T(4,128)(2,1)}, u32[]{:S(2)}) copy-start(bf16[1,32,3,3,4]{4,3,2,1,0:T(4,128)(2,1)} %get-tuple-element.57) | copy-start | bytes 6916
  47.5 10.1 %copy-start.24 = (bf16[1,3,2,4,10,32]{5,3,1,4,2,0:T(4,128)(2,1)S(1)}, bf16[1,3,2,4,10,32]{5,3,1,4,2,0:T(4,128)(2,1)}, u32[]{:S(2)}) copy-start(bf16[1,3,2,4,10,32]{5,3,1,4,2,0:T(4,128)(2,1)} %get-tuple-element.92) | copy-start | bytes 46084
  48.8 8.9 %copy-start.22 = (bf16[1,3,2,4,10,32]{5,3,1,4,2,0:T(4,128)(2,1)S(1)}, bf16[1,3,2,4,10,32]{5,3,1,4,2,0:T(4,128)(2,1)}, u32[]{:S(2)}) copy-start(bf16[1,3,2,4,10,32]{5,3,1,4,2,0:T(4,128)(2,1)} %get-tuple-element.91) | copy-start | bytes 46084
  63.9 6.1 %copy-start.17 = (bf16[1,32,3,3,4]{4,3,2,1,0:T(4,128)(2,1)S(1)}, bf16[1,32,3,3,4]{4,3,2,1,0:T(4,128)(2,1)}, u32[]{:S(2)}) copy-start(bf16[1,32,3,3,4]{4,3,2,1,0:T(4,128)(2,1)} %get-tuple-element.65) | copy-start | bytes 6916
  66.2 8.2 %copy-start.23 = (bf16[1,3,2,4,10,32]{5,3,1,4,2,0:T(4,128)(2,1)S(1)}, bf16[1,3,2,4,10,32]{5,3,1,4,2,0:T(4,128)(2,1)}, u32[]{:S(2)}) copy-start(bf16[1,3,2,4,10,32]{5,3,1,4,2,0:T(4,128)(2,1)} %get-tuple-element.108) | copy-start | bytes 46084
  70.7 4.8 %copy-start.21 = (bf16[1,3,2,4,10,32]{5,3,1,4,2,0:T(4,128)(2,1)S(1)}, bf16[1,3,2,4,10,32]{5,3,1,4,2,0:T(4,128)(2,1)}, u32[]{:S(2)}) copy-start(bf16[1,3,2,4,10,32]{5,3,1,4,2,0:T(4,128)(2,1)} %get-tuple-element.106) | copy-start | bytes 46084
  70.7 4.9 %copy-start.20 = (bf16[1,3,2,4,10,32]{5,3,1,4,2,0:T(4,128)(2,1)S(1)}, bf16[1,3,2,4,10,32]{5,3,1,4,2,0:T(4,128)(2,1)}, u32[]{:S(2)}) copy-start(bf16[1,3,2,4,10,32]{5,3,1,4,2,0:T(4,128)(2,1)} %get-tuple-element.105) | copy-start | bytes 46084
  82.1 12.1 %collective-permute-start.9 = (bf16[4,64,256]{2,1,0:T(8,128)(2,1)}, bf16[4,64,256]{2,1,0:T(8,128)(2,1)S(1)}, u32[]{:S(2)}, u32[]{:S(2)}) collective-permute-start(bf16[4,64,256]{2,1,0:T(8,128)(2,1)} %get-tuple-element.52), channel_id=1, source_target_pairs={{0,2},{1,3},{2,0},{3,1},{4,6},{5,7},{6,4},{7,5},{8,10},{9,11},{10,... | collective-permute-start | bytes 393224 | tf_op jit(solution)/shard_map/ppermute | solution.py:217
  86.6 10.5 %collective-permute-start.3 = (bf16[4,64,256]{2,1,0:T(8,128)(2,1)}, bf16[4,64,256]{2,1,0:T(8,128)(2,1)S(1)}, u32[]{:S(2)}, u32[]{:S(2)}) collective-permute-start(bf16[4,64,256]{2,1,0:T(8,128)(2,1)} %get-tuple-element.54), channel_id=1, source_target_pairs={{0,2},{1,3},{2,0},{3,1},{4,6},{5,7},{6,4},{7,5},{8,10},{9,11},{10,... | collective-permute-start | bytes 393224 | tf_op jit(solution)/shard_map/ppermute | solution.py:217
  94.3 6.2 %collective-permute-start.10 = (bf16[4,64,256]{2,1,0:T(8,128)(2,1)}, bf16[4,64,256]{2,1,0:T(8,128)(2,1)S(1)}, u32[]{:S(2)}, u32[]{:S(2)}) collective-permute-start(bf16[4,64,256]{2,1,0:T(8,128)(2,1)} %get-tuple-element.52), channel_id=1, source_target_pairs={{0,3},{1,0},{2,1},{3,2},{4,7},{5,4},{6,5},{7,6},{8,11},{9,8},{10,9... | collective-permute-start | bytes 393224 | tf_op jit(solution)/shard_map/ppermute | solution.py:217
  97.0 5.2 %collective-permute-start.4 = (bf16[4,64,256]{2,1,0:T(8,128)(2,1)}, bf16[4,64,256]{2,1,0:T(8,128)(2,1)S(1)}, u32[]{:S(2)}, u32[]{:S(2)}) collective-permute-start(bf16[4,64,256]{2,1,0:T(8,128)(2,1)} %get-tuple-element.54), channel_id=1, source_target_pairs={{0,3},{1,0},{2,1},{3,2},{4,7},{5,4},{6,5},{7,6},{8,11},{9,8},{10,9... | collective-permute-start | bytes 393224 | tf_op jit(solution)/shard_map/ppermute | solution.py:217
  100.5 4.9 %copy-start.2 = (bf16[4,256,256]{2,1,0:T(8,128)(2,1)}, bf16[4,256,256]{2,1,0:T(8,128)(2,1)S(1)}, u32[]{:S(2)}) copy-start(bf16[4,256,256]{2,1,0:T(8,128)(2,1)S(1)} %constant_dynamic-update-slice_fusion.32.refs_1_.refs_2_) | copy-start | bytes 1572868
  102.2 3.2 %copy-start.3 = (bf16[4,256,256]{2,1,0:T(8,128)(2,1)}, bf16[4,256,256]{2,1,0:T(8,128)(2,1)S(1)}, u32[]{:S(2)}) copy-start(bf16[4,256,256]{2,1,0:T(8,128)(2,1)S(1)} %constant_dynamic-update-slice_fusion.40.base_ref) | copy-start | bytes 1572868
  105.4 1.0 copy-start.1
  119.6 5.2 %collective-permute-start.11 = (bf16[4,256,256]{2,1,0:T(8,128)(2,1)}, bf16[4,256,256]{2,1,0:T(8,128)(2,1)S(1)}, u32[]{:S(2)}, u32[]{:S(2)}) collective-permute-start(bf16[4,256,256]{2,1,0:T(8,128)(2,1)} %get-tuple-element.24.v_ref), channel_id=1, source_target_pairs={{0,4},{4,0},{1,5},{5,1},{2,6},{6,2},{3,7},{7,3},{8,12},{12,8},{9,1... | collective-permute-start | bytes 1572872 | tf_op jit(solution)/shard_map/ppermute | solution.py:359
  120.3 4.5 %copy-start.27 = (bf16[32,1,3,3,4]{0,4,3,2,1:T(4,128)(2,1)S(1)}, bf16[32,1,3,3,4]{0,4,3,2,1:T(4,128)(2,1)}, u32[]{:S(2)}) copy-start(bf16[32,1,3,3,4]{0,4,3,2,1:T(4,128)(2,1)} %copy.249) | copy-start | bytes 6916
  120.3 4.5 %copy-start.28 = (bf16[1,32,3,3,4]{1,4,3,2,0:T(4,128)(2,1)S(1)}, bf16[1,32,3,3,4]{1,4,3,2,0:T(4,128)(2,1)}, u32[]{:S(2)}) copy-start(bf16[1,32,3,3,4]{1,4,3,2,0:T(4,128)(2,1)} %copy.250) | copy-start | bytes 6916
  124.8 0.8 copy-start.6
  139.7 4.8 %collective-permute-start.12 = (bf16[4,256,256]{2,1,0:T(8,128)(2,1)}, bf16[4,256,256]{2,1,0:T(8,128)(2,1)S(1)}, u32[]{:S(2)}, u32[]{:S(2)}) collective-permute-start(bf16[4,256,256]{2,1,0:T(8,128)(2,1)} %get-tuple-element.27), channel_id=1, source_target_pairs={{0,4},{4,0},{1,5},{5,1},{2,6},{6,2},{3,7},{7,3},{8,12},{12,8},{9,1... | collective-permute-start | bytes 1572872 | tf_op jit(solution)/shard_map/ppermute | solution.py:359
  142.8 1.3 copy-start.16
  142.8 1.4 copy-start.15
  144.5 0.8 copy-start.5
  158.7 2.1 collective-permute-start.13
  160.8 0.8 copy-start.9
  175.7 2.2 collective-permute-start.14
  178.0 0.8 copy-start.10
  192.2 2.5 collective-permute-start.15
  192.6 2.1 copy-start.25
  192.6 2.1 copy-start.26
  194.8 0.8 copy-start.7
  209.9 4.4 %collective-permute-start.16 = (bf16[4,256,256]{2,1,0:T(8,128)(2,1)}, bf16[4,256,256]{2,1,0:T(8,128)(2,1)S(1)}, u32[]{:S(2)}, u32[]{:S(2)}) collective-permute-start(bf16[4,256,256]{2,1,0:T(8,128)(2,1)} %get-tuple-element.35), channel_id=1, source_target_pairs={{0,4},{4,0},{1,5},{5,1},{2,6},{6,2},{3,7},{7,3},{8,12},{12,8},{9,1... | collective-permute-start | bytes 1572872 | tf_op jit(solution)/shard_map/ppermute | solution.py:359
  212.6 1.3 copy-start.14
  212.6 1.4 copy-start.13
  214.3 0.8 copy-start.4
  228.5 2.5 collective-permute-start.17
  231.0 0.8 copy-start.8
  245.9 2.1 collective-permute-start.18
  249.3 5.6 %collective-permute-start.19 = (bf16[4,64,256]{2,1,0:T(8,128)(2,1)S(1)}, bf16[4,64,256]{2,1,0:T(8,128)(2,1)S(1)}, u32[]{:S(2)}, u32[]{:S(2)}) collective-permute-start(bf16[4,64,256]{2,1,0:T(8,128)(2,1)S(1)} %select_convert_fusion), channel_id=1, source_target_pairs={{0,16},{16,0},{1,17},{17,1},{2,18},{18,2},{3,19},{19,3},{4,20},{20... | collective-permute-start | bytes 393224 | tf_op jit(solution)/shard_map/ppermute | solution.py:395
  252.2 2.7 %copy-start.11 = (f32[1,4,2,1,64,256]{5,4,3,2,1,0:T(8,128)}, f32[1,4,2,1,64,256]{5,4,3,2,1,0:T(8,128)S(1)}, u32[]{:S(2)}) copy-start(f32[1,4,2,1,64,256]{5,4,3,2,1,0:T(8,128)S(1)} %bitcast_dynamic-update-slice_fusion) | copy-start | bytes 1572868

commit v2 on v1

v2 whole, which is shorter than its diff:
```python
import functools
import math

import jax
import jax.numpy as jnp
from jax import lax
from jax.experimental import pallas as pl
from jax.experimental.pallas import tpu as pltpu
from jax.sharding import Mesh
from jax.sharding import PartitionSpec as P

BF = jnp.bfloat16
F32 = jnp.float32
ROWS = 8
UNROLL = 4
LANES = 128


def half_tables(length):
    half = length // 2
    slot = jnp.arange(half, dtype=jnp.int32)
    index = jnp.arange(length, dtype=jnp.int32)
    product = slot[:, None] * index[None, :] % length
    angle = product.astype(F32) * (2.0 * math.pi / length)
    scale = 1.0 / math.sqrt(length)
    odd = (index % 2).astype(F32)[None, :] * scale
    even = scale - odd
    first = slot[:, None] == 0
    cos = jnp.where(first, even, jnp.cos(angle) * scale)
    sin = jnp.where(first, odd, jnp.sin(angle) * scale)
    return jnp.concatenate([cos, sin], axis=0).astype(BF)


def slot_order(length):
    half = length // 2
    slot = jnp.arange(length, dtype=jnp.int32)
    return jnp.where(slot <= half, slot, length + half - slot)


def unpack_mask(mask_bits, length_z):
    half = mask_bits.shape[1] // 2
    mask_bits = jnp.concatenate(
        [mask_bits[:, : half + 1], jnp.flip(mask_bits[:, half + 1 :], axis=1)], axis=1
    )
    column = slot_order(length_z)
    word_count = mask_bits.shape[2]
    chosen = jnp.zeros(mask_bits.shape[:2] + (length_z,), jnp.int32)
    for word in range(word_count):
        chosen = jnp.where(column // 30 == word, mask_bits[:, :, word : word + 1], chosen)
    return (jnp.right_shift(chosen, column % 30) & 1).astype(F32)


def dot(left, right):
    return jnp.dot(left, right, preferred_element_type=F32)


def shifted_lanes(values, step):
    length = values.shape[1]
    lane = lax.broadcasted_iota(jnp.int32, values.shape, 1)
    if step > 0:
        return jnp.where(lane == 0, 0.0, pltpu.roll(values, 1, 1))
    return jnp.where(lane == length - 1, 0.0, pltpu.roll(values, length - 1, 1))


def first_lane(on, other):
    lane = lax.broadcasted_iota(jnp.int32, on.shape, 1)
    return jnp.where(lane == 0, on, other)


def first_row(on, other):
    row = lax.broadcasted_iota(jnp.int32, (8, on.shape[1]), 0)
    return jnp.concatenate([jnp.where(row == 0, on[:8], other[:8]), other[8:]], axis=0)


def spread(cos_re, sin_re, cos_im, sin_im, pick):
    add_re = pick(sin_re, sin_im)
    add_im = pick(sin_im, -sin_re)
    return cos_re + add_re, cos_re - add_re, cos_im + add_im, cos_im - add_im


def folded(plus_re, minus_re, plus_im, minus_im, pick):
    sum_re, odd_re = plus_re + minus_re, plus_re - minus_re
    sum_im, odd_im = plus_im + minus_im, plus_im - minus_im
    return sum_re, pick(odd_re, -odd_im), sum_im, pick(odd_im, odd_re)


def joined(parts, axis):
    return jnp.concatenate([part.astype(BF) for part in parts], axis=axis)


def consistency_kernel(phases, width, cascade, neighbours, place_ref, base_ref, *refs):
    part_refs = refs[:neighbours]
    (
        maps_ref,
        adjoint_ref,
        mask_ref,
        pack_ref,
        table_z,
        table_zt,
        table_y,
        table_yt,
        rows_ref,
        dc_ref,
        v_ref,
        image,
        total,
    ) = refs[neighbours:]
    channels, length_y, length_z = base_ref.shape
    half_y, half_z = length_y // 2, length_z // 2
    for channel in range(channels):
        value = base_ref[channel].astype(F32)
        for part in part_refs:
            value = value + part[channel].astype(F32)
        image[channel] = value
        total[channel] = -adjoint_ref[channel].astype(F32)
    row_count = rows_ref.shape[1]
    start = pl.multiple_of(place_ref[0] * row_count, row_count)
    rows_ref[...] = image[:, pl.ds(start, row_count), :]

    def item(map_re, map_im, phase):
        image_re = image[2 * phase].astype(BF).astype(F32)
        image_im = image[2 * phase + 1].astype(BF).astype(F32)
        coil_img = joined(
            [map_re * image_re - map_im * image_im, map_re * image_im + map_im * image_re], 0
        )
        value = dot(coil_img, table_zt[...])
        kz = joined(
            spread(
                value[:length_y, :half_z],
                value[:length_y, half_z:],
                value[length_y:, :half_z],
                value[length_y:, half_z:],
                first_lane,
            ),
            1,
        )
        value = dot(table_y[...], kz)
        plus_re, minus_re, plus_im, minus_im = spread(
            value[:half_y, :length_z],
            value[half_y:, :length_z],
            value[:half_y, length_z:],
            value[half_y:, length_z:],
            first_row,
        )
        plus = mask_ref[phase, :half_y]
        minus = mask_ref[phase, half_y:]
        even_re, odd_re, even_im, odd_im = folded(
            plus_re * plus, minus_re * minus, plus_im * plus, minus_im * minus, first_row
        )
        spectrum = jnp.concatenate(
            [joined([even_re, even_im], 1), joined([odd_re, odd_im], 1)], axis=0
        )
        value = dot(table_yt[...], spectrum)
        even_re, odd_re, even_im, odd_im = folded(
            value[:, :half_z],
            value[:, half_z:length_z],
            value[:, length_z : length_z + half_z],
            value[:, length_z + half_z :],
            first_lane,
        )
        back = dot(
            jnp.concatenate([joined([even_re, odd_re], 1), joined([even_im, odd_im], 1)], axis=0),
            table_z[...],
        )
        back_re, back_im = back[:length_y], back[length_y:]
        total[2 * phase] += map_re * back_re + map_im * back_im
        total[2 * phase + 1] += map_re * back_im - map_im * back_re

    def coil(index, carry):
        maps = maps_ref[index].astype(F32)
        for phase in range(phases):
            item(maps[:, :length_z], maps[:, length_z:], phase)
        return carry

    lax.fori_loop(0, maps_ref.shape[0], coil, 0)
    step = pack_ref[cascade, 2 * width : 2 * width + 1, 1:2]
    for channel in range(channels):
        value = image[channel] - step * total[channel]
        dc_ref[channel] = value
        v_ref[channel] = value.astype(BF)


def refine_kernel(neighbours, width, cascade, v_ref, *refs):
    other_refs = refs[:neighbours]
    dc_ref, pack_ref, select1_ref, select2_ref, base_ref = refs[neighbours : neighbours + 5]
    send_refs = refs[neighbours + 5 : 2 * neighbours + 5]
    mixed, taps, hidden, weight1, weight2 = refs[2 * neighbours + 5 :]
    channels, length_y, length_z = v_ref.shape
    tiles, mixed_rows, lanes = mixed.shape
    padded = length_y + 2 * ROWS
    per_row = mixed_rows // padded
    count = select1_ref.shape[1]
    bias_at = weight1.shape[1] - 2 * ROWS

    small1 = pack_ref[cascade, :width, :count].astype(BF)
    small2 = pack_ref[cascade, width : 2 * width, :count].astype(BF)
    bias = pack_ref[cascade, 2 * width :, 0:1]
    terms = []
    for _ in range(3):
        terms.append(bias.astype(BF).astype(F32))
        bias = bias - terms[-1]
    for row in range(ROWS):
        value = dot(small1, select1_ref[row])
        column = lax.broadcasted_iota(jnp.int32, value.shape, 1)
        for at, term in enumerate(terms):
            value = jnp.where(column == bias_at + at, term, value)
        weight1[row * width : (row + 1) * width, :] = value.astype(BF)
    repeated = jnp.concatenate([small2] * (ROWS + 2), axis=0)
    shape = weight2.shape
    column = lax.broadcasted_iota(jnp.int32, shape, 1)
    lower = (lax.broadcasted_iota(jnp.int32, shape, 0) & (ROWS - 1)) * width
    value = jnp.zeros(shape, F32)
    for tap in range(3):
        placed = lax.dot_general(
            select2_ref[tap], repeated, (((1,), (1,)), ((), ())), preferred_element_type=F32
        )
        low = lower + tap * width
        value = jnp.where((column >= low) & (column < low + width), placed, value)
    weight2[...] = value.astype(BF)

    for tile in range(tiles):
        mixed[tile, 0:per_row, :] = jnp.zeros((per_row, lanes), F32)
        tail = (length_y + 1) * per_row
        mixed[tile, tail:, :] = jnp.zeros((mixed_rows - tail, lanes), F32)
    hidden[0:width, :] = jnp.zeros((width, length_z), BF)
    hidden[(length_y + 1) * width :, :] = jnp.zeros((width, length_z), BF)
    sources = [v_ref, *other_refs]
    for at in range(per_row):
        plane, channel = divmod(at, channels)
        if plane < len(sources):
            value = sources[plane][channel].astype(F32)
        else:
            value = jnp.zeros((length_y, length_z), F32)
        for tile in range(tiles):
            mixed[tile, pl.ds(per_row + at, length_y, stride=per_row), :] = value[
                :, tile * lanes : (tile + 1) * lanes
            ]

    group = 2 * ROWS

    def build(block, carry):
        start = pl.multiple_of(block * (group * per_row), group * per_row)
        window = jnp.concatenate(
            [mixed[tile, pl.ds(start, group * per_row), :] for tile in range(tiles)], axis=1
        )
        shape = (group, per_row, length_z)
        value = jnp.stack(
            [
                shifted_lanes(window, 1).reshape(shape),
                window.reshape(shape),
                shifted_lanes(window, -1).reshape(shape),
            ],
            axis=1,
        )
        store = pl.multiple_of(block * (group * 3 * per_row), group * 3 * per_row)
        taps[pl.ds(store, group * 3 * per_row), :] = value.reshape(-1, length_z).astype(BF)
        return carry

    lax.fori_loop(0, padded // group, build, 0)
    ones_row = lax.broadcasted_iota(jnp.int32, (2 * ROWS, length_z), 0)
    ones = jnp.where(ones_row < 3, 1.0, 0.0).astype(BF)

    def first(block, carry):
        for part in range(UNROLL):
            at = block * UNROLL + part
            start = pl.multiple_of(at * (ROWS * 3 * per_row), ROWS * 3 * per_row)
            window = jnp.concatenate(
                [taps[pl.ds(start, (ROWS + 2) * 3 * per_row), :], ones], axis=0
            )
            value = dot(weight1[...], window)
            store = pl.multiple_of((at * ROWS + 1) * width, width)
            hidden[pl.ds(store, ROWS * width), :] = jnp.maximum(value, 0.0).astype(BF)
        return carry

    lax.fori_loop(0, length_y // (UNROLL * ROWS), first, 0)
    block_rows = channels * ROWS

    def second(block, carry):
        results = []
        for part in range(UNROLL):
            at = block * UNROLL + part
            start = pl.multiple_of(at * (ROWS * width), ROWS * width)
            parts = dot(weight2[...], hidden[pl.ds(start, (ROWS + 2) * width), :])
            third = parts.shape[0] // 3
            results.append(
                shifted_lanes(parts[:third], 1)
                + parts[third : 2 * third]
                + shifted_lanes(parts[2 * third :], -1)
            )
        span = UNROLL * ROWS
        rows = pl.ds(pl.multiple_of(block * span, span), span)
        for plane in range(neighbours + 1):
            for channel in range(channels):
                lo = plane * block_rows + channel * ROWS
                value = jnp.concatenate([piece[lo : lo + ROWS] for piece in results], axis=0)
                if plane == 0:
                    base_ref[channel, rows, :] = dc_ref[channel, rows, :] + value
                else:
                    send_refs[plane - 1][channel, rows, :] = value.astype(BF)
        return carry

    lax.fori_loop(0, length_y // (UNROLL * ROWS), second, 0)


def gathered_rows(value, axis, dim):
    count = lax.axis_size(axis)
    index = lax.axis_index(axis)
    size = value.shape[dim]
    shape = list(value.shape)
    shape[dim] = size * count
    whole = jnp.zeros(shape, value.dtype)
    for step in range(count):
        block = value
        if step:
            block = lax.ppermute(value, axis, [(i, (i + step) % count) for i in range(count)])
        whole = lax.dynamic_update_slice_in_dim(
            whole, block, (index - step) % count * size, dim
        )
    return whole


def per_device(image, sens, adjoint, mask_bits, step_size, conv1_w, conv1_b, conv2_w):
    channels, slab_count, _, row_count, length_z = image.shape
    phases, length_y = mask_bits.shape[:2]
    planes = lax.axis_size("coil")
    coil_local = sens.shape[0]
    width = conv1_w.shape[1]
    groups = lax.axis_size("group")
    members = lax.axis_size("member")
    cascades = groups * members
    group = lax.axis_index("group")
    member = lax.axis_index("member")
    plane = lax.axis_index("coil")
    section = group * members + member
    table_z = half_tables(length_z)
    table_y = table_z if length_y == length_z else half_tables(length_y)
    tables = (table_z, table_z.T, table_y, table_y.T)
    sampled = unpack_mask(mask_bits, length_z)
    count = conv1_w.shape[2]
    extra = jnp.concatenate(
        [conv1_b.T, jnp.broadcast_to(step_size.reshape(1, 1), (width, 1))], axis=1
    )
    packed = jnp.concatenate(
        [
            jnp.pad(part, ((0, 0), (0, -(-count // LANES) * LANES - part.shape[1])))
            for part in (conv1_w[0].astype(F32), conv2_w[0].astype(F32), extra)
        ],
        axis=0,
    )[None]
    packed = gathered_rows(gathered_rows(packed, "member", 0), "group", 0)

    if planes == 1:
        sides = []
    elif planes == 2:
        sides = [None]
    else:
        sides = [-1, 1]
    neighbours = len(sides)
    involved = neighbours + 1
    per_row = -(-(involved * channels) // 8) * 8

    def tap_of(side, sign):
        if side is None:
            return jnp.where(plane == 0, 1 + sign, 1 - sign)
        return jnp.full((), 1 + sign * side, jnp.int32)

    one = jnp.ones((), jnp.int32)
    planes1 = [one] + [tap_of(side, 1) for side in sides]
    planes2 = [one] + [tap_of(side, -1) for side in sides]
    window = ROWS + 2
    used = window * 3 * per_row
    shape = (ROWS, count, used + 2 * ROWS)
    row = lax.broadcasted_iota(jnp.int32, shape, 0)
    tap = lax.broadcasted_iota(jnp.int32, shape, 1)
    column = lax.broadcasted_iota(jnp.int32, shape, 2)
    slot = column % per_row
    wanted = jnp.full(shape, -1, jnp.int32)
    for at, value in enumerate(planes1):
        wanted = jnp.where(slot // channels == at, value, wanted)
    select1 = (
        (column < used)
        & (tap // (9 * channels) == wanted)
        & (tap // (3 * channels) % 3 == column // (3 * per_row) - row)
        & (tap // channels % 3 == column // per_row % 3)
        & (tap % channels == slot % channels)
    ).astype(BF)
    shape = (3, 3 * involved * channels * ROWS, count)
    row = lax.broadcasted_iota(jnp.int32, shape, 1)
    tap = lax.broadcasted_iota(jnp.int32, shape, 2)
    at_plane = row // (channels * ROWS) % involved
    wanted = jnp.full(shape, -1, jnp.int32)
    for at, value in enumerate(planes2):
        wanted = jnp.where(at_plane == at, value, wanted)
    select2 = (
        (tap // (9 * channels) == wanted)
        & (tap // (3 * channels) % 3 == lax.broadcasted_iota(jnp.int32, shape, 0))
        & (tap // channels % 3 == row // (involved * channels * ROWS))
        & (tap % channels == row // ROWS % channels)
    ).astype(BF)

    maps = lax.dynamic_index_in_dim(sens, group, 1, keepdims=False)
    maps = lax.all_to_all(maps, "coil", split_axis=1, concat_axis=0, tiled=True)
    maps = gathered_rows(maps[:, 0], "space", 1)
    own_image = lax.dynamic_index_in_dim(image, group, 1, keepdims=False)[:, 0].astype(BF)
    own_adjoint = lax.dynamic_index_in_dim(adjoint, group, 1, keepdims=False)[:, 0].astype(BF)
    base = gathered_rows(own_image, "space", 1)
    target = gathered_rows(own_adjoint, "space", 1)

    full = jax.ShapeDtypeStruct((channels, length_y, length_z), F32)
    half = jax.ShapeDtypeStruct((channels, length_y, length_z), BF)
    vmem = pl.BlockSpec(memory_space=pltpu.VMEM)
    smem = pl.BlockSpec(memory_space=pltpu.SMEM)
    params = pltpu.CompilerParams(vmem_limit_bytes=56 * 1024 * 1024)

    place = lax.axis_index("space").reshape(1)
    rows_shape = jax.ShapeDtypeStruct((channels, row_count, length_z), F32)

    def consistency(cascade, base, parts):
        return pl.pallas_call(
            functools.partial(consistency_kernel, phases, width, cascade, len(parts)),
            out_shape=(rows_shape, full, half),
            in_specs=[smem] + [vmem] * (9 + len(parts)),
            out_specs=(vmem, vmem, vmem),
            scratch_shapes=[pltpu.VMEM((channels, length_y, length_z), F32)] * 2,
            compiler_params=params,
        )(place, base, *parts, maps, target, sampled, packed, *tables)

    def refine(cascade, value, others, updated):
        padded = length_y + 2 * ROWS
        return pl.pallas_call(
            functools.partial(refine_kernel, neighbours, width, cascade),
            out_shape=(full,) + (half,) * neighbours,
            in_specs=[vmem] * (5 + neighbours),
            out_specs=(vmem,) * (1 + neighbours),
            scratch_shapes=[
                pltpu.VMEM((length_z // LANES, padded * per_row, LANES), F32),
                pltpu.VMEM((padded * 3 * per_row, length_z), BF),
                pltpu.VMEM(((length_y + 2) * width, length_z), BF),
                pltpu.VMEM((ROWS * width, select1.shape[2]), BF),
                pltpu.VMEM((select2.shape[1], (ROWS + 2) * width), BF),
            ],
            compiler_params=params,
        )(value, *others, updated, packed, select1, select2)

    def exchanged(values):
        received = []
        for value, side in zip(values, sides):
            if side is None:
                pairs = [(0, 1), (1, 0)]
            else:
                pairs = [(i, i - side) for i in range(planes) if 0 <= i - side < planes]
            received.append(lax.ppermute(value, "coil", pairs))
        return received

    row_start = lax.axis_index("space") * row_count

    def own_rows(value):
        return lax.dynamic_slice_in_dim(value, row_start, row_count, 1)

    results = []
    parts = []
    for cascade in range(cascades):
        rows, updated, value = consistency(cascade, base, parts)
        if cascade:
            results.append(rows)
        others = exchanged([value] * neighbours)
        base, *sends = refine(cascade, value, others, updated)
        turned = sends[::-1] if neighbours == 2 else sends
        parts = exchanged(turned)[::-1] if neighbours == 2 else exchanged(turned)
    last = own_rows(base)
    for part in parts:
        last = last + own_rows(part).astype(F32)
    results.append(last)

    def result_of(wanted):
        chosen = results[0]
        for cascade in range(1, cascades):
            chosen = jnp.where(wanted == cascade, results[cascade], chosen)
        return chosen

    output = jnp.zeros((channels, slab_count, row_count, length_z), F32)
    for step in range(groups):
        if step == 0:
            chosen = result_of(section)
        else:
            target_group = (group - step) % groups
            chosen = result_of(target_group * members + member).astype(BF)
            chosen = lax.ppermute(
                chosen, "group", [(i, (i - step) % groups) for i in range(groups)]
            ).astype(F32)
        output = lax.dynamic_update_slice_in_dim(
            output, chosen[:, None], (group + step) % groups, 1
        )
    return output[None, :, :, None]


def solution(mesh):
    sections, coils, spaces = mesh.devices.shape
    def run(image, *args):
        groups = image.shape[1]
        fine = Mesh(
            mesh.devices.reshape(groups, sections // groups, coils, spaces),
            ("group", "member", "coil", "space"),
        )
        section = ("group", "member")
        in_specs = (
            P(None, None, "coil", "space", None),
            P("coil", None, None, "space", None),
            P(None, None, "coil", "space", None),
            P(),
            P(section),
            P(section, None, None),
            P(section, None),
            P(section, None, None),
        )
        out_specs = P(section, None, None, "coil", "space", None)
        return jax.shard_map(
            per_device, mesh=fine, in_specs=in_specs, out_specs=out_specs, check_vma=False
        )(image, *args)

    return run
```

time: 258 us -> 185 us (0.72)
  local copies, waits for them, and re-layouts: 88.9 us -> 16.3 us
  Pallas kernels: 110 us -> 86.9 us
  other arithmetic: 8.49 us -> 22.4 us
  waiting for transfers between devices: 19.9 us -> 33.7 us
    another operation x69 -> x0, local copies, waits for them, and re-layouts: 42.3 us -> none  [the longest x48 27.9 us: banded(): jnp.stack([jnp.pad(base, (*pads, (row, window - taps - row), (0, 0))) for...]
    pallas_call x8, Pallas kernels: 110 us -> 86.9 us  [the longest x4 47.7 us: refine(): pl.pallas_call(functools.partial(refine_kernel, neighbours, width, cascad...]
    convert_element_type x18 -> x0, local copies, waits for them, and re-layouts: 11.8 us -> none  [the longest x8 7.18 us: weights_of(): big2.reshape(3 * involved * channels * ROWS, (ROWS + 2) * width).astype(BF)]
    ppermute x8, waiting for transfers between devices: 3.61 us -> 12.9 us  [exchanged(): received.append(lax.ppermute(value, 'coil', pairs))]
    dynamic_slice x8 -> x0, local copies, waits for them, and re-layouts: 5.86 us -> none  [the longest x4 3.52 us: weights_of(): lax.dynamic_index_in_dim(w2, tap_of(side, -1), 1, keepdims=False)]
    squeeze x8 -> x0, local copies, waits for them, and re-layouts: 4.16 us -> none  [the longest x4 2.43 us: weights_of(): w2 = all_w2[cascade]]
    ppermute x11, waiting for transfers between devices: 13.6 us -> 17.7 us  [gathered_rows(): lax.ppermute(value, axis, [(i, (i + step) % count) for i in range(count)])]
    dynamic_update_slice x16 -> x15, local copies, waits for them, and re-layouts: 9.83 us -> 5.73 us  [gathered_rows(): lax.dynamic_update_slice_in_dim(whole, block, (index - step) % count * si...]
  transfers between devices with their start and end apart: 20 -> 20, of which waited for: 8 -> 15; matrix products, arithmetic and copies ran while one was open for 34% -> 15% of each run, Pallas kernels for 0% -> 0%
where the time goes in v2:
time: 185 us; the launch traced here: 184 us
  Pallas kernels  86.9 us (47%)
  waiting for transfers between devices  33.7 us (18%)
  other arithmetic  22.4 us (12%)
  starting transfers between devices  19.3 us (10%)
  local copies, waits for them, and re-layouts  16.3 us (9%)
  blocking collectives  3.94 us (2%)
    pallas_call x4, Pallas kernels, refine(): pl.pallas_call(functools.partial(refine_kernel, neighbours, width, cascad...  47.7 us
    pallas_call x4, Pallas kernels, consistency(): pl.pallas_call(functools.partial(consistency_kernel, phases, width, casca...  39.2 us
    ppermute x11, waiting for transfers between devices, gathered_rows(): lax.ppermute(value, axis, [(i, (i + step) % count) for i in range(count)])  17.7 us
    ppermute x11, starting transfers between devices, gathered_rows(): lax.ppermute(value, axis, [(i, (i + step) % count) for i in range(count)])  15.6 us
    ppermute x8, waiting for transfers between devices, exchanged(): received.append(lax.ppermute(value, 'coil', pairs))  12.9 us
    unnamed x166, local copies, waits for them, and re-layouts  9.26 us
    dynamic_update_slice x15, local copies, waits for them, and re-layouts, gathered_rows(): lax.dynamic_update_slice_in_dim(whole, block, (index - step) % count * si...  5.73 us
    all_to_all x1, blocking collectives, per_device(): maps = lax.all_to_all(maps, 'coil', split_axis=1, concat_axis=0, tiled=True)  3.94 us
  transfers between devices with their start and end apart: 20, of which 15 were waited for; matrix products, arithmetic and copies ran while one was open for 15% of the time, Pallas kernels for 0%

profile of v2, /device:TPU:0, one launch (start us, length us, event | category | flops | bytes accessed | tf_op | source)
XLA Modules:
  0.0 184.4 jit_solution(10201794767479287435)
XLA Ops:
  0.0 1.0 copy-done
  1.1 3.9 %all_to_all.15 = bf16[2,2,64,512]{3,2,0,1:T(8,128)(2,1)S(1)} all-to-all(bf16[2,2,64,512]{3,2,0,1:T(8,128)(2,1)S(1)} %copy.39), channel_id=1, replica_groups=mesh['group'=2,'member'=2,'coil'=2,'space'=4] {'coil'}, dimensions={1} | all-to-all | bytes 524288 | tf_op jit(solution)/shard_map/all_to_all | solution.py:402
  5.0 3.1 %collective-permute-start.3 = (bf16[4,64,512]{2,1,0:T(8,128)(2,1)S(1)}, bf16[4,64,512]{2,1,0:T(8,128)(2,1)}, u32[]{:S(2)}, u32[]{:S(2)}) collective-permute-start(bf16[4,64,512]{2,1,0:T(8,128)(2,1)S(1)} %bitcast.66), channel_id=1, source_target_pairs={{0,1},{1,2},{2,3},{3,0},{4,5},{5,6},{6,7},{7,4},{8,9},{9,10},{10,1... | collective-permute-start | bytes 786440 | tf_op jit(solution)/shard_map/ppermute | solution.py:315
  8.1 2.6 %collective-permute-start.4 = (bf16[4,64,512]{2,1,0:T(8,128)(2,1)S(1)}, bf16[4,64,512]{2,1,0:T(8,128)(2,1)}, u32[]{:S(2)}, u32[]{:S(2)}) collective-permute-start(bf16[4,64,512]{2,1,0:T(8,128)(2,1)S(1)} %bitcast.67), channel_id=1, source_target_pairs={{0,2},{1,3},{2,0},{3,1},{4,6},{5,7},{6,4},{7,5},{8,10},{9,11},{10,... | collective-permute-start | bytes 786440 | tf_op jit(solution)/shard_map/ppermute | solution.py:315
  10.7 1.3 collective-permute-start.5
  12.1 1.0 constant_dynamic-update-slice_fusion.7
  13.1 0.7 collective-permute-start.6
  14.6 0.6 maximum_bitcast_fusion
  15.2 1.5 collective-permute-start.9
  16.9 0.7 fusion.59
  17.6 0.7 fusion.53
  18.3 0.6 broadcast_compare_fusion
  18.9 0.6 broadcast_compare_fusion.2
  22.2 0.6 compare_and_fusion.7
  22.8 0.6 iota_divide_fusion.1
  28.5 0.6 iota_shift-right-logical_fusion.2
  29.1 0.6 compare_and_fusion
  30.4 1.6 constant_dynamic-update-slice_fusion.15
  32.8 0.7 fusion.71
  34.3 1.5 and_convert_fusion.refs_2_.refs_3_
  36.5 1.1 fusion.35.refs_4_
  38.1 0.8 copy.42.refs_4_.refs_6_.refs_5_.refs_7_
  38.9 0.6 collective-permute-start
  39.5 3.2 %collective-permute-start.7 = (bf16[4,64,256]{2,1,0:T(8,128)(2,1)S(1)}, bf16[4,64,256]{2,1,0:T(8,128)(2,1)S(1)}, u32[]{:S(2)}, u32[]{:S(2)}) collective-permute-start(bf16[4,64,256]{2,1,0:T(8,128)(2,1)S(1)} %get-tuple-element.44), channel_id=1, source_target_pairs={{0,2},{1,3},{2,0},{3,1},{4,6},{5,7},{6,4},{7,5},{8,10},{9,11},{10,... | collective-permute-start | bytes 393224 | tf_op jit(solution)/shard_map/ppermute | solution.py:315
  42.7 0.9 constant_dynamic-update-slice_fusion.6
  43.7 3.6 %collective-permute-done = bf16[4,64,256]{2,1,0:T(8,128)(2,1)S(1)} collective-permute-done((bf16[4,64,256]{2,1,0:T(8,128)(2,1)}, bf16[4,64,256]{2,1,0:T(8,128)(2,1)S(1)}, u32[]{:S(2)}, u32[]{:S(2)}) %collective-permute-start) | collective-permute-done | bytes 131104 | tf_op jit(solution)/shard_map/ppermute | solution.py:315
  47.4 6.4 %collective-permute-done.7 = bf16[4,64,256]{2,1,0:T(8,128)(2,1)S(1)} collective-permute-done((bf16[4,64,256]{2,1,0:T(8,128)(2,1)S(1)}, bf16[4,64,256]{2,1,0:T(8,128)(2,1)S(1)}, u32[]{:S(2)}, u32[]{:S(2)}) %collective-permute-start.7) | collective-permute-done | bytes 131104 | tf_op jit(solution)/shard_map/ppermute | solution.py:315
  53.8 1.1 collective-permute-start.8
  54.9 1.7 collective-permute-done.1
  56.6 2.9 %collective-permute-done.8 = bf16[4,64,256]{2,1,0:T(8,128)(2,1)S(1)} collective-permute-done((bf16[4,64,256]{2,1,0:T(8,128)(2,1)S(1)}, bf16[4,64,256]{2,1,0:T(8,128)(2,1)S(1)}, u32[]{:S(2)}, u32[]{:S(2)}) %collective-permute-start.8) | collective-permute-done | bytes 131104 | tf_op jit(solution)/shard_map/ppermute | solution.py:315
  59.5 1.5 collective-permute-start.10
  61.0 0.7 collective-permute-done.2
  61.7 2.4 %collective-permute-done.10 = f32[2,96,128]{2,1,0:T(8,128)S(1)} collective-permute-done((f32[2,96,128]{2,1,0:T(8,128)S(1)}, f32[2,96,128]{2,1,0:T(8,128)S(1)}, u32[]{:S(2)}, u32[]{:S(2)}) %collective-permute-start.10) | collective-permute-done | bytes 98336 | tf_op jit(solution)/shard_map/ppermute | solution.py:315
  64.2 1.0 constant_dynamic-update-slice_fusion.10
  65.2 1.0 constant_dynamic-update-slice_fusion.9
  66.3 1.0 copy-done.1
  67.4 9.6 %shard_map.82 = (f32[4,64,256]{2,1,0:T(8,128)}, f32[4,256,256]{2,1,0:T(8,128)}, bf16[4,256,256]{2,1,0:T(8,128)(2,1)}) custom-call(s32[1]{0:T(128)} %bitcast.place_ref, bf16[4,256,256]{2,1,0:T(8,128)(2,1)} %copy-done.4, bf16[4,256,512]{2,1,0:T(8,128)(2,1)} %copy-done.1, bf16[4,256,256]{2,1,0:T(8,128)(2,1)} %copy-done.3, ...), custom_call_target="tpu_custom_call" | custom-call | tf_op jit(solution)/shard_map/pallas_call | solution.py:419
  77.6 1.3 fusion.19.refs_3_
  79.1 0.8 copy-done.12
  79.9 11.9 %shard_map.83 = (f32[4,256,256]{2,1,0:T(8,128)}, bf16[4,256,256]{2,1,0:T(8,128)(2,1)}) custom-call(bf16[4,256,256]{2,1,0:T(8,128)(2,1)} %get-tuple-element.24.v_ref, bf16[4,256,256]{2,1,0:T(8,128)(2,1)} %copy-done.12, f32[4,256,256]{2,1,0:T(8,128)} %get-tuple-element.25.refs_1_, f32[4,96,128]{2,1,0:T(8,128)} %copy-done.2, ...), custom_call_target="tpu_custom_call" | custom-call | tf_op jit(solution)/shard_map/pallas_call | solution.py:430
  92.1 1.8 collective-permute-done.12.refs_0_
  93.9 0.8 copy-done.9
  94.7 9.9 %shard_map.84 = (f32[4,64,256]{2,1,0:T(8,128)}, f32[4,256,256]{2,1,0:T(8,128)}, bf16[4,256,256]{2,1,0:T(8,128)(2,1)}) custom-call(s32[1]{0:T(128)} %bitcast.place_ref, f32[4,256,256]{2,1,0:T(8,128)} %get-tuple-element.26.base_ref, bf16[4,256,256]{2,1,0:T(8,128)(2,1)} %copy-done.9, bf16[4,256,512]{2,1,0:T(8,128)(2,1)} %copy-done.1, ...), custom_call_target="tpu_custom_call" | custom-call | tf_op jit(solution)/shard_map/pallas_call | solution.py:419
  104.9 1.8 collective-permute-done.13.refs_0_
  106.7 0.8 copy-done.14
  107.5 11.9 %shard_map.85 = (f32[4,256,256]{2,1,0:T(8,128)}, bf16[4,256,256]{2,1,0:T(8,128)(2,1)}) custom-call(bf16[4,256,256]{2,1,0:T(8,128)(2,1)} %get-tuple-element.28.v_ref, bf16[4,256,256]{2,1,0:T(8,128)(2,1)} %copy-done.14, f32[4,256,256]{2,1,0:T(8,128)} %get-tuple-element.29.refs_1_, f32[4,96,128]{2,1,0:T(8,128)} %copy-done.2, ...), custom_call_target="tpu_custom_call" | custom-call | tf_op jit(solution)/shard_map/pallas_call | solution.py:430
  119.7 1.8 collective-permute-done.14.refs_0_
  121.5 0.8 copy-done.10
  122.3 9.9 %shard_map.86 = (f32[4,64,256]{2,1,0:T(8,128)}, f32[4,256,256]{2,1,0:T(8,128)}, bf16[4,256,256]{2,1,0:T(8,128)(2,1)}) custom-call(s32[1]{0:T(128)} %bitcast.place_ref, f32[4,256,256]{2,1,0:T(8,128)} %get-tuple-element.30.base_ref, bf16[4,256,256]{2,1,0:T(8,128)(2,1)} %copy-done.10, bf16[4,256,512]{2,1,0:T(8,128)(2,1)} %copy-done.1, ...), custom_call_target="tpu_custom_call" | custom-call | tf_op jit(solution)/shard_map/pallas_call | solution.py:419
  132.5 1.8 collective-permute-done.15.refs_0_
  134.3 0.8 copy-done.15
  135.1 11.9 %shard_map.87 = (f32[4,256,256]{2,1,0:T(8,128)}, bf16[4,256,256]{2,1,0:T(8,128)(2,1)}) custom-call(bf16[4,256,256]{2,1,0:T(8,128)(2,1)} %get-tuple-element.32.v_ref, bf16[4,256,256]{2,1,0:T(8,128)(2,1)} %copy-done.15, f32[4,256,256]{2,1,0:T(8,128)} %get-tuple-element.33.refs_1_, f32[4,96,128]{2,1,0:T(8,128)} %copy-done.2, ...), custom_call_target="tpu_custom_call" | custom-call | tf_op jit(solution)/shard_map/pallas_call | solution.py:430
  147.3 1.8 collective-permute-done.16.refs_0_
  149.1 0.8 copy-done.8
  149.9 9.9 %shard_map.88 = (f32[4,64,256]{2,1,0:T(8,128)}, f32[4,256,256]{2,1,0:T(8,128)}, bf16[4,256,256]{2,1,0:T(8,128)(2,1)}) custom-call(s32[1]{0:T(128)} %bitcast.place_ref, f32[4,256,256]{2,1,0:T(8,128)} %get-tuple-element.34.base_ref, bf16[4,256,256]{2,1,0:T(8,128)(2,1)} %copy-done.8, bf16[4,256,512]{2,1,0:T(8,128)(2,1)} %copy-done.1, ...), custom_call_target="tpu_custom_call" | custom-call | tf_op jit(solution)/shard_map/pallas_call | solution.py:419
  160.1 1.8 collective-permute-done.17.refs_0_
  161.9 0.8 copy-done.13
  162.7 12.0 %shard_map.89 = (f32[4,256,256]{2,1,0:T(8,128)}, bf16[4,256,256]{2,1,0:T(8,128)(2,1)}) custom-call(bf16[4,256,256]{2,1,0:T(8,128)(2,1)} %get-tuple-element.36.v_ref, bf16[4,256,256]{2,1,0:T(8,128)(2,1)} %copy-done.13, f32[4,256,256]{2,1,0:T(8,128)} %get-tuple-element.37.refs_1_, f32[4,96,128]{2,1,0:T(8,128)} %copy-done.2, ...), custom_call_target="tpu_custom_call" | custom-call | tf_op jit(solution)/shard_map/pallas_call | solution.py:430
  175.1 1.8 collective-permute-done.18
  176.9 1.0 select_convert_fusion
  177.9 1.6 collective-permute-start.19
  179.6 1.0 bitcast_dynamic-update-slice_fusion
  180.6 3.1 %collective-permute-done.19 = bf16[4,64,256]{2,1,0:T(8,128)(2,1)S(1)} collective-permute-done((bf16[4,64,256]{2,1,0:T(8,128)(2,1)S(1)}, bf16[4,64,256]{2,1,0:T(8,128)(2,1)S(1)}, u32[]{:S(2)}, u32[]{:S(2)}) %collective-permute-start.19) | collective-permute-done | bytes 131104 | tf_op jit(solution)/shard_map/ppermute | solution.py:488
  183.7 0.7 convert_dynamic-update-slice_fusion
  (216 shorter events, 14.2 us)
Async XLA Ops:
  5.0 59.1 %collective-permute-start.3 = (bf16[4,64,512]{2,1,0:T(8,128)(2,1)S(1)}, bf16[4,64,512]{2,1,0:T(8,128)(2,1)}, u32[]{:S(2)}, u32[]{:S(2)}) collective-permute-start(bf16[4,64,512]{2,1,0:T(8,128)(2,1)S(1)} %bitcast.66), channel_id=1, source_target_pairs={{0,1},{1,2},{2,3},{3,0},{4,5},{5,6},{6,7},{7,4},{8,9},{9,10},{10,1... | collective-permute-start | bytes 786440 | tf_op jit(solution)/shard_map/ppermute | solution.py:315
  8.1 57.1 %collective-permute-start.4 = (bf16[4,64,512]{2,1,0:T(8,128)(2,1)S(1)}, bf16[4,64,512]{2,1,0:T(8,128)(2,1)}, u32[]{:S(2)}, u32[]{:S(2)}) collective-permute-start(bf16[4,64,512]{2,1,0:T(8,128)(2,1)S(1)} %bitcast.67), channel_id=1, source_target_pairs={{0,2},{1,3},{2,0},{3,1},{4,6},{5,7},{6,4},{7,5},{8,10},{9,11},{10,... | collective-permute-start | bytes 786440 | tf_op jit(solution)/shard_map/ppermute | solution.py:315
  10.7 55.5 %collective-permute-start.5 = (bf16[4,64,512]{2,1,0:T(8,128)(2,1)S(1)}, bf16[4,64,512]{2,1,0:T(8,128)(2,1)S(1)}, u32[]{:S(2)}, u32[]{:S(2)}) collective-permute-start(bf16[4,64,512]{2,1,0:T(8,128)(2,1)S(1)} %bitcast.68), channel_id=1, source_target_pairs={{0,3},{1,0},{2,1},{3,2},{4,7},{5,4},{6,5},{7,6},{8,11},{9,8},{10,9... | collective-permute-start | bytes 786440 | tf_op jit(solution)/shard_map/ppermute | solution.py:315
  13.1 26.5 %collective-permute-start.6 = (bf16[4,64,256]{2,1,0:T(8,128)(2,1)S(1)}, bf16[4,64,256]{2,1,0:T(8,128)(2,1)}, u32[]{:S(2)}, u32[]{:S(2)}) collective-permute-start(bf16[4,64,256]{2,1,0:T(8,128)(2,1)S(1)} %get-tuple-element.44), channel_id=1, source_target_pairs={{0,1},{1,2},{2,3},{3,0},{4,5},{5,6},{6,7},{7,4},{8,9},{9,10},{10,1... | collective-permute-start | bytes 393224 | tf_op jit(solution)/shard_map/ppermute | solution.py:315
  15.2 23.7 %collective-permute-start.9 = (f32[1,96,128]{2,1,0:T(8,128)}, f32[1,96,128]{2,1,0:T(8,128)S(1)}, u32[]{:S(2)}, u32[]{:S(2)}) collective-permute-start(f32[1,96,128]{2,1,0:T(8,128)} %maximum_bitcast_fusion), channel_id=1, source_target_pairs={{0,8},{8,0},{1,9},{9,1},{2,10},{10,2},{3,11},{11,3},{4,12},{12,4},... | collective-permute-start | bytes 147464 | tf_op jit(solution)/shard_map/ppermute | solution.py:315
  34.2 1.7 copy-start.37
  34.2 1.7 copy-start.38
  34.2 1.7 copy-start.39
  34.2 1.7 copy-start.40
  34.2 1.7 copy-start.43
  34.2 1.7 copy-start.45
  34.2 1.7 copy-start.47
  34.2 1.7 copy-start.49
  34.2 1.7 copy-start.51
  34.2 1.7 copy-start.53
  34.3 1.7 copy-start.55
  34.3 1.7 copy-start.57
  34.3 1.7 copy-start.59
  34.3 1.7 copy-start.61
  34.3 1.7 copy-start.63
  34.3 1.7 copy-start.79
  34.3 1.7 copy-start.80
  38.9 8.4 %collective-permute-start = (bf16[4,64,256]{2,1,0:T(8,128)(2,1)}, bf16[4,64,256]{2,1,0:T(8,128)(2,1)S(1)}, u32[]{:S(2)}, u32[]{:S(2)}) collective-permute-start(bf16[4,64,256]{2,1,0:T(8,128)(2,1)} %get-tuple-element.46), channel_id=1, source_target_pairs={{0,1},{1,2},{2,3},{3,0},{4,5},{5,6},{6,7},{7,4},{8,9},{9,10},{10,1... | collective-permute-start | bytes 393224 | tf_op jit(solution)/shard_map/ppermute | solution.py:315
  39.5 14.2 %collective-permute-start.7 = (bf16[4,64,256]{2,1,0:T(8,128)(2,1)S(1)}, bf16[4,64,256]{2,1,0:T(8,128)(2,1)S(1)}, u32[]{:S(2)}, u32[]{:S(2)}) collective-permute-start(bf16[4,64,256]{2,1,0:T(8,128)(2,1)S(1)} %get-tuple-element.44), channel_id=1, source_target_pairs={{0,2},{1,3},{2,0},{3,1},{4,6},{5,7},{6,4},{7,5},{8,10},{9,11},{10,... | collective-permute-start | bytes 393224 | tf_op jit(solution)/shard_map/ppermute | solution.py:315
  42.7 4.6 %copy-start.16 = (bf16[4,64,256]{2,1,0:T(8,128)(2,1)S(1)}, bf16[4,64,256]{2,1,0:T(8,128)(2,1)}, u32[]{:S(2)}) copy-start(bf16[4,64,256]{2,1,0:T(8,128)(2,1)} %get-tuple-element.46) | copy-start | bytes 393220
  47.3 9.2 %collective-permute-start.1 = (bf16[4,64,256]{2,1,0:T(8,128)(2,1)S(1)}, bf16[4,64,256]{2,1,0:T(8,128)(2,1)S(1)}, u32[]{:S(2)}, u32[]{:S(2)}) collective-permute-start(bf16[4,64,256]{2,1,0:T(8,128)(2,1)S(1)} %copy-done.16), channel_id=1, source_target_pairs={{0,2},{1,3},{2,0},{3,1},{4,6},{5,7},{6,4},{7,5},{8,10},{9,11},{10,... | collective-permute-start | bytes 393224 | tf_op jit(solution)/shard_map/ppermute | solution.py:315
  53.8 5.7 %collective-permute-start.8 = (bf16[4,64,256]{2,1,0:T(8,128)(2,1)S(1)}, bf16[4,64,256]{2,1,0:T(8,128)(2,1)S(1)}, u32[]{:S(2)}, u32[]{:S(2)}) collective-permute-start(bf16[4,64,256]{2,1,0:T(8,128)(2,1)S(1)} %get-tuple-element.44), channel_id=1, source_target_pairs={{0,3},{1,0},{2,1},{3,2},{4,7},{5,4},{6,5},{7,6},{8,11},{9,8},{10,9... | collective-permute-start | bytes 393224 | tf_op jit(solution)/shard_map/ppermute | solution.py:315
  56.6 5.1 %collective-permute-start.2 = (bf16[4,64,256]{2,1,0:T(8,128)(2,1)S(1)}, bf16[4,64,256]{2,1,0:T(8,128)(2,1)S(1)}, u32[]{:S(2)}, u32[]{:S(2)}) collective-permute-start(bf16[4,64,256]{2,1,0:T(8,128)(2,1)S(1)} %copy-done.16), channel_id=1, source_target_pairs={{0,3},{1,0},{2,1},{3,2},{4,7},{5,4},{6,5},{7,6},{8,11},{9,8},{10,9... | collective-permute-start | bytes 393224 | tf_op jit(solution)/shard_map/ppermute | solution.py:315
  59.5 4.6 %collective-permute-start.10 = (f32[2,96,128]{2,1,0:T(8,128)S(1)}, f32[2,96,128]{2,1,0:T(8,128)S(1)}, u32[]{:S(2)}, u32[]{:S(2)}) collective-permute-start(f32[2,96,128]{2,1,0:T(8,128)S(1)} %constant_dynamic-update-slice_fusion.2), channel_id=1, source_target_pairs={{0,16},{16,0},{1,17},{17,1},{2,18},{18,2},{3,19},{19,3},{4,20},{20... | collective-permute-start | bytes 294920 | tf_op jit(solution)/shard_map/ppermute | solution.py:315
  61.0 5.2 %copy-start.3 = (bf16[4,256,256]{2,1,0:T(8,128)(2,1)}, bf16[4,256,256]{2,1,0:T(8,128)(2,1)S(1)}, u32[]{:S(2)}) copy-start(bf16[4,256,256]{2,1,0:T(8,128)(2,1)S(1)} %constant_dynamic-update-slice_fusion.4.refs_1_.refs_2_) | copy-start | bytes 1572868
  61.7 4.5 %copy-start.4 = (bf16[4,256,256]{2,1,0:T(8,128)(2,1)}, bf16[4,256,256]{2,1,0:T(8,128)(2,1)S(1)}, u32[]{:S(2)}) copy-start(bf16[4,256,256]{2,1,0:T(8,128)(2,1)S(1)} %constant_dynamic-update-slice_fusion.12.base_ref) | copy-start | bytes 1572868
  67.2 9.7 %copy-start.30 = (s32[256]{0:T(256)S(1)}, s32[256]{0:T(256)}, u32[]{:S(2)}) copy-start(s32[256]{0:T(256)} %get-tuple-element.81) | copy-start | bytes 3076
  67.2 9.8 %copy-start.31 = (s32[256]{0:T(256)S(1)}, s32[256]{0:T(256)}, u32[]{:S(2)}) copy-start(s32[256]{0:T(256)} %get-tuple-element.84) | copy-start | bytes 3076
  67.2 9.8 %copy-start.32 = (s32[256]{0:T(256)S(1)}, s32[256]{0:T(256)}, u32[]{:S(2)}) copy-start(s32[256]{0:T(256)} %get-tuple-element.85) | copy-start | bytes 3076
  67.2 9.8 %copy-start.33 = (s32[256]{0:T(256)S(1)}, s32[256]{0:T(256)}, u32[]{:S(2)}) copy-start(s32[256]{0:T(256)} %get-tuple-element.90) | copy-start | bytes 3076
  67.2 9.8 %copy-start.34 = (s32[256]{0:T(256)S(1)}, s32[256]{0:T(256)}, u32[]{:S(2)}) copy-start(s32[256]{0:T(256)} %get-tuple-element.91) | copy-start | bytes 3076
  67.2 9.8 %copy-start.44 = (pred[108]{0:T(512)(128)(4,1)S(1)}, pred[108]{0:T(512)(128)(4,1)}, u32[]{:S(2)}) copy-start(pred[108]{0:T(512)(128)(4,1)} %get-tuple-element.63) | copy-start | bytes 328
  67.3 9.8 %copy-start.46 = (pred[108]{0:T(512)(128)(4,1)S(1)}, pred[108]{0:T(512)(128)(4,1)}, u32[]{:S(2)}) copy-start(pred[108]{0:T(512)(128)(4,1)} %get-tuple-element.66) | copy-start | bytes 328
  67.3 9.8 %copy-start.48 = (pred[108]{0:T(512)(128)(4,1)S(1)}, pred[108]{0:T(512)(128)(4,1)}, u32[]{:S(2)}) copy-start(pred[108]{0:T(512)(128)(4,1)} %get-tuple-element.67) | copy-start | bytes 328
  67.3 9.8 %copy-start.50 = (s32[108]{0:T(128)S(1)}, s32[108]{0:T(128)}, u32[]{:S(2)}) copy-start(s32[108]{0:T(128)} %get-tuple-element.86) | copy-start | bytes 1300
  67.3 9.8 %copy-start.52 = (s32[108]{0:T(128)S(1)}, s32[108]{0:T(128)}, u32[]{:S(2)}) copy-start(s32[108]{0:T(128)} %get-tuple-element.87) | copy-start | bytes 1300
  67.3 9.8 %copy-start.54 = (s32[108]{0:T(128)S(1)}, s32[108]{0:T(128)}, u32[]{:S(2)}) copy-start(s32[108]{0:T(128)} %get-tuple-element.88) | copy-start | bytes 1300
  67.3 9.8 %copy-start.56 = (s32[108]{0:T(128)S(1)}, s32[108]{0:T(128)}, u32[]{:S(2)}) copy-start(s32[108]{0:T(128)} %get-tuple-element.89) | copy-start | bytes 1300
  67.3 9.8 %copy-start.58 = (s32[108]{0:T(128)S(1)}, s32[108]{0:T(128)}, u32[]{:S(2)}) copy-start(s32[108]{0:T(128)} %get-tuple-element.92) | copy-start | bytes 1300
  67.3 9.8 %copy-start.60 = (s32[108]{0:T(128)S(1)}, s32[108]{0:T(128)}, u32[]{:S(2)}) copy-start(s32[108]{0:T(128)} %get-tuple-element.93) | copy-start | bytes 1300
  67.3 9.8 %copy-start.62 = (s32[108]{0:T(128)S(1)}, s32[108]{0:T(128)}, u32[]{:S(2)}) copy-start(s32[108]{0:T(128)} %get-tuple-element.94) | copy-start | bytes 1300
  67.3 9.8 %copy-start.64 = (s32[108]{0:T(128)S(1)}, s32[108]{0:T(128)}, u32[]{:S(2)}) copy-start(s32[108]{0:T(128)} %get-tuple-element.95) | copy-start | bytes 1300
  67.4 9.8 %copy-start.66 = (pred[256]{0:T(512)(128)(4,1)S(1)}, pred[256]{0:T(512)(128)(4,1)}, u32[]{:S(2)}) copy-start(pred[256]{0:T(512)(128)(4,1)} %get-tuple-element.64) | copy-start | bytes 772
  67.4 9.8 %copy-start.67 = (pred[256]{0:T(512)(128)(4,1)S(1)}, pred[256]{0:T(512)(128)(4,1)}, u32[]{:S(2)}) copy-start(pred[256]{0:T(512)(128)(4,1)} %get-tuple-element.65) | copy-start | bytes 772
  67.4 9.8 %copy-start.68 = (pred[256]{0:T(512)(128)(4,1)S(1)}, pred[256]{0:T(512)(128)(4,1)}, u32[]{:S(2)}) copy-start(pred[256]{0:T(512)(128)(4,1)} %get-tuple-element.82) | copy-start | bytes 772
  67.4 9.8 %copy-start.69 = (pred[256]{0:T(512)(128)(4,1)S(1)}, pred[256]{0:T(512)(128)(4,1)}, u32[]{:S(2)}) copy-start(pred[256]{0:T(512)(128)(4,1)} %get-tuple-element.83) | copy-start | bytes 772
  76.9 2.1 %collective-permute-start.11 = (bf16[4,256,256]{2,1,0:T(8,128)(2,1)}, bf16[4,256,256]{2,1,0:T(8,128)(2,1)S(1)}, u32[]{:S(2)}, u32[]{:S(2)}) collective-permute-start(bf16[4,256,256]{2,1,0:T(8,128)(2,1)} %get-tuple-element.24.v_ref), channel_id=1, source_target_pairs={{0,4},{4,0},{1,5},{5,1},{2,6},{6,2},{3,7},{7,3},{8,12},{12,8},{9,1... | collective-permute-start | bytes 1572872 | tf_op jit(solution)/shard_map/ppermute | solution.py:452
  91.8 2.1 %collective-permute-start.12 = (bf16[4,256,256]{2,1,0:T(8,128)(2,1)}, bf16[4,256,256]{2,1,0:T(8,128)(2,1)S(1)}, u32[]{:S(2)}, u32[]{:S(2)}) collective-permute-start(bf16[4,256,256]{2,1,0:T(8,128)(2,1)} %get-tuple-element.27), channel_id=1, source_target_pairs={{0,4},{4,0},{1,5},{5,1},{2,6},{6,2},{3,7},{7,3},{8,12},{12,8},{9,1... | collective-permute-start | bytes 1572872 | tf_op jit(solution)/shard_map/ppermute | solution.py:452
  104.6 2.1 %collective-permute-start.13 = (bf16[4,256,256]{2,1,0:T(8,128)(2,1)}, bf16[4,256,256]{2,1,0:T(8,128)(2,1)S(1)}, u32[]{:S(2)}, u32[]{:S(2)}) collective-permute-start(bf16[4,256,256]{2,1,0:T(8,128)(2,1)} %get-tuple-element.28.v_ref), channel_id=1, source_target_pairs={{0,4},{4,0},{1,5},{5,1},{2,6},{6,2},{3,7},{7,3},{8,12},{12,8},{9,1... | collective-permute-start | bytes 1572872 | tf_op jit(solution)/shard_map/ppermute | solution.py:452
  119.4 2.1 %collective-permute-start.14 = (bf16[4,256,256]{2,1,0:T(8,128)(2,1)}, bf16[4,256,256]{2,1,0:T(8,128)(2,1)S(1)}, u32[]{:S(2)}, u32[]{:S(2)}) collective-permute-start(bf16[4,256,256]{2,1,0:T(8,128)(2,1)} %get-tuple-element.31), channel_id=1, source_target_pairs={{0,4},{4,0},{1,5},{5,1},{2,6},{6,2},{3,7},{7,3},{8,12},{12,8},{9,1... | collective-permute-start | bytes 1572872 | tf_op jit(solution)/shard_map/ppermute | solution.py:452
  132.2 2.1 %collective-permute-start.15 = (bf16[4,256,256]{2,1,0:T(8,128)(2,1)}, bf16[4,256,256]{2,1,0:T(8,128)(2,1)S(1)}, u32[]{:S(2)}, u32[]{:S(2)}) collective-permute-start(bf16[4,256,256]{2,1,0:T(8,128)(2,1)} %get-tuple-element.32.v_ref), channel_id=1, source_target_pairs={{0,4},{4,0},{1,5},{5,1},{2,6},{6,2},{3,7},{7,3},{8,12},{12,8},{9,1... | collective-permute-start | bytes 1572872 | tf_op jit(solution)/shard_map/ppermute | solution.py:452
  147.0 2.1 %collective-permute-start.16 = (bf16[4,256,256]{2,1,0:T(8,128)(2,1)}, bf16[4,256,256]{2,1,0:T(8,128)(2,1)S(1)}, u32[]{:S(2)}, u32[]{:S(2)}) collective-permute-start(bf16[4,256,256]{2,1,0:T(8,128)(2,1)} %get-tuple-element.35), channel_id=1, source_target_pairs={{0,4},{4,0},{1,5},{5,1},{2,6},{6,2},{3,7},{7,3},{8,12},{12,8},{9,1... | collective-permute-start | bytes 1572872 | tf_op jit(solution)/shard_map/ppermute | solution.py:452
  159.8 2.1 %collective-permute-start.17 = (bf16[4,256,256]{2,1,0:T(8,128)(2,1)}, bf16[4,256,256]{2,1,0:T(8,128)(2,1)S(1)}, u32[]{:S(2)}, u32[]{:S(2)}) collective-permute-start(bf16[4,256,256]{2,1,0:T(8,128)(2,1)} %get-tuple-element.36.v_ref), channel_id=1, source_target_pairs={{0,4},{4,0},{1,5},{5,1},{2,6},{6,2},{3,7},{7,3},{8,12},{12,8},{9,1... | collective-permute-start | bytes 1572872 | tf_op jit(solution)/shard_map/ppermute | solution.py:452
  162.7 14.1 %copy-start.5 = (f32[4,64,256]{2,1,0:T(8,128)S(1)}, f32[4,64,256]{2,1,0:T(8,128)}, u32[]{:S(2)}) copy-start(f32[4,64,256]{2,1,0:T(8,128)} %get-tuple-element.42) | copy-start | bytes 786436
  162.7 14.1 %copy-start.6 = (f32[4,64,256]{2,1,0:T(8,128)S(1)}, f32[4,64,256]{2,1,0:T(8,128)}, u32[]{:S(2)}) copy-start(f32[4,64,256]{2,1,0:T(8,128)} %get-tuple-element.41) | copy-start | bytes 786436
  162.7 14.1 %copy-start.7 = (f32[4,64,256]{2,1,0:T(8,128)S(1)}, f32[4,64,256]{2,1,0:T(8,128)}, u32[]{:S(2)}) copy-start(f32[4,64,256]{2,1,0:T(8,128)} %get-tuple-element.40) | copy-start | bytes 786436
  174.8 2.1 %collective-permute-start.18 = (bf16[4,256,256]{2,1,0:T(8,128)(2,1)}, bf16[4,256,256]{2,1,0:T(8,128)(2,1)S(1)}, u32[]{:S(2)}, u32[]{:S(2)}) collective-permute-start(bf16[4,256,256]{2,1,0:T(8,128)(2,1)} %get-tuple-element.39), channel_id=1, source_target_pairs={{0,4},{4,0},{1,5},{5,1},{2,6},{6,2},{3,7},{7,3},{8,12},{12,8},{9,1... | collective-permute-start | bytes 1572872 | tf_op jit(solution)/shard_map/ppermute | solution.py:452
  177.9 5.8 %collective-permute-start.19 = (bf16[4,64,256]{2,1,0:T(8,128)(2,1)S(1)}, bf16[4,64,256]{2,1,0:T(8,128)(2,1)S(1)}, u32[]{:S(2)}, u32[]{:S(2)}) collective-permute-start(bf16[4,64,256]{2,1,0:T(8,128)(2,1)S(1)} %select_convert_fusion), channel_id=1, source_target_pairs={{0,16},{16,0},{1,17},{17,1},{2,18},{18,2},{3,19},{19,3},{4,20},{20... | collective-permute-start | bytes 393224 | tf_op jit(solution)/shard_map/ppermute | solution.py:488
  180.6 3.1 %copy-start.11 = (f32[1,4,2,1,64,256]{5,4,3,2,1,0:T(8,128)}, f32[1,4,2,1,64,256]{5,4,3,2,1,0:T(8,128)S(1)}, u32[]{:S(2)}) copy-start(f32[1,4,2,1,64,256]{5,4,3,2,1,0:T(8,128)S(1)} %bitcast_dynamic-update-slice_fusion) | copy-start | bytes 1572868
  (39 other events, 33.6 us)

commit v3 on v2

--- a/solution.py
+++ b/solution.py
@@ -1,8 +1,8 @@
 import functools
-import math
 
 import jax
 import jax.numpy as jnp
+import numpy as np
 from jax import lax
 from jax.experimental import pallas as pl
 from jax.experimental.pallas import tpu as pltpu
@@ -18,36 +18,53 @@
 
 def half_tables(length):
     half = length // 2
-    slot = jnp.arange(half, dtype=jnp.int32)
-    index = jnp.arange(length, dtype=jnp.int32)
-    product = slot[:, None] * index[None, :] % length
-    angle = product.astype(F32) * (2.0 * math.pi / length)
-    scale = 1.0 / math.sqrt(length)
-    odd = (index % 2).astype(F32)[None, :] * scale
-    even = scale - odd
-    first = slot[:, None] == 0
-    cos = jnp.where(first, even, jnp.cos(angle) * scale)
-    sin = jnp.where(first, odd, jnp.sin(angle) * scale)
-    return jnp.concatenate([cos, sin], axis=0).astype(BF)
+    index = np.arange(length)
+    angle = np.arange(half)[:, None] * index[None, :] % length * (2.0 * np.pi / length)
+    scale = 1.0 / np.sqrt(length)
+    cos = np.cos(angle) * scale
+    sin = np.sin(angle) * scale
+    cos[0] = np.where(index % 2 == 0, scale, 0.0)
+    sin[0] = np.where(index % 2 == 0, 0.0, scale)
+    return np.concatenate([cos, sin], axis=0).astype(BF)
 
 
 def slot_order(length):
     half = length // 2
-    slot = jnp.arange(length, dtype=jnp.int32)
-    return jnp.where(slot <= half, slot, length + half - slot)
-
-
-def unpack_mask(mask_bits, length_z):
-    half = mask_bits.shape[1] // 2
-    mask_bits = jnp.concatenate(
-        [mask_bits[:, : half + 1], jnp.flip(mask_bits[:, half + 1 :], axis=1)], axis=1
+    slot = np.arange(length)
+    return np.where(slot <= half, slot, length + half - slot)
+
+
+def tap_selectors(channels, per_row, offsets):
+    count = 27 * channels
+    involved = len(offsets)
+    used = (ROWS + 2) * 3 * per_row
+    columns = -(-(used + 3) // LANES) * LANES
+    tap = np.arange(count)
+    plane, tap_y, tap_z, channel = (
+        tap // (9 * channels),
+        tap // (3 * channels) % 3,
+        tap // channels % 3,
+        tap % channels,
     )
-    column = slot_order(length_z)
-    word_count = mask_bits.shape[2]
-    chosen = jnp.zeros(mask_bits.shape[:2] + (length_z,), jnp.int32)
-    for word in range(word_count):
-        chosen = jnp.where(column // 30 == word, mask_bits[:, :, word : word + 1], chosen)
-    return (jnp.right_shift(chosen, column % 30) & 1).astype(F32)
+    column = np.arange(columns)
+    slot = column % per_row
+    offset = np.array(list(offsets) + [9] * (per_row // channels + 1))[slot // channels]
+    first = (
+        (column[None] < 9 * per_row)
+        & (plane[:, None] == 1 + offset[None])
+        & (tap_y[:, None] == column[None] // (3 * per_row))
+        & (tap_z[:, None] == column[None] // per_row % 3)
+        & (channel[:, None] == slot[None] % channels)
+    )
+    row = np.arange(3 * involved * channels * ROWS)
+    offset = np.array(offsets)[row // (channels * ROWS) % involved]
+    second = (
+        (plane[None] == 1 - offset[:, None])
+        & (tap_z[None] == row[:, None] // (involved * channels * ROWS))
+        & (channel[None] == row[:, None] // ROWS % channels)
+    )
+    second = np.stack([second & (tap_y[None] == at) for at in range(3)])
+    return first.astype(BF), second.astype(BF)
 
 
 def dot(left, right):
@@ -167,12 +184,13 @@
         total[2 * phase + 1] += map_re * back_im - map_im * back_re
 
     def coil(index, carry):
-        maps = maps_ref[index].astype(F32)
+        map_re = maps_ref[2 * index].astype(F32)
+        map_im = maps_ref[2 * index + 1].astype(F32)
         for phase in range(phases):
-            item(maps[:, :length_z], maps[:, length_z:], phase)
+            item(map_re, map_im, phase)
         return carry
 
-    lax.fori_loop(0, maps_ref.shape[0], coil, 0)
+    lax.fori_loop(0, maps_ref.shape[0] // 2, coil, 0)
     step = pack_ref[cascade, 2 * width : 2 * width + 1, 1:2]
     for channel in range(channels):
         value = image[channel] - step * total[channel]
@@ -180,43 +198,24 @@
         v_ref[channel] = value.astype(BF)
 
 
-def refine_kernel(neighbours, width, cascade, v_ref, *refs):
+def refine_kernel(neighbours, width, cascade, place_ref, v_ref, *refs):
     other_refs = refs[:neighbours]
-    dc_ref, pack_ref, select1_ref, select2_ref, base_ref = refs[neighbours : neighbours + 5]
-    send_refs = refs[neighbours + 5 : 2 * neighbours + 5]
-    mixed, taps, hidden, weight1, weight2 = refs[2 * neighbours + 5 :]
+    dc_ref, weight1_ref, weight2_ref, base_ref = refs[neighbours : neighbours + 4]
+    send_refs = refs[neighbours + 4 : 2 * neighbours + 4]
+    mixed, taps, hidden = refs[2 * neighbours + 4 :]
     channels, length_y, length_z = v_ref.shape
     tiles, mixed_rows, lanes = mixed.shape
     padded = length_y + 2 * ROWS
     per_row = mixed_rows // padded
-    count = select1_ref.shape[1]
-    bias_at = weight1.shape[1] - 2 * ROWS
-
-    small1 = pack_ref[cascade, :width, :count].astype(BF)
-    small2 = pack_ref[cascade, width : 2 * width, :count].astype(BF)
-    bias = pack_ref[cascade, 2 * width :, 0:1]
-    terms = []
-    for _ in range(3):
-        terms.append(bias.astype(BF).astype(F32))
-        bias = bias - terms[-1]
-    for row in range(ROWS):
-        value = dot(small1, select1_ref[row])
-        column = lax.broadcasted_iota(jnp.int32, value.shape, 1)
-        for at, term in enumerate(terms):
-            value = jnp.where(column == bias_at + at, term, value)
-        weight1[row * width : (row + 1) * width, :] = value.astype(BF)
-    repeated = jnp.concatenate([small2] * (ROWS + 2), axis=0)
-    shape = weight2.shape
-    column = lax.broadcasted_iota(jnp.int32, shape, 1)
-    lower = (lax.broadcasted_iota(jnp.int32, shape, 0) & (ROWS - 1)) * width
-    value = jnp.zeros(shape, F32)
-    for tap in range(3):
-        placed = lax.dot_general(
-            select2_ref[tap], repeated, (((1,), (1,)), ((), ())), preferred_element_type=F32
-        )
-        low = lower + tap * width
-        value = jnp.where((column >= low) & (column < low + width), placed, value)
-    weight2[...] = value.astype(BF)
+    total_blocks = length_y // ROWS
+    out_rows = base_ref.shape[1]
+    if out_rows == length_y:
+        first_block, out_block, blocks = 0, 0, total_blocks
+    else:
+        wanted = out_rows // ROWS + 2
+        blocks = min(total_blocks, -(-wanted // UNROLL) * UNROLL)
+        out_block = place_ref[0] * (out_rows // ROWS)
+        first_block = jnp.clip(out_block - 1, 0, total_blocks - blocks)
 
     for tile in range(tiles):
         mixed[tile, 0:per_row, :] = jnp.zeros((per_row, lanes), F32)
@@ -256,66 +255,155 @@
         taps[pl.ds(store, group * 3 * per_row), :] = value.reshape(-1, length_z).astype(BF)
         return carry
 
-    lax.fori_loop(0, padded // group, build, 0)
-    ones_row = lax.broadcasted_iota(jnp.int32, (2 * ROWS, length_z), 0)
+    builds = min(padded // group, blocks * ROWS // group + 2)
+    if builds == padded // group:
+        build_at = 0
+    else:
+        build_at = jnp.minimum(first_block * ROWS // group, padded // group - builds)
+    lax.fori_loop(build_at, build_at + builds, build, 0)
+    spare = weight1_ref.shape[2] - (ROWS + 2) * 3 * per_row
+    ones_row = lax.broadcasted_iota(jnp.int32, (spare, length_z), 0)
     ones = jnp.where(ones_row < 3, 1.0, 0.0).astype(BF)
 
     def first(block, carry):
         for part in range(UNROLL):
-            at = block * UNROLL + part
+            at = first_block + block * UNROLL + part
             start = pl.multiple_of(at * (ROWS * 3 * per_row), ROWS * 3 * per_row)
             window = jnp.concatenate(
                 [taps[pl.ds(start, (ROWS + 2) * 3 * per_row), :], ones], axis=0
             )
-            value = dot(weight1[...], window)
+            value = dot(weight1_ref[cascade], window)
             store = pl.multiple_of((at * ROWS + 1) * width, width)
             hidden[pl.ds(store, ROWS * width), :] = jnp.maximum(value, 0.0).astype(BF)
         return carry
 
-    lax.fori_loop(0, length_y // (UNROLL * ROWS), first, 0)
+    lax.fori_loop(0, blocks // UNROLL, first, 0)
     block_rows = channels * ROWS
+    unroll = min(UNROLL, out_rows // ROWS)
+    span = unroll * ROWS
 
     def second(block, carry):
         results = []
-        for part in range(UNROLL):
-            at = block * UNROLL + part
+        for part in range(unroll):
+            at = out_block + block * unroll + part
             start = pl.multiple_of(at * (ROWS * width), ROWS * width)
-            parts = dot(weight2[...], hidden[pl.ds(start, (ROWS + 2) * width), :])
+            parts = dot(weight2_ref[cascade], hidden[pl.ds(start, (ROWS + 2) * width), :])
             third = parts.shape[0] // 3
             results.append(
                 shifted_lanes(parts[:third], 1)
                 + parts[third : 2 * third]
                 + shifted_lanes(parts[2 * third :], -1)
             )
-        span = UNROLL * ROWS
         rows = pl.ds(pl.multiple_of(block * span, span), span)
+        from_rows = pl.ds(pl.multiple_of(out_block * ROWS + block * span, ROWS * 2), span)
         for plane in range(neighbours + 1):
             for channel in range(channels):
                 lo = plane * block_rows + channel * ROWS
                 value = jnp.concatenate([piece[lo : lo + ROWS] for piece in results], axis=0)
                 if plane == 0:
-                    base_ref[channel, rows, :] = dc_ref[channel, rows, :] + value
+                    base_ref[channel, rows, :] = dc_ref[channel, from_rows, :] + value
                 else:
                     send_refs[plane - 1][channel, rows, :] = value.astype(BF)
         return carry
 
-    lax.fori_loop(0, length_y // (UNROLL * ROWS), second, 0)
-
-
-def gathered_rows(value, axis, dim):
+    lax.fori_loop(0, out_rows // span, second, 0)
+
+
+def prepare_kernel(
+    width,
+    per_row,
+    place_ref,
+    pack_ref,
+    bits_ref,
+    columns_ref,
+    order_ref,
+    select1_ref,
+    select2_ref,
+    weight1_ref,
+    weight2_ref,
+    mask_ref,
+):
+    phases, length_y, length_z = mask_ref.shape
+    for phase in range(phases):
+        bits = bits_ref[phase]
+        chosen = jnp.zeros((length_y, length_z), jnp.int32)
+        for word in range(bits.shape[1]):
+            chosen = jnp.where(columns_ref[0:1] == word, bits[:, word : word + 1], chosen)
+        shift = jnp.broadcast_to(columns_ref[1:2], chosen.shape)
+        taken = lax.shift_right_logical(chosen, shift) & 1
+        mask_ref[phase] = dot(order_ref[...], taken.astype(F32).astype(BF))
+
+    variant = place_ref[1] if select1_ref.shape[0] > 1 else 0
+    count = select1_ref.shape[1]
+    for cascade in range(pack_ref.shape[0]):
+        small1 = pack_ref[cascade, :width, :count].astype(BF)
+        small2 = pack_ref[cascade, width : 2 * width, :count].astype(BF)
+        bias = pack_ref[cascade, 2 * width :, 0:1]
+        terms = []
+        for _ in range(3):
+            terms.append(bias.astype(BF).astype(F32))
+            bias = bias - terms[-1]
+        base = dot(small1, select1_ref[variant])
+        column = lax.broadcasted_iota(jnp.int32, base.shape, 1)
+        step = per_row
+        for row in range(ROWS):
+            value = base if row == 0 else pltpu.roll(base, row * 3 * step, 1)
+            for at, term in enumerate(terms):
+                value = jnp.where(column == (ROWS + 2) * 3 * step + at, term, value)
+            weight1_ref[cascade, row * width : (row + 1) * width, :] = value.astype(BF)
+        repeated = jnp.concatenate([small2] * (ROWS + 2), axis=0)
+        shape = weight2_ref.shape[1:]
+        column = lax.broadcasted_iota(jnp.int32, shape, 1)
+        lower = (lax.broadcasted_iota(jnp.int32, shape, 0) & (ROWS - 1)) * width
+        value = jnp.zeros(shape, F32)
+        for tap in range(3):
+            placed = lax.dot_general(
+                select2_ref[variant, tap],
+                repeated,
+                (((1,), (1,)), ((), ())),
+                preferred_element_type=F32,
+            )
+            low = lower + tap * width
+            value = jnp.where((column >= low) & (column < low + width), placed, value)
+        weight2_ref[cascade] = value.astype(BF)
+
+
+def assemble_kernel(members, spaces, place_ref, *refs):
+    local_ref = refs[0]
+    block_refs = refs[1 : 1 + (spaces - 1) * members]
+    out_refs = refs[1 + (spaces - 1) * members :]
+    rows = local_ref.shape[2]
+
+    def put(owner, at, block):
+        where = pl.ds(pl.multiple_of(at * rows, rows), rows)
+        taken = 0
+        for out_ref in out_refs:
+            size = out_ref.shape[0] // members
+            for index in range(size):
+                out_ref[owner * size + index, where, :] = block[taken + index]
+            taken += size
+
+    for member in range(members):
+        put(member, place_ref[0], local_ref[member])
+    for step in range(1, spaces):
+        at = lax.rem(place_ref[0] - step + spaces, spaces)
+        for offset in range(members):
+            owner = lax.rem(place_ref[2] + offset, members)
+            put(owner, at, block_refs[(step - 1) * members + offset])
+
+
+def ring(value, axis, step):
+    count = lax.axis_size(axis)
+    return lax.ppermute(value, axis, [(i, (i + step) % count) for i in range(count)])
+
+
+def gathered(value, axis):
     count = lax.axis_size(axis)
     index = lax.axis_index(axis)
-    size = value.shape[dim]
-    shape = list(value.shape)
-    shape[dim] = size * count
-    whole = jnp.zeros(shape, value.dtype)
+    whole = jnp.zeros((count,) + value.shape, value.dtype)
     for step in range(count):
-        block = value
-        if step:
-            block = lax.ppermute(value, axis, [(i, (i + step) % count) for i in range(count)])
-        whole = lax.dynamic_update_slice_in_dim(
-            whole, block, (index - step) % count * size, dim
-        )
+        block = ring(value, axis, step) if step else value
+        whole = lax.dynamic_update_index_in_dim(whole, block, (index - step) % count, 0)
     return whole
 
 
@@ -333,9 +421,8 @@
     plane = lax.axis_index("coil")
     section = group * members + member
     table_z = half_tables(length_z)
-    table_y = table_z if length_y == length_z else half_tables(length_y)
-    tables = (table_z, table_z.T, table_y, table_y.T)
-    sampled = unpack_mask(mask_bits, length_z)
+    table_y = half_tables(length_y)
+    tables = tuple(jnp.asarray(value) for value in (table_z, table_z.T, table_y, table_y.T))
     count = conv1_w.shape[2]
     extra = jnp.concatenate(
         [conv1_b.T, jnp.broadcast_to(step_size.reshape(1, 1), (width, 1))], axis=1
@@ -346,73 +433,77 @@
             for part in (conv1_w[0].astype(F32), conv2_w[0].astype(F32), extra)
         ],
         axis=0,
-    )[None]
-    packed = gathered_rows(gathered_rows(packed, "member", 0), "group", 0)
+    )
+    packed = gathered(gathered(packed, "member"), "group")
+    packed = packed.reshape((cascades,) + packed.shape[2:])
 
     if planes == 1:
-        sides = []
+        sides, variants = [], [[0]]
     elif planes == 2:
-        sides = [None]
+        sides, variants = [None], [[0, 1], [0, -1]]
     else:
-        sides = [-1, 1]
+        sides, variants = [-1, 1], [[0, -1, 1]]
     neighbours = len(sides)
     involved = neighbours + 1
     per_row = -(-(involved * channels) // 8) * 8
-
-    def tap_of(side, sign):
-        if side is None:
-            return jnp.where(plane == 0, 1 + sign, 1 - sign)
-        return jnp.full((), 1 + sign * side, jnp.int32)
-
-    one = jnp.ones((), jnp.int32)
-    planes1 = [one] + [tap_of(side, 1) for side in sides]
-    planes2 = [one] + [tap_of(side, -1) for side in sides]
-    window = ROWS + 2
-    used = window * 3 * per_row
-    shape = (ROWS, count, used + 2 * ROWS)
-    row = lax.broadcasted_iota(jnp.int32, shape, 0)
-    tap = lax.broadcasted_iota(jnp.int32, shape, 1)
-    column = lax.broadcasted_iota(jnp.int32, shape, 2)
-    slot = column % per_row
-    wanted = jnp.full(shape, -1, jnp.int32)
-    for at, value in enumerate(planes1):
-        wanted = jnp.where(slot // channels == at, value, wanted)
-    select1 = (
-        (column < used)
-        & (tap // (9 * channels) == wanted)
-        & (tap // (3 * channels) % 3 == column // (3 * per_row) - row)
-        & (tap // channels % 3 == column // per_row % 3)
-        & (tap % channels == slot % channels)
-    ).astype(BF)
-    shape = (3, 3 * involved * channels * ROWS, count)
-    row = lax.broadcasted_iota(jnp.int32, shape, 1)
-    tap = lax.broadcasted_iota(jnp.int32, shape, 2)
-    at_plane = row // (channels * ROWS) % involved
-    wanted = jnp.full(shape, -1, jnp.int32)
-    for at, value in enumerate(planes2):
-        wanted = jnp.where(at_plane == at, value, wanted)
-    select2 = (
-        (tap // (9 * channels) == wanted)
-        & (tap // (3 * channels) % 3 == lax.broadcasted_iota(jnp.int32, shape, 0))
-        & (tap // channels % 3 == row // (involved * channels * ROWS))
-        & (tap % channels == row // ROWS % channels)
-    ).astype(BF)
-
+    chosen = [tap_selectors(channels, per_row, offsets) for offsets in variants]
+    select1, select2 = (jnp.asarray(np.stack(parts)) for parts in zip(*chosen))
+
+    place = jnp.stack([lax.axis_index("space"), plane, member]).astype(jnp.int32)
+    spaces = lax.axis_size("space")
     maps = lax.dynamic_index_in_dim(sens, group, 1, keepdims=False)
-    maps = lax.all_to_all(maps, "coil", split_axis=1, concat_axis=0, tiled=True)
-    maps = gathered_rows(maps[:, 0], "space", 1)
+    maps = lax.all_to_all(maps, "coil", split_axis=1, concat_axis=0, tiled=True)[:, 0]
+    coils = maps.shape[0]
+    maps = maps.reshape(coils, row_count, 2, length_z).transpose(0, 2, 1, 3)
     own_image = lax.dynamic_index_in_dim(image, group, 1, keepdims=False)[:, 0].astype(BF)
     own_adjoint = lax.dynamic_index_in_dim(adjoint, group, 1, keepdims=False)[:, 0].astype(BF)
-    base = gathered_rows(own_image, "space", 1)
-    target = gathered_rows(own_adjoint, "space", 1)
+    shared = members if phases % members == 0 and coils % members == 0 else 1
+    local = jnp.concatenate(
+        [
+            part.reshape(shared, -1, row_count, length_z)
+            for part in (own_image, maps, own_adjoint)
+        ],
+        axis=1,
+    )
+    mine = lax.dynamic_index_in_dim(local, member % shared, 0, keepdims=False)
+    blocks = []
+    for step in range(1, spaces):
+        block = ring(mine, "space", step)
+        blocks.append(block)
+        for offset in range(1, shared):
+            blocks.append(ring(block, "member", -offset))
 
     full = jax.ShapeDtypeStruct((channels, length_y, length_z), F32)
     half = jax.ShapeDtypeStruct((channels, length_y, length_z), BF)
     vmem = pl.BlockSpec(memory_space=pltpu.VMEM)
     smem = pl.BlockSpec(memory_space=pltpu.SMEM)
-    params = pltpu.CompilerParams(vmem_limit_bytes=56 * 1024 * 1024)
-
-    place = lax.axis_index("space").reshape(1)
+    params = pltpu.CompilerParams(vmem_limit_bytes=32 * 1024 * 1024)
+    base, maps, target = pl.pallas_call(
+        functools.partial(assemble_kernel, shared, spaces),
+        out_shape=(
+            half,
+            jax.ShapeDtypeStruct((2 * coils, length_y, length_z), BF),
+            half,
+        ),
+        in_specs=[smem] + [vmem] * (1 + len(blocks)),
+        out_specs=(vmem,) * 3,
+        compiler_params=params,
+    )(place, local, *blocks)
+    order = np.eye(length_y)[slot_order(length_y)].astype(BF)
+    column = slot_order(length_z)
+    columns = np.stack([column // 30, column % 30]).astype(np.int32)
+    weight1, weight2, sampled = pl.pallas_call(
+        functools.partial(prepare_kernel, width, per_row),
+        out_shape=(
+            jax.ShapeDtypeStruct((cascades, ROWS * width, select1.shape[2]), BF),
+            jax.ShapeDtypeStruct((cascades, select2.shape[2], (ROWS + 2) * width), BF),
+            jax.ShapeDtypeStruct((phases, length_y, length_z), F32),
+        ),
+        in_specs=[smem] + [vmem] * 6,
+        out_specs=(vmem,) * 3,
+        compiler_params=params,
+    )(place, packed, mask_bits, jnp.asarray(columns), jnp.asarray(order), select1, select2)
+
     rows_shape = jax.ShapeDtypeStruct((channels, row_count, length_z), F32)
 
     def consistency(cascade, base, parts):
@@ -427,20 +518,21 @@
 
     def refine(cascade, value, others, updated):
         padded = length_y + 2 * ROWS
+        height = row_count if cascade == cascades - 1 and row_count % (2 * ROWS) == 0 else length_y
+        shape = (channels, height, length_z)
         return pl.pallas_call(
             functools.partial(refine_kernel, neighbours, width, cascade),
-            out_shape=(full,) + (half,) * neighbours,
-            in_specs=[vmem] * (5 + neighbours),
+            out_shape=(jax.ShapeDtypeStruct(shape, F32),)
+            + (jax.ShapeDtypeStruct(shape, BF),) * neighbours,
+            in_specs=[smem] + [vmem] * (4 + neighbours),
             out_specs=(vmem,) * (1 + neighbours),
             scratch_shapes=[
                 pltpu.VMEM((length_z // LANES, padded * per_row, LANES), F32),
                 pltpu.VMEM((padded * 3 * per_row, length_z), BF),
                 pltpu.VMEM(((length_y + 2) * width, length_z), BF),
-                pltpu.VMEM((ROWS * width, select1.shape[2]), BF),
-                pltpu.VMEM((select2.shape[1], (ROWS + 2) * width), BF),
             ],
             compiler_params=params,
-        )(value, *others, updated, packed, select1, select2)
+        )(place, value, *others, updated, weight1, weight2)
 
     def exchanged(values):
         received = []
@@ -455,6 +547,8 @@
     row_start = lax.axis_index("space") * row_count
 
     def own_rows(value):
+        if value.shape[1] == row_count:
+            return value
         return lax.dynamic_slice_in_dim(value, row_start, row_count, 1)
 
     results = []

time: 185 us -> 130 us (0.70)
  Pallas kernels: 86.9 us -> 63.6 us
  other arithmetic: 22.4 us -> 1.24 us
  local copies, waits for them, and re-layouts: 16.3 us -> 5.91 us
  blocking collectives: 3.94 us -> 0 us
  waiting for transfers between devices: 33.7 us -> 35.9 us
    pallas_call x4, Pallas kernels: 47.7 us -> 31.2 us  [refine(): pl.pallas_call(functools.partial(refine_kernel, neighbours, width, cascad...]
    pallas_call x4, Pallas kernels: 39.2 us -> 29.3 us  [consistency(): pl.pallas_call(functools.partial(consistency_kernel, phases, width, casca...]
    dynamic_update_slice x15 -> x4, local copies, waits for them, and re-layouts: 5.73 us -> 0.05 us  [gathered(): lax.dynamic_update_index_in_dim(whole, block, (index - step) % count, 0)]
    unnamed x166 -> x27, local copies, waits for them, and re-layouts: 9.26 us -> 3.71 us
    all_to_all x1 -> x0, blocking collectives: 3.94 us -> none  [per_device(): maps = lax.all_to_all(maps, 'coil', split_axis=1, concat_axis=0, tiled=True)]
    convert_element_type x3 -> x0, other arithmetic: 3.89 us -> none  [the longest x1 1.49 us: unpack_mask(): return (jnp.right_shift(chosen, column % 30) & 1).astype(F32)]
    all_to_all x0 -> x1, starting transfers between devices: none -> 3.44 us  [per_device(): lax.all_to_all(maps, 'coil', split_axis=1, concat_axis=0, tiled=True)[:, 0]]
    and x6 -> x0, other arithmetic: 3.37 us -> none  [the longest x1 0.6 us: per_device(): tap // (9 * channels) == wanted]
  transfers between devices with their start and end apart: 20 -> 18, of which waited for: 15 -> 14; matrix products, arithmetic and copies ran while one was open for 15% -> 1% of each run, Pallas kernels for 0% -> 2%
where the time goes in v3:
time: 130 us; the launch traced here: 128 us
  Pallas kernels  63.6 us (49%)
  waiting for transfers between devices  35.9 us (28%)
  starting transfers between devices  20.1 us (15%)
  local copies, waits for them, and re-layouts  5.91 us (5%)
    pallas_call x4, Pallas kernels, refine(): pl.pallas_call(functools.partial(refine_kernel, neighbours, width, cascad...  31.2 us
    pallas_call x4, Pallas kernels, consistency(): pl.pallas_call(functools.partial(consistency_kernel, phases, width, casca...  29.3 us
    ppermute x8, waiting for transfers between devices, ring(): lax.ppermute(value, axis, [(i, (i + step) % count) for i in range(count)])  16.7 us
    ppermute x8, waiting for transfers between devices, exchanged(): received.append(lax.ppermute(value, 'coil', pairs))  13.8 us
    ppermute x8, starting transfers between devices, ring(): lax.ppermute(value, axis, [(i, (i + step) % count) for i in range(count)])  13.7 us
    ppermute x1, waiting for transfers between devices, per_device(): lax.ppermute(chosen, 'group', [(i, (i - step) % groups) for i in range(gr...  3.88 us
    unnamed x27, local copies, waits for them, and re-layouts  3.71 us
    all_to_all x1, starting transfers between devices, per_device(): lax.all_to_all(maps, 'coil', split_axis=1, concat_axis=0, tiled=True)[:, 0]  3.44 us
  transfers between devices with their start and end apart: 18, of which 14 were waited for; matrix products, arithmetic and copies ran while one was open for 1% of the time, Pallas kernels for 2%

profile of v3, /device:TPU:0, one launch (start us, length us, event | category | flops | bytes accessed | tf_op | source)
XLA Modules:
  0.0 127.8 jit_solution(9858909329586769745)
XLA Ops:
  0.0 1.0 copy-done
  1.1 0.7 copy.43
  1.8 3.4 %all-to-all-start = ((bf16[2,2,64,512]{3,2,0,1:T(8,128)(2,1)}), bf16[2,2,64,512]{3,2,0,1:T(8,128)(2,1)S(1)}, u32[]{:S(2)}, u32[]{:S(2)}) async-start(bf16[2,2,64,512]{3,2,0,1:T(8,128)(2,1)} %copy.43), calls=%async_computation | async-start | bytes 524288 | tf_op jit(solution)/shard_map/all_to_all | solution.py:455
  5.3 1.5 %all-to-all-done = bf16[2,2,64,512]{3,2,0,1:T(8,128)(2,1)S(1)} async-done(((bf16[2,2,64,512]{3,2,0,1:T(8,128)(2,1)}), bf16[2,2,64,512]{3,2,0,1:T(8,128)(2,1)S(1)}, u32[]{:S(2)}, u32[]{:S(2)}) %all-to-all-start) | async-done | bytes 262176 | tf_op jit(solution)/shard_map/all_to_all | solution.py:455
  6.8 0.1 reshape_squeeze.3
  6.9 1.1 dynamic-slice_convert_fusion
  8.0 0.1 pad_maximum_fusion.refs_0_
  8.1 3.1 %collective-permute-start = (bf16[8,64,256]{2,1,0:T(8,128)(2,1)S(1)}, bf16[8,64,256]{2,1,0:T(8,128)(2,1)S(1)}, u32[]{:S(2)}, u32[]{:S(2)}) collective-permute-start(bf16[8,64,256]{2,1,0:T(8,128)(2,1)S(1)} %dynamic-slice_bitcast_fusion), channel_id=1, source_target_pairs={{0,1},{1,2},{2,3},{3,0},{4,5},{5,6},{6,7},{7,4},{8,9},{9,10},{10,1... | collective-permute-start | bytes 786440 | tf_op jit(solution)/shard_map/ppermute | solution.py:397
  11.2 2.6 %collective-permute-start.2 = (bf16[8,64,256]{2,1,0:T(8,128)(2,1)S(1)}, bf16[8,64,256]{2,1,0:T(8,128)(2,1)S(1)}, u32[]{:S(2)}, u32[]{:S(2)}) collective-permute-start(bf16[8,64,256]{2,1,0:T(8,128)(2,1)S(1)} %dynamic-slice_bitcast_fusion), channel_id=1, source_target_pairs={{0,2},{1,3},{2,0},{3,1},{4,6},{5,7},{6,4},{7,5},{8,10},{9,11},{10,... | collective-permute-start | bytes 786440 | tf_op jit(solution)/shard_map/ppermute | solution.py:397
  13.8 1.3 %collective-permute-start.4 = (bf16[8,64,256]{2,1,0:T(8,128)(2,1)S(1)}, bf16[8,64,256]{2,1,0:T(8,128)(2,1)S(1)}, u32[]{:S(2)}, u32[]{:S(2)}) collective-permute-start(bf16[8,64,256]{2,1,0:T(8,128)(2,1)S(1)} %dynamic-slice_bitcast_fusion), channel_id=1, source_target_pairs={{0,3},{1,0},{2,1},{3,2},{4,7},{5,4},{6,5},{7,6},{8,11},{9,8},{10,9... | collective-permute-start | bytes 786440 | tf_op jit(solution)/shard_map/ppermute | solution.py:397
  15.1 0.1 copy.45
  15.3 0.1 copy.46
  16.1 0.6 copy-done.11
  16.7 0.1 pad_maximum_fusion.1
  16.8 1.6 %collective-permute-start.6 = (f32[96,128]{0,1:T(8,128)S(1)}, f32[96,128]{0,1:T(8,128)S(1)}, u32[]{:S(2)}, u32[]{:S(2)}) collective-permute-start(f32[96,128]{0,1:T(8,128)S(1)} %pad_maximum_fusion.1), channel_id=1, source_target_pairs={{0,8},{8,0},{1,9},{9,1},{2,10},{10,2},{3,11},{11,3},{4,12},{12,4},... | collective-permute-start | bytes 147464 | tf_op jit(solution)/shard_map/ppermute | solution.py:397
  18.4 0.1 fusion
  18.5 0.1 copy.47
  18.6 0.1 pad_add_fusion.place_ref
  18.7 0.7 copy-done.8
  19.4 0.1 copy.49.bits_ref
  19.6 1.6 %collective-permute-done.6 = f32[96,128]{0,1:T(8,128)S(1)} collective-permute-done((f32[96,128]{0,1:T(8,128)S(1)}, f32[96,128]{0,1:T(8,128)S(1)}, u32[]{:S(2)}, u32[]{:S(2)}) %collective-permute-start.6) | collective-permute-done | bytes 49184 | tf_op jit(solution)/shard_map/ppermute | solution.py:397
  21.2 0.1 copy.48
  21.3 0.0 copy-start.3
  21.3 1.6 %collective-permute-start.7 = (f32[2,96,128]{2,1,0:T(8,128)S(1)}, f32[2,96,128]{2,1,0:T(8,128)S(1)}, u32[]{:S(2)}, u32[]{:S(2)}) collective-permute-start(f32[2,96,128]{2,1,0:T(8,128)S(1)} %constant_dynamic-update-slice_fusion), channel_id=1, source_target_pairs={{0,16},{16,0},{1,17},{17,1},{2,18},{18,2},{3,19},{19,3},{4,20},{20... | collective-permute-start | bytes 294920 | tf_op jit(solution)/shard_map/ppermute | solution.py:397
  22.9 1.5 %collective-permute-start.1 = (bf16[8,64,256]{2,1,0:T(8,128)(2,1)S(1)}, bf16[8,64,256]{2,1,0:T(8,128)(2,1)S(1)}, u32[]{:S(2)}, u32[]{:S(2)}) collective-permute-start(bf16[8,64,256]{2,1,0:T(8,128)(2,1)S(1)} %collective-permute-done.refs_1_), channel_id=1, source_target_pairs={{0,8},{8,0},{1,9},{9,1},{2,10},{10,2},{3,11},{11,3},{4,12},{12,4},... | collective-permute-start | bytes 786440 | tf_op jit(solution)/shard_map/ppermute | solution.py:397
  24.4 6.8 %collective-permute-done.2.refs_3_ = bf16[8,64,256]{2,1,0:T(8,128)(2,1)S(1)} collective-permute-done((bf16[8,64,256]{2,1,0:T(8,128)(2,1)S(1)}, bf16[8,64,256]{2,1,0:T(8,128)(2,1)S(1)}, u32[]{:S(2)}, u32[]{:S(2)}) %collective-permute-start.2) | collective-permute-done | bytes 262176 | tf_op jit(solution)/shard_map/ppermute | solution.py:397
  31.2 1.5 %collective-permute-start.3 = (bf16[8,64,256]{2,1,0:T(8,128)(2,1)S(1)}, bf16[8,64,256]{2,1,0:T(8,128)(2,1)S(1)}, u32[]{:S(2)}, u32[]{:S(2)}) collective-permute-start(bf16[8,64,256]{2,1,0:T(8,128)(2,1)S(1)} %collective-permute-done.2.refs_3_), channel_id=1, source_target_pairs={{0,8},{8,0},{1,9},{9,1},{2,10},{10,2},{3,11},{11,3},{4,12},{12,4},... | collective-permute-start | bytes 786440 | tf_op jit(solution)/shard_map/ppermute | solution.py:397
  32.7 0.5 collective-permute-start.5
  33.3 0.0 copy-start.5
  33.3 0.0 copy-start.4
  33.4 0.8 copy-done.5
  34.2 0.1 copy-done.4
  34.2 2.4 %shard_map.155 = (bf16[4,256,256]{2,1,0:T(8,128)(2,1)S(1)}, bf16[4,192,320]{2,1,0:T(8,128)(2,1)S(1)}, f32[2,256,256]{2,1,0:T(8,128)S(1)}) custom-call(s32[3]{0:T(128)S(1)} %pad_add_fusion.place_ref, f32[4,96,128]{2,1,0:T(8,128)S(1)} %bitcast.43, s32[2,256,9]{2,1,0:T(8,128)S(1)} %copy.49.bits_ref, s32[2,256]{1,0:T(2,128)S(1)} %copy-done.6, ...), custom_call_target="tpu_custom_call" | custom-call | tf_op jit(solution)/shard_map/pallas_call | solution.py:495
  36.7 3.7 %collective-permute-done.3.refs_4_ = bf16[8,64,256]{2,1,0:T(8,128)(2,1)S(1)} collective-permute-done((bf16[8,64,256]{2,1,0:T(8,128)(2,1)S(1)}, bf16[8,64,256]{2,1,0:T(8,128)(2,1)S(1)}, u32[]{:S(2)}, u32[]{:S(2)}) %collective-permute-start.3) | collective-permute-done | bytes 262176 | tf_op jit(solution)/shard_map/ppermute | solution.py:397
  40.4 4.6 %collective-permute-done.5.refs_6_ = bf16[8,64,256]{2,1,0:T(8,128)(2,1)S(1)} collective-permute-done((bf16[8,64,256]{2,1,0:T(8,128)(2,1)S(1)}, bf16[8,64,256]{2,1,0:T(8,128)(2,1)S(1)}, u32[]{:S(2)}, u32[]{:S(2)}) %collective-permute-start.5) | collective-permute-done | bytes 262176 | tf_op jit(solution)/shard_map/ppermute | solution.py:397
  45.0 0.7 shard_map.154
  45.7 7.8 %shard_map.156 = (f32[4,64,256]{2,1,0:T(8,128)}, f32[4,256,256]{2,1,0:T(8,128)S(1)}, bf16[4,256,256]{2,1,0:T(8,128)(2,1)S(1)}) custom-call(s32[3]{0:T(128)S(1)} %pad_add_fusion.place_ref, bf16[4,256,256]{2,1,0:T(8,128)(2,1)S(1)} %get-tuple-element.30.base_ref, bf16[8,256,256]{2,1,0:T(8,128)(2,1)S(1)} %get-tuple-element.31.refs_0_.refs_1_, ...), custom_call_target="tpu_custom_call" | custom-call | tf_op jit(solution)/shard_map/pallas_call | solution.py:510
  53.5 1.9 %collective-permute-done.8.refs_0_ = bf16[4,256,256]{2,1,0:T(8,128)(2,1)S(1)} collective-permute-done((bf16[4,256,256]{2,1,0:T(8,128)(2,1)S(1)}, bf16[4,256,256]{2,1,0:T(8,128)(2,1)S(1)}, u32[]{:S(2)}, u32[]{:S(2)}) %collective-permute-start.8) | collective-permute-done | bytes 524320 | tf_op jit(solution)/shard_map/ppermute | solution.py:544
  55.4 9.1 %shard_map.157 = (f32[4,256,256]{2,1,0:T(8,128)S(1)}, bf16[4,256,256]{2,1,0:T(8,128)(2,1)S(1)}) custom-call(s32[3]{0:T(128)S(1)} %pad_add_fusion.place_ref, bf16[4,256,256]{2,1,0:T(8,128)(2,1)S(1)} %get-tuple-element.34.v_ref, bf16[4,256,256]{2,1,0:T(8,128)(2,1)S(1)} %collective-permute-done.8.refs_0_, f32[4,256,256]{2,1,0:T(8,128)S(1)} %get-tuple-element.35.refs_1_, ...), custom_call_target="tpu_custom_call" | custom-call | tf_op jit(solution)/shard_map/pallas_call | solution.py:523
  64.6 0.2 collective-permute-start.9
  64.8 1.8 %collective-permute-done.9.refs_0_ = bf16[4,256,256]{2,1,0:T(8,128)(2,1)S(1)} collective-permute-done((bf16[4,256,256]{2,1,0:T(8,128)(2,1)S(1)}, bf16[4,256,256]{2,1,0:T(8,128)(2,1)S(1)}, u32[]{:S(2)}, u32[]{:S(2)}) %collective-permute-start.9) | collective-permute-done | bytes 524320 | tf_op jit(solution)/shard_map/ppermute | solution.py:544
  66.6 7.1 %shard_map.158 = (f32[4,64,256]{2,1,0:T(8,128)S(1)}, f32[4,256,256]{2,1,0:T(8,128)S(1)}, bf16[4,256,256]{2,1,0:T(8,128)(2,1)S(1)}) custom-call(s32[3]{0:T(128)S(1)} %pad_add_fusion.place_ref, f32[4,256,256]{2,1,0:T(8,128)S(1)} %get-tuple-element.38.base_ref, bf16[4,256,256]{2,1,0:T(8,128)(2,1)S(1)} %collective-permute-done.9.refs_0_, ...), custom_call_target="tpu_custom_call" | custom-call | tf_op jit(solution)/shard_map/pallas_call | solution.py:510
  73.7 0.2 collective-permute-start.10
  73.9 1.8 %collective-permute-done.10.refs_0_ = bf16[4,256,256]{2,1,0:T(8,128)(2,1)S(1)} collective-permute-done((bf16[4,256,256]{2,1,0:T(8,128)(2,1)S(1)}, bf16[4,256,256]{2,1,0:T(8,128)(2,1)S(1)}, u32[]{:S(2)}, u32[]{:S(2)}) %collective-permute-start.10) | collective-permute-done | bytes 524320 | tf_op jit(solution)/shard_map/ppermute | solution.py:544
  75.7 9.1 %shard_map.159 = (f32[4,256,256]{2,1,0:T(8,128)S(1)}, bf16[4,256,256]{2,1,0:T(8,128)(2,1)S(1)}) custom-call(s32[3]{0:T(128)S(1)} %pad_add_fusion.place_ref, bf16[4,256,256]{2,1,0:T(8,128)(2,1)S(1)} %get-tuple-element.40.v_ref, bf16[4,256,256]{2,1,0:T(8,128)(2,1)S(1)} %collective-permute-done.10.refs_0_, f32[4,256,256]{2,1,0:T(8,128)S(1)} %get-tuple-element.41.refs_1_, ...), custom_call_target="tpu_custom_call" | custom-call | tf_op jit(solution)/shard_map/pallas_call | solution.py:523
  84.8 0.2 collective-permute-start.11
  85.0 1.8 %collective-permute-done.11.refs_0_ = bf16[4,256,256]{2,1,0:T(8,128)(2,1)S(1)} collective-permute-done((bf16[4,256,256]{2,1,0:T(8,128)(2,1)S(1)}, bf16[4,256,256]{2,1,0:T(8,128)(2,1)S(1)}, u32[]{:S(2)}, u32[]{:S(2)}) %collective-permute-start.11) | collective-permute-done | bytes 524320 | tf_op jit(solution)/shard_map/ppermute | solution.py:544
  86.8 7.1 %shard_map.160 = (f32[4,64,256]{2,1,0:T(8,128)S(1)}, f32[4,256,256]{2,1,0:T(8,128)S(1)}, bf16[4,256,256]{2,1,0:T(8,128)(2,1)S(1)}) custom-call(s32[3]{0:T(128)S(1)} %pad_add_fusion.place_ref, f32[4,256,256]{2,1,0:T(8,128)S(1)} %get-tuple-element.42.base_ref, bf16[4,256,256]{2,1,0:T(8,128)(2,1)S(1)} %collective-permute-done.11.refs_0_, ...), custom_call_target="tpu_custom_call" | custom-call | tf_op jit(solution)/shard_map/pallas_call | solution.py:510
  93.9 0.2 collective-permute-start.12
  94.1 1.8 %collective-permute-done.12.refs_0_ = bf16[4,256,256]{2,1,0:T(8,128)(2,1)S(1)} collective-permute-done((bf16[4,256,256]{2,1,0:T(8,128)(2,1)S(1)}, bf16[4,256,256]{2,1,0:T(8,128)(2,1)S(1)}, u32[]{:S(2)}, u32[]{:S(2)}) %collective-permute-start.12) | collective-permute-done | bytes 524320 | tf_op jit(solution)/shard_map/ppermute | solution.py:544
  95.9 9.1 %shard_map.161 = (f32[4,256,256]{2,1,0:T(8,128)S(1)}, bf16[4,256,256]{2,1,0:T(8,128)(2,1)S(1)}) custom-call(s32[3]{0:T(128)S(1)} %pad_add_fusion.place_ref, bf16[4,256,256]{2,1,0:T(8,128)(2,1)S(1)} %get-tuple-element.44.v_ref, bf16[4,256,256]{2,1,0:T(8,128)(2,1)S(1)} %collective-permute-done.12.refs_0_, f32[4,256,256]{2,1,0:T(8,128)S(1)} %get-tuple-element.45.refs_1_, ...), custom_call_target="tpu_custom_call" | custom-call | tf_op jit(solution)/shard_map/pallas_call | solution.py:523
  105.0 0.2 collective-permute-start.13
  105.2 1.8 %collective-permute-done.13.refs_0_ = bf16[4,256,256]{2,1,0:T(8,128)(2,1)S(1)} collective-permute-done((bf16[4,256,256]{2,1,0:T(8,128)(2,1)S(1)}, bf16[4,256,256]{2,1,0:T(8,128)(2,1)S(1)}, u32[]{:S(2)}, u32[]{:S(2)}) %collective-permute-start.13) | collective-permute-done | bytes 524320 | tf_op jit(solution)/shard_map/ppermute | solution.py:544
  107.0 7.1 %shard_map.162 = (f32[4,64,256]{2,1,0:T(8,128)S(1)}, f32[4,256,256]{2,1,0:T(8,128)S(1)}, bf16[4,256,256]{2,1,0:T(8,128)(2,1)S(1)}) custom-call(s32[3]{0:T(128)S(1)} %pad_add_fusion.place_ref, f32[4,256,256]{2,1,0:T(8,128)S(1)} %get-tuple-element.46.base_ref, bf16[4,256,256]{2,1,0:T(8,128)(2,1)S(1)} %collective-permute-done.13.refs_0_, ...), custom_call_target="tpu_custom_call" | custom-call | tf_op jit(solution)/shard_map/pallas_call | solution.py:510
  114.2 0.2 collective-permute-start.14
  114.4 1.8 %collective-permute-done.14.refs_0_ = bf16[4,256,256]{2,1,0:T(8,128)(2,1)S(1)} collective-permute-done((bf16[4,256,256]{2,1,0:T(8,128)(2,1)S(1)}, bf16[4,256,256]{2,1,0:T(8,128)(2,1)S(1)}, u32[]{:S(2)}, u32[]{:S(2)}) %collective-permute-start.14) | collective-permute-done | bytes 524320 | tf_op jit(solution)/shard_map/ppermute | solution.py:544
  116.2 3.8 %shard_map.163 = (f32[4,64,256]{2,1,0:T(8,128)S(1)}, bf16[4,64,256]{2,1,0:T(8,128)(2,1)S(1)}) custom-call(s32[3]{0:T(128)S(1)} %pad_add_fusion.place_ref, bf16[4,256,256]{2,1,0:T(8,128)(2,1)S(1)} %get-tuple-element.48.v_ref, bf16[4,256,256]{2,1,0:T(8,128)(2,1)S(1)} %collective-permute-done.14.refs_0_, f32[4,256,256]{2,1,0:T(8,128)S(1)} %get-tuple-element.49.refs_1_, ...), custom_call_target="tpu_custom_call" | custom-call | tf_op jit(solution)/shard_map/pallas_call | solution.py:523
  120.0 0.2 collective-permute-start.15
  120.2 1.2 collective-permute-done.15
  121.4 0.1 select_convert_fusion
  121.5 1.6 %collective-permute-start.16 = (bf16[4,64,256]{2,1,0:T(8,128)(2,1)S(1)}, bf16[4,64,256]{2,1,0:T(8,128)(2,1)S(1)}, u32[]{:S(2)}, u32[]{:S(2)}) collective-permute-start(bf16[4,64,256]{2,1,0:T(8,128)(2,1)S(1)} %select_convert_fusion), channel_id=1, source_target_pairs={{0,16},{16,0},{1,17},{17,1},{2,18},{18,2},{3,19},{19,3},{4,20},{20... | collective-permute-start | bytes 393224 | tf_op jit(solution)/shard_map/ppermute | solution.py:582
  123.1 0.1 bitcast_dynamic-update-slice_fusion
  123.2 3.9 %collective-permute-done.16 = bf16[4,64,256]{2,1,0:T(8,128)(2,1)S(1)} collective-permute-done((bf16[4,64,256]{2,1,0:T(8,128)(2,1)S(1)}, bf16[4,64,256]{2,1,0:T(8,128)(2,1)S(1)}, u32[]{:S(2)}, u32[]{:S(2)}) %collective-permute-start.16) | collective-permute-done | bytes 131104 | tf_op jit(solution)/shard_map/ppermute | solution.py:582
  127.1 0.7 convert_dynamic-update-slice_fusion
  (33 shorter events, 0.3 us)
Async XLA Ops:
  0.0 1.0 copy-start
  1.8 5.0 %all-to-all-start = ((bf16[2,2,64,512]{3,2,0,1:T(8,128)(2,1)}), bf16[2,2,64,512]{3,2,0,1:T(8,128)(2,1)S(1)}, u32[]{:S(2)}, u32[]{:S(2)}) async-start(bf16[2,2,64,512]{3,2,0,1:T(8,128)(2,1)} %copy.43), calls=%async_computation | async-start | bytes 524288 | tf_op jit(solution)/shard_map/all_to_all | solution.py:455
  8.0 7.1 %copy-start.9 = (bf16[1,32,108]{2,1,0:T(8,128)(2,1)S(1)}, bf16[1,32,108]{2,1,0:T(8,128)(2,1)}, u32[]{:S(2)}) copy-start(bf16[1,32,108]{2,1,0:T(8,128)(2,1)} %param.21) | copy-start | bytes 20740
  8.1 7.2 %copy-start.10 = (bf16[1,32,108]{2,1,0:T(8,128)(2,1)S(1)}, bf16[1,32,108]{2,1,0:T(8,128)(2,1)}, u32[]{:S(2)}) copy-start(bf16[1,32,108]{2,1,0:T(8,128)(2,1)} %param.23) | copy-start | bytes 20740
  8.1 14.8 %collective-permute-start = (bf16[8,64,256]{2,1,0:T(8,128)(2,1)S(1)}, bf16[8,64,256]{2,1,0:T(8,128)(2,1)S(1)}, u32[]{:S(2)}, u32[]{:S(2)}) collective-permute-start(bf16[8,64,256]{2,1,0:T(8,128)(2,1)S(1)} %dynamic-slice_bitcast_fusion), channel_id=1, source_target_pairs={{0,1},{1,2},{2,3},{3,0},{4,5},{5,6},{6,7},{7,4},{8,9},{9,10},{10,1... | collective-permute-start | bytes 786440 | tf_op jit(solution)/shard_map/ppermute | solution.py:397
  11.2 20.0 %collective-permute-start.2 = (bf16[8,64,256]{2,1,0:T(8,128)(2,1)S(1)}, bf16[8,64,256]{2,1,0:T(8,128)(2,1)S(1)}, u32[]{:S(2)}, u32[]{:S(2)}) collective-permute-start(bf16[8,64,256]{2,1,0:T(8,128)(2,1)S(1)} %dynamic-slice_bitcast_fusion), channel_id=1, source_target_pairs={{0,2},{1,3},{2,0},{3,1},{4,6},{5,7},{6,4},{7,5},{8,10},{9,11},{10,... | collective-permute-start | bytes 786440 | tf_op jit(solution)/shard_map/ppermute | solution.py:397
  13.8 18.9 %collective-permute-start.4 = (bf16[8,64,256]{2,1,0:T(8,128)(2,1)S(1)}, bf16[8,64,256]{2,1,0:T(8,128)(2,1)S(1)}, u32[]{:S(2)}, u32[]{:S(2)}) collective-permute-start(bf16[8,64,256]{2,1,0:T(8,128)(2,1)S(1)} %dynamic-slice_bitcast_fusion), channel_id=1, source_target_pairs={{0,3},{1,0},{2,1},{3,2},{4,7},{5,4},{6,5},{7,6},{8,11},{9,8},{10,9... | collective-permute-start | bytes 786440 | tf_op jit(solution)/shard_map/ppermute | solution.py:397
  16.1 0.7 copy-start.11
  16.8 4.3 %collective-permute-start.6 = (f32[96,128]{0,1:T(8,128)S(1)}, f32[96,128]{0,1:T(8,128)S(1)}, u32[]{:S(2)}, u32[]{:S(2)}) collective-permute-start(f32[96,128]{0,1:T(8,128)S(1)} %pad_maximum_fusion.1), channel_id=1, source_target_pairs={{0,8},{8,0},{1,9},{9,1},{2,10},{10,2},{3,11},{11,3},{4,12},{12,4},... | collective-permute-start | bytes 147464 | tf_op jit(solution)/shard_map/ppermute | solution.py:397
  18.7 0.7 copy-start.8
  21.3 12.1 %copy-start.3 = (bf16[2,3,192,108]{3,2,1,0:T(8,128)(2,1)S(1)}, bf16[2,3,192,108]{3,2,1,0:T(8,128)(2,1)}, u32[]{:S(2)}) copy-start(bf16[2,3,192,108]{3,2,1,0:T(8,128)(2,1)} %constant.108.clone.select2_ref) | copy-start | bytes 746500
  21.3 12.0 %collective-permute-start.7 = (f32[2,96,128]{2,1,0:T(8,128)S(1)}, f32[2,96,128]{2,1,0:T(8,128)S(1)}, u32[]{:S(2)}, u32[]{:S(2)}) collective-permute-start(f32[2,96,128]{2,1,0:T(8,128)S(1)} %constant_dynamic-update-slice_fusion), channel_id=1, source_target_pairs={{0,16},{16,0},{1,17},{17,1},{2,18},{18,2},{3,19},{19,3},{4,20},{20... | collective-permute-start | bytes 294920 | tf_op jit(solution)/shard_map/ppermute | solution.py:397
  22.9 13.8 %collective-permute-start.1 = (bf16[8,64,256]{2,1,0:T(8,128)(2,1)S(1)}, bf16[8,64,256]{2,1,0:T(8,128)(2,1)S(1)}, u32[]{:S(2)}, u32[]{:S(2)}) collective-permute-start(bf16[8,64,256]{2,1,0:T(8,128)(2,1)S(1)} %collective-permute-done.refs_1_), channel_id=1, source_target_pairs={{0,8},{8,0},{1,9},{9,1},{2,10},{10,2},{3,11},{11,3},{4,12},{12,4},... | collective-permute-start | bytes 786440 | tf_op jit(solution)/shard_map/ppermute | solution.py:397
  31.2 9.2 %collective-permute-start.3 = (bf16[8,64,256]{2,1,0:T(8,128)(2,1)S(1)}, bf16[8,64,256]{2,1,0:T(8,128)(2,1)S(1)}, u32[]{:S(2)}, u32[]{:S(2)}) collective-permute-start(bf16[8,64,256]{2,1,0:T(8,128)(2,1)S(1)} %collective-permute-done.2.refs_3_), channel_id=1, source_target_pairs={{0,8},{8,0},{1,9},{9,1},{2,10},{10,2},{3,11},{11,3},{4,12},{12,4},... | collective-permute-start | bytes 786440 | tf_op jit(solution)/shard_map/ppermute | solution.py:397
  32.7 12.3 %collective-permute-start.5 = (bf16[8,64,256]{2,1,0:T(8,128)(2,1)S(1)}, bf16[8,64,256]{2,1,0:T(8,128)(2,1)S(1)}, u32[]{:S(2)}, u32[]{:S(2)}) collective-permute-start(bf16[8,64,256]{2,1,0:T(8,128)(2,1)S(1)} %collective-permute-done.4.refs_5_), channel_id=1, source_target_pairs={{0,8},{8,0},{1,9},{9,1},{2,10},{10,2},{3,11},{11,3},{4,12},{12,4},... | collective-permute-start | bytes 786440 | tf_op jit(solution)/shard_map/ppermute | solution.py:397
  33.3 0.9 copy-start.5
  33.3 0.9 copy-start.4
  33.3 0.9 copy-start.6
  36.7 9.0 %copy-start.1 = (bf16[256,256]{1,0:T(8,128)(2,1)S(1)}, bf16[256,256]{1,0:T(8,128)(2,1)}, u32[]{:S(2)}) copy-start(bf16[256,256]{1,0:T(8,128)(2,1)} %constant.105.clone.refs_4_.refs_6_.refs_5_.refs_7_) | copy-start | bytes 393220
  36.7 9.0 %copy-start.2 = (bf16[256,256]{1,0:T(8,128)(2,1)S(1)}, bf16[256,256]{1,0:T(8,128)(2,1)}, u32[]{:S(2)}) copy-start(bf16[256,256]{1,0:T(8,128)(2,1)} %constant.106.clone.refs_5_.refs_7_.refs_6_.refs_8_) | copy-start | bytes 393220
  53.5 1.9 %collective-permute-start.8 = (bf16[4,256,256]{2,1,0:T(8,128)(2,1)S(1)}, bf16[4,256,256]{2,1,0:T(8,128)(2,1)S(1)}, u32[]{:S(2)}, u32[]{:S(2)}) collective-permute-start(bf16[4,256,256]{2,1,0:T(8,128)(2,1)S(1)} %get-tuple-element.34.v_ref), channel_id=1, source_target_pairs={{0,4},{4,0},{1,5},{5,1},{2,6},{6,2},{3,7},{7,3},{8,12},{12,8},{9,1... | collective-permute-start | bytes 1572872 | tf_op jit(solution)/shard_map/ppermute | solution.py:544
  64.6 2.0 %collective-permute-start.9 = (bf16[4,256,256]{2,1,0:T(8,128)(2,1)S(1)}, bf16[4,256,256]{2,1,0:T(8,128)(2,1)S(1)}, u32[]{:S(2)}, u32[]{:S(2)}) collective-permute-start(bf16[4,256,256]{2,1,0:T(8,128)(2,1)S(1)} %get-tuple-element.39), channel_id=1, source_target_pairs={{0,4},{4,0},{1,5},{5,1},{2,6},{6,2},{3,7},{7,3},{8,12},{12,8},{9,1... | collective-permute-start | bytes 1572872 | tf_op jit(solution)/shard_map/ppermute | solution.py:544
  73.7 2.0 %collective-permute-start.10 = (bf16[4,256,256]{2,1,0:T(8,128)(2,1)S(1)}, bf16[4,256,256]{2,1,0:T(8,128)(2,1)S(1)}, u32[]{:S(2)}, u32[]{:S(2)}) collective-permute-start(bf16[4,256,256]{2,1,0:T(8,128)(2,1)S(1)} %get-tuple-element.40.v_ref), channel_id=1, source_target_pairs={{0,4},{4,0},{1,5},{5,1},{2,6},{6,2},{3,7},{7,3},{8,12},{12,8},{9,1... | collective-permute-start | bytes 1572872 | tf_op jit(solution)/shard_map/ppermute | solution.py:544
  84.8 2.0 %collective-permute-start.11 = (bf16[4,256,256]{2,1,0:T(8,128)(2,1)S(1)}, bf16[4,256,256]{2,1,0:T(8,128)(2,1)S(1)}, u32[]{:S(2)}, u32[]{:S(2)}) collective-permute-start(bf16[4,256,256]{2,1,0:T(8,128)(2,1)S(1)} %get-tuple-element.43), channel_id=1, source_target_pairs={{0,4},{4,0},{1,5},{5,1},{2,6},{6,2},{3,7},{7,3},{8,12},{12,8},{9,1... | collective-permute-start | bytes 1572872 | tf_op jit(solution)/shard_map/ppermute | solution.py:544
  93.9 2.0 %collective-permute-start.12 = (bf16[4,256,256]{2,1,0:T(8,128)(2,1)S(1)}, bf16[4,256,256]{2,1,0:T(8,128)(2,1)S(1)}, u32[]{:S(2)}, u32[]{:S(2)}) collective-permute-start(bf16[4,256,256]{2,1,0:T(8,128)(2,1)S(1)} %get-tuple-element.44.v_ref), channel_id=1, source_target_pairs={{0,4},{4,0},{1,5},{5,1},{2,6},{6,2},{3,7},{7,3},{8,12},{12,8},{9,1... | collective-permute-start | bytes 1572872 | tf_op jit(solution)/shard_map/ppermute | solution.py:544
  105.0 2.0 %collective-permute-start.13 = (bf16[4,256,256]{2,1,0:T(8,128)(2,1)S(1)}, bf16[4,256,256]{2,1,0:T(8,128)(2,1)S(1)}, u32[]{:S(2)}, u32[]{:S(2)}) collective-permute-start(bf16[4,256,256]{2,1,0:T(8,128)(2,1)S(1)} %get-tuple-element.47), channel_id=1, source_target_pairs={{0,4},{4,0},{1,5},{5,1},{2,6},{6,2},{3,7},{7,3},{8,12},{12,8},{9,1... | collective-permute-start | bytes 1572872 | tf_op jit(solution)/shard_map/ppermute | solution.py:544
  114.2 2.0 %collective-permute-start.14 = (bf16[4,256,256]{2,1,0:T(8,128)(2,1)S(1)}, bf16[4,256,256]{2,1,0:T(8,128)(2,1)S(1)}, u32[]{:S(2)}, u32[]{:S(2)}) collective-permute-start(bf16[4,256,256]{2,1,0:T(8,128)(2,1)S(1)} %get-tuple-element.48.v_ref), channel_id=1, source_target_pairs={{0,4},{4,0},{1,5},{5,1},{2,6},{6,2},{3,7},{7,3},{8,12},{12,8},{9,1... | collective-permute-start | bytes 1572872 | tf_op jit(solution)/shard_map/ppermute | solution.py:544
  120.0 1.4 %collective-permute-start.15 = (bf16[4,64,256]{2,1,0:T(8,128)(2,1)S(1)}, bf16[4,64,256]{2,1,0:T(8,128)(2,1)S(1)}, u32[]{:S(2)}, u32[]{:S(2)}) collective-permute-start(bf16[4,64,256]{2,1,0:T(8,128)(2,1)S(1)} %get-tuple-element.51), channel_id=1, source_target_pairs={{0,4},{4,0},{1,5},{5,1},{2,6},{6,2},{3,7},{7,3},{8,12},{12,8},{9,1... | collective-permute-start | bytes 393224 | tf_op jit(solution)/shard_map/ppermute | solution.py:544
  121.5 5.6 %collective-permute-start.16 = (bf16[4,64,256]{2,1,0:T(8,128)(2,1)S(1)}, bf16[4,64,256]{2,1,0:T(8,128)(2,1)S(1)}, u32[]{:S(2)}, u32[]{:S(2)}) collective-permute-start(bf16[4,64,256]{2,1,0:T(8,128)(2,1)S(1)} %select_convert_fusion), channel_id=1, source_target_pairs={{0,16},{16,0},{1,17},{17,1},{2,18},{18,2},{3,19},{19,3},{4,20},{20... | collective-permute-start | bytes 393224 | tf_op jit(solution)/shard_map/ppermute | solution.py:582
  123.2 3.9 %copy-start.7 = (f32[1,4,2,1,64,256]{5,4,3,2,1,0:T(8,128)}, f32[1,4,2,1,64,256]{5,4,3,2,1,0:T(8,128)S(1)}, u32[]{:S(2)}) copy-start(f32[1,4,2,1,64,256]{5,4,3,2,1,0:T(8,128)S(1)} %bitcast_dynamic-update-slice_fusion) | copy-start | bytes 1572868

commit v4 on v3

--- a/solution.py
+++ b/solution.py
@@ -80,13 +80,17 @@
 
 
 def first_lane(on, other):
-    lane = lax.broadcasted_iota(jnp.int32, on.shape, 1)
+    lane = lax.broadcasted_iota(jnp.int32, on.shape, on.ndim - 1)
     return jnp.where(lane == 0, on, other)
 
 
 def first_row(on, other):
-    row = lax.broadcasted_iota(jnp.int32, (8, on.shape[1]), 0)
-    return jnp.concatenate([jnp.where(row == 0, on[:8], other[:8]), other[8:]], axis=0)
+    row = lax.broadcasted_iota(jnp.int32, on.shape, on.ndim - 2)
+    return jnp.where(row == 0, on, other)
+
+
+def other_rows(on, other):
+    return other
 
 
 def spread(cos_re, sin_re, cos_im, sin_im, pick):
@@ -121,76 +125,117 @@
         v_ref,
         image,
         total,
+        rounded,
+        kz,
+        kspace,
+        spectrum,
+        along_z,
     ) = refs[neighbours:]
     channels, length_y, length_z = base_ref.shape
-    half_y, half_z = length_y // 2, length_z // 2
+    half_z = length_z // 2
     for channel in range(channels):
         value = base_ref[channel].astype(F32)
         for part in part_refs:
             value = value + part[channel].astype(F32)
         image[channel] = value
+        rounded[channel] = value.astype(BF).astype(F32)
         total[channel] = -adjoint_ref[channel].astype(F32)
     row_count = rows_ref.shape[1]
     start = pl.multiple_of(place_ref[0] * row_count, row_count)
     rows_ref[...] = image[:, pl.ds(start, row_count), :]
 
-    def item(map_re, map_im, phase):
-        image_re = image[2 * phase].astype(BF).astype(F32)
-        image_im = image[2 * phase + 1].astype(BF).astype(F32)
-        coil_img = joined(
-            [map_re * image_re - map_im * image_im, map_re * image_im + map_im * image_re], 0
+    def multiplied(index, phase):
+        parts = []
+        for at in range(0, length_y, ROWS):
+            rows = slice(at, at + ROWS)
+            map_re = maps_ref[2 * index, rows]
+            map_im = maps_ref[2 * index + 1, rows]
+            image_re = rounded[2 * phase, rows]
+            image_im = rounded[2 * phase + 1, rows]
+            parts.append(map_re * image_re - map_im * image_im)
+            parts.append(map_re * image_im + map_im * image_re)
+        value = dot(joined(parts, 0), table_zt[...]).reshape(length_y // ROWS, 2, ROWS, length_z)
+        kz[phase, :, :length_z] = value[:, 0].reshape(length_y, length_z).astype(BF)
+        kz[phase, :, length_z:] = value[:, 1].reshape(length_y, length_z).astype(BF)
+
+    def transformed(phase):
+        kspace[phase] = dot(table_y[...], kz[phase])
+
+    def masked(phase):
+        for at in range(0, length_y, 2 * ROWS):
+            upper = kspace[phase, at : at + ROWS]
+            lower = kspace[phase, at + ROWS : at + 2 * ROWS]
+            pick = other_rows if at else first_row
+            cut = [slice(half_z * part, half_z * (part + 1)) for part in range(4)]
+            even_re, odd_re, even_im, odd_im = cut
+            cos = spread(
+                upper[:, even_re], lower[:, even_re], upper[:, even_im], lower[:, even_im], pick
+            )
+            sin = spread(
+                upper[:, odd_re], lower[:, odd_re], upper[:, odd_im], lower[:, odd_im], pick
+            )
+            sides = []
+            for side in range(2):
+                plus_re, minus_re, plus_im, minus_im = spread(
+                    cos[side], sin[side], cos[2 + side], sin[2 + side], first_lane
+                )
+                rows = slice(at + side * ROWS, at + (side + 1) * ROWS)
+                plus = mask_ref[phase, rows, :half_z]
+                minus = mask_ref[phase, rows, half_z:]
+                sides.append(
+                    folded(
+                        plus_re * plus, minus_re * minus, plus_im * plus, minus_im * minus,
+                        first_lane,
+                    )
+                )
+            cos = folded(sides[0][0], sides[1][0], sides[0][2], sides[1][2], pick)
+            sin = folded(sides[0][1], sides[1][1], sides[0][3], sides[1][3], pick)
+            spectrum[phase, at : at + 2 * ROWS, :] = jnp.concatenate(
+                [
+                    jnp.concatenate([cos[0], sin[0], cos[2], sin[2]], axis=1),
+                    jnp.concatenate([cos[1], sin[1], cos[3], sin[3]], axis=1),
+                ],
+                axis=0,
+            ).astype(BF)
+
+    def returned(phase):
+        value = dot(table_yt[...], spectrum[phase])
+        shape = (length_y // ROWS, ROWS, length_z)
+        value = jnp.stack(
+            [value[:, :length_z].reshape(shape), value[:, length_z:].reshape(shape)], axis=1
         )
-        value = dot(coil_img, table_zt[...])
-        kz = joined(
-            spread(
-                value[:length_y, :half_z],
-                value[:length_y, half_z:],
-                value[length_y:, :half_z],
-                value[length_y:, half_z:],
-                first_lane,
-            ),
-            1,
-        )
-        value = dot(table_y[...], kz)
-        plus_re, minus_re, plus_im, minus_im = spread(
-            value[:half_y, :length_z],
-            value[half_y:, :length_z],
-            value[:half_y, length_z:],
-            value[half_y:, length_z:],
-            first_row,
-        )
-        plus = mask_ref[phase, :half_y]
-        minus = mask_ref[phase, half_y:]
-        even_re, odd_re, even_im, odd_im = folded(
-            plus_re * plus, minus_re * minus, plus_im * plus, minus_im * minus, first_row
-        )
-        spectrum = jnp.concatenate(
-            [joined([even_re, even_im], 1), joined([odd_re, odd_im], 1)], axis=0
-        )
-        value = dot(table_yt[...], spectrum)
-        even_re, odd_re, even_im, odd_im = folded(
-            value[:, :half_z],
-            value[:, half_z:length_z],
-            value[:, length_z : length_z + half_z],
-            value[:, length_z + half_z :],
-            first_lane,
-        )
-        back = dot(
-            jnp.concatenate([joined([even_re, odd_re], 1), joined([even_im, odd_im], 1)], axis=0),
-            table_z[...],
-        )
-        back_re, back_im = back[:length_y], back[length_y:]
-        total[2 * phase] += map_re * back_re + map_im * back_im
-        total[2 * phase + 1] += map_re * back_im - map_im * back_re
+        along_z[phase] = value.reshape(2 * length_y, length_z).astype(BF)
+
+    def summed(index, phase):
+        back = dot(along_z[phase], table_z[...])
+        for at in range(0, length_y, ROWS):
+            rows = slice(at, at + ROWS)
+            map_re = maps_ref[2 * index, rows]
+            map_im = maps_ref[2 * index + 1, rows]
+            back_re = back[2 * at : 2 * at + ROWS]
+            back_im = back[2 * at + ROWS : 2 * at + 2 * ROWS]
+            total[2 * phase, rows] += map_re * back_re + map_im * back_im
+            total[2 * phase + 1, rows] += map_re * back_im - map_im * back_re
+
+    coils = maps_ref.shape[0] // 2
+    for phase in range(phases):
+        multiplied(0, phase)
+    transformed(0)
+    along_z[phases - 1] = jnp.zeros(along_z.shape[1:], BF)
 
     def coil(index, carry):
-        map_re = maps_ref[2 * index].astype(F32)
-        map_im = maps_ref[2 * index + 1].astype(F32)
+        after = jnp.minimum(index + 1, coils - 1)
         for phase in range(phases):
-            item(map_re, map_im, phase)
+            before = index if phase else jnp.maximum(index - 1, 0)
+            transformed((phase + 1) % phases)
+            masked(phase)
+            multiplied(after, phase)
+            returned(phase)
+            summed(before, (phase - 1) % phases)
         return carry
 
-    lax.fori_loop(0, maps_ref.shape[0] // 2, coil, 0)
+    lax.fori_loop(0, coils, coil, 0)
+    summed(coils - 1, phases - 1)
     step = pack_ref[cascade, 2 * width : 2 * width + 1, 1:2]
     for channel in range(channels):
         value = image[channel] - step * total[channel]
@@ -260,7 +305,10 @@
         build_at = 0
     else:
         build_at = jnp.minimum(first_block * ROWS // group, padded // group - builds)
-    lax.fori_loop(build_at, build_at + builds, build, 0)
+    skewed = out_rows == length_y and blocks // UNROLL > 2
+    per_group = UNROLL * ROWS // group
+    early = 2 * per_group + per_group + 1
+    lax.fori_loop(build_at, build_at + (early if skewed else builds), build, 0)
     spare = weight1_ref.shape[2] - (ROWS + 2) * 3 * per_row
     ones_row = lax.broadcasted_iota(jnp.int32, (spare, length_z), 0)
     ones = jnp.where(ones_row < 3, 1.0, 0.0).astype(BF)
@@ -277,7 +325,7 @@
             hidden[pl.ds(store, ROWS * width), :] = jnp.maximum(value, 0.0).astype(BF)
         return carry
 
-    lax.fori_loop(0, blocks // UNROLL, first, 0)
+    lax.fori_loop(0, 2 if skewed else blocks // UNROLL, first, 0)
     block_rows = channels * ROWS
     unroll = min(UNROLL, out_rows // ROWS)
     span = unroll * ROWS
@@ -306,7 +354,19 @@
                     send_refs[plane - 1][channel, rows, :] = value.astype(BF)
         return carry
 
-    lax.fori_loop(0, out_rows // span, second, 0)
+    def both(block, carry):
+        second(block - 2, 0)
+        first(block, 0)
+        for part in range(per_group):
+            at = (block + 1) * per_group + 1 + part
+            build(jnp.minimum(at, padded // group - 1), 0)
+        return carry
+
+    if skewed:
+        lax.fori_loop(2, blocks // UNROLL, both, 0)
+        lax.fori_loop(blocks // UNROLL - 2, blocks // UNROLL, second, 0)
+    else:
+        lax.fori_loop(0, out_rows // span, second, 0)
 
 
 def prepare_kernel(
@@ -368,10 +428,9 @@
         weight2_ref[cascade] = value.astype(BF)
 
 
-def assemble_kernel(members, spaces, place_ref, *refs):
-    local_ref = refs[0]
-    block_refs = refs[1 : 1 + (spaces - 1) * members]
-    out_refs = refs[1 + (spaces - 1) * members :]
+def assemble_kernel(members, spaces, steps, place_ref, local_ref, *refs):
+    block_refs = refs[: len(steps) * members]
+    out_refs = refs[len(steps) * members :]
     rows = local_ref.shape[2]
 
     def put(owner, at, block):
@@ -380,16 +439,16 @@
         for out_ref in out_refs:
             size = out_ref.shape[0] // members
             for index in range(size):
-                out_ref[owner * size + index, where, :] = block[taken + index]
+                out_ref[owner * size + index, where, :] = block[taken + index].astype(out_ref.dtype)
             taken += size
 
     for member in range(members):
         put(member, place_ref[0], local_ref[member])
-    for step in range(1, spaces):
+    for turn, step in enumerate(steps):
         at = lax.rem(place_ref[0] - step + spaces, spaces)
         for offset in range(members):
             owner = lax.rem(place_ref[2] + offset, members)
-            put(owner, at, block_refs[(step - 1) * members + offset])
+            put(owner, at, block_refs[turn * members + offset])
 
 
 def ring(value, axis, step):
@@ -421,7 +480,8 @@
     plane = lax.axis_index("coil")
     section = group * members + member
     table_z = half_tables(length_z)
-    table_y = half_tables(length_y)
+    alternate = np.arange(length_y).reshape(2, -1, ROWS).swapaxes(0, 1).reshape(-1)
+    table_y = half_tables(length_y)[alternate]
     tables = tuple(jnp.asarray(value) for value in (table_z, table_z.T, table_y, table_y.T))
     count = conv1_w.shape[2]
     extra = jnp.concatenate(
@@ -451,45 +511,50 @@
 
     place = jnp.stack([lax.axis_index("space"), plane, member]).astype(jnp.int32)
     spaces = lax.axis_size("space")
-    maps = lax.dynamic_index_in_dim(sens, group, 1, keepdims=False)
-    maps = lax.all_to_all(maps, "coil", split_axis=1, concat_axis=0, tiled=True)[:, 0]
+    slab_sens = lax.dynamic_index_in_dim(sens, group, 1, keepdims=False)
+    own_image = lax.dynamic_index_in_dim(image, group, 1, keepdims=False)[:, 0].astype(BF)
+    own_adjoint = lax.dynamic_index_in_dim(adjoint, group, 1, keepdims=False)[:, 0].astype(BF)
+    if planes == 2:
+        own = lax.dynamic_index_in_dim(slab_sens, plane, 1, keepdims=False)
+        sent = lax.dynamic_index_in_dim(slab_sens, 1 - plane, 1, keepdims=False)
+        maps = jnp.concatenate([own, ring(sent, "coil", 1)], axis=0)
+    else:
+        maps = lax.all_to_all(slab_sens, "coil", split_axis=1, concat_axis=0, tiled=True)[:, 0]
     coils = maps.shape[0]
     maps = maps.reshape(coils, row_count, 2, length_z).transpose(0, 2, 1, 3)
-    own_image = lax.dynamic_index_in_dim(image, group, 1, keepdims=False)[:, 0].astype(BF)
-    own_adjoint = lax.dynamic_index_in_dim(adjoint, group, 1, keepdims=False)[:, 0].astype(BF)
     shared = members if phases % members == 0 and coils % members == 0 else 1
-    local = jnp.concatenate(
-        [
-            part.reshape(shared, -1, row_count, length_z)
-            for part in (own_image, maps, own_adjoint)
-        ],
-        axis=1,
-    )
-    mine = lax.dynamic_index_in_dim(local, member % shared, 0, keepdims=False)
-    blocks = []
-    for step in range(1, spaces):
-        block = ring(mine, "space", step)
-        blocks.append(block)
-        for offset in range(1, shared):
-            blocks.append(ring(block, "member", -offset))
+    steps = sorted(range(1, spaces), key=lambda step: min(step, spaces - step))
+
+    def joined_rows(parts, dtypes):
+        local = jnp.concatenate(
+            [part.reshape(shared, -1, row_count, length_z) for part in parts], axis=1
+        )
+        mine = lax.dynamic_index_in_dim(local, member % shared, 0, keepdims=False)
+        blocks = []
+        for step in steps:
+            block = ring(mine, "space", step)
+            blocks.append(block)
+            for offset in range(1, shared):
+                blocks.append(ring(block, "member", -offset))
+        return pl.pallas_call(
+            functools.partial(assemble_kernel, shared, spaces, steps),
+            out_shape=tuple(
+                jax.ShapeDtypeStruct((part.shape[0], length_y, length_z), dtype)
+                for part, dtype in zip(parts, dtypes)
+            ),
+            in_specs=[smem] + [vmem] * (1 + len(blocks)),
+            out_specs=(vmem,) * len(parts),
+            compiler_params=params,
+        )(place, local, *blocks)
 
     full = jax.ShapeDtypeStruct((channels, length_y, length_z), F32)
     half = jax.ShapeDtypeStruct((channels, length_y, length_z), BF)
     vmem = pl.BlockSpec(memory_space=pltpu.VMEM)
     smem = pl.BlockSpec(memory_space=pltpu.SMEM)
     params = pltpu.CompilerParams(vmem_limit_bytes=32 * 1024 * 1024)
-    base, maps, target = pl.pallas_call(
-        functools.partial(assemble_kernel, shared, spaces),
-        out_shape=(
-            half,
-            jax.ShapeDtypeStruct((2 * coils, length_y, length_z), BF),
-            half,
-        ),
-        in_specs=[smem] + [vmem] * (1 + len(blocks)),
-        out_specs=(vmem,) * 3,
-        compiler_params=params,
-    )(place, local, *blocks)
-    order = np.eye(length_y)[slot_order(length_y)].astype(BF)
+    base, target = joined_rows([own_image, own_adjoint], [BF, BF])
+    (maps,) = joined_rows([maps.reshape(2 * coils, row_count, length_z)], [F32])
+    order = np.eye(length_y)[slot_order(length_y)[alternate]].astype(BF)
     column = slot_order(length_z)
     columns = np.stack([column // 30, column % 30]).astype(np.int32)
     weight1, weight2, sampled = pl.pallas_call(
@@ -512,7 +577,9 @@
             out_shape=(rows_shape, full, half),
             in_specs=[smem] + [vmem] * (9 + len(parts)),
             out_specs=(vmem, vmem, vmem),
-            scratch_shapes=[pltpu.VMEM((channels, length_y, length_z), F32)] * 2,
+            scratch_shapes=[pltpu.VMEM((channels, length_y, length_z), F32)] * 3
+            + [pltpu.VMEM((phases, length_y, 2 * length_z), dtype) for dtype in (BF, F32, BF)]
+            + [pltpu.VMEM((phases, 2 * length_y, length_z), BF)],
             compiler_params=params,
         )(place, base, *parts, maps, target, sampled, packed, *tables)
 

time: 130 us -> 110 us (0.85); the launches traced: 128 us -> 110 us
  Pallas kernels: 63.6 us -> 49.7 us
  waiting for transfers between devices: 35.9 us -> 30.1 us
  starting transfers between devices: 20.1 us -> 22.7 us
  local copies, waits for them, and re-layouts: 5.91 us -> 4.28 us
    pallas_call x4, Pallas kernels: 29.3 us -> 21.4 us  [consistency(): pl.pallas_call(functools.partial(consistency_kernel, phases, width, casca...]
    ppermute x8 -> x15, starting transfers between devices: 13.7 us -> 20.7 us  [ring(): lax.ppermute(value, axis, [(i, (i + step) % count) for i in range(count)])]
    pallas_call x4, Pallas kernels: 31.2 us -> 24.7 us  [refine(): pl.pallas_call(functools.partial(refine_kernel, neighbours, width, cascad...]
    ppermute x8 -> x15, waiting for transfers between devices: 16.7 us -> 11.4 us  [ring(): lax.ppermute(value, axis, [(i, (i + step) % count) for i in range(count)])]
    all_to_all x1 -> x0, starting transfers between devices: 3.44 us -> none  [per_device(): lax.all_to_all(maps, 'coil', split_axis=1, concat_axis=0, tiled=True)[:, 0]]
    unnamed x27 -> x23, local copies, waits for them, and re-layouts: 3.71 us -> 1.84 us
    all_to_all x1 -> x0, waiting for transfers between devices: 1.53 us -> none  [per_device(): lax.all_to_all(maps, 'coil', split_axis=1, concat_axis=0, tiled=True)[:, 0]]
  transfers between devices with their start and end apart: 18 -> 24, of which waited for: 14 -> 13; matrix products, arithmetic and copies ran while one was open for 1% -> 4% of each run, Pallas kernels for 2% -> 3%
where the time goes in v4:
time: 110 us
  Pallas kernels  49.7 us (45%)
  waiting for transfers between devices  30.1 us (27%)
  starting transfers between devices  22.7 us (21%)
  local copies, waits for them, and re-layouts  4.28 us (4%)
  other arithmetic  2.23 us (2%)
  between operations  1.13 us (1%)
    pallas_call x4, Pallas kernels, refine(): pl.pallas_call(functools.partial(refine_kernel, neighbours, width, cascad...  24.7 us
    pallas_call x4, Pallas kernels, consistency(): pl.pallas_call(functools.partial(consistency_kernel, phases, width, casca...  21.4 us
    ppermute x15, starting transfers between devices, ring(): lax.ppermute(value, axis, [(i, (i + step) % count) for i in range(count)])  20.7 us
    ppermute x8, waiting for transfers between devices, exchanged(): received.append(lax.ppermute(value, 'coil', pairs))  13.8 us
    ppermute x15, waiting for transfers between devices, ring(): lax.ppermute(value, axis, [(i, (i + step) % count) for i in range(count)])  11.4 us
    ppermute x1, waiting for transfers between devices, per_device(): lax.ppermute(chosen, 'group', [(i, (i - step) % groups) for i in range(gr...  4.9 us
    pallas_call x1, Pallas kernels, per_device(): pl.pallas_call(functools.partial(prepare_kernel, width, per_row), out_sha...  2.39 us
  transfers between devices with their start and end apart: 24, of which 13 were waited for; matrix products, arithmetic and copies ran while one was open for 4% of the time, Pallas kernels for 3%

profile of v4, /device:TPU:0, one launch (start us, length us, event | category | flops | bytes accessed | tf_op | source)
XLA Modules:
  0.0 110.2 jit_solution(10082541628610783701)
XLA Ops:
  0.0 1.1 dynamic-slice_convert_fusion
  1.1 3.1 %collective-permute-start = (bf16[4,64,256]{2,1,0:T(8,128)(2,1)S(1)}, bf16[4,64,256]{2,1,0:T(8,128)(2,1)S(1)}, u32[]{:S(2)}, u32[]{:S(2)}) collective-permute-start(bf16[4,64,256]{2,1,0:T(8,128)(2,1)S(1)} %fusion.1), channel_id=1, source_target_pairs={{0,1},{1,2},{2,3},{3,0},{4,5},{5,6},{6,7},{7,4},{8,9},{9,10},{10,1... | collective-permute-start | bytes 393224 | tf_op jit(solution)/shard_map/ppermute | solution.py:456
  4.2 2.1 %collective-permute-start.2 = (bf16[4,64,256]{2,1,0:T(8,128)(2,1)S(1)}, bf16[4,64,256]{2,1,0:T(8,128)(2,1)S(1)}, u32[]{:S(2)}, u32[]{:S(2)}) collective-permute-start(bf16[4,64,256]{2,1,0:T(8,128)(2,1)S(1)} %fusion.1), channel_id=1, source_target_pairs={{0,3},{1,0},{2,1},{3,2},{4,7},{5,4},{6,5},{7,6},{8,11},{9,8},{10,9... | collective-permute-start | bytes 393224 | tf_op jit(solution)/shard_map/ppermute | solution.py:456
  6.3 0.9 collective-permute-start.4
  7.3 1.0 constant_dynamic-slice_fusion
  8.2 0.1 collective-permute-start.6
  8.3 0.8 copy.25
  9.1 0.8 copy.26
  10.6 0.7 pad_select_fusion
  11.3 0.1 pad_maximum_fusion.1
  11.4 0.0 copy-start.4
  11.5 1.6 %collective-permute-start.13 = (f32[96,128]{0,1:T(8,128)S(1)}, f32[96,128]{0,1:T(8,128)S(1)}, u32[]{:S(2)}, u32[]{:S(2)}) collective-permute-start(f32[96,128]{0,1:T(8,128)S(1)} %pad_maximum_fusion.1), channel_id=1, source_target_pairs={{0,8},{8,0},{1,9},{9,1},{2,10},{10,2},{3,11},{11,3},{4,12},{12,4},... | collective-permute-start | bytes 147464 | tf_op jit(solution)/shard_map/ppermute | solution.py:456
  13.0 0.1 fusion.2
  13.2 0.1 copy.27
  13.3 0.1 pad_add_fusion.place_ref
  13.4 0.1 copy.29.bits_ref
  13.6 2.4 %collective-permute-done.13 = f32[96,128]{0,1:T(8,128)S(1)} collective-permute-done((f32[96,128]{0,1:T(8,128)S(1)}, f32[96,128]{0,1:T(8,128)S(1)}, u32[]{:S(2)}, u32[]{:S(2)}) %collective-permute-start.13) | collective-permute-done | bytes 49184 | tf_op jit(solution)/shard_map/ppermute | solution.py:456
  16.0 0.1 copy.28
  16.1 1.6 %collective-permute-start.14 = (f32[2,96,128]{2,1,0:T(8,128)S(1)}, f32[2,96,128]{2,1,0:T(8,128)S(1)}, u32[]{:S(2)}, u32[]{:S(2)}) collective-permute-start(f32[2,96,128]{2,1,0:T(8,128)S(1)} %constant_dynamic-update-slice_fusion), channel_id=1, source_target_pairs={{0,16},{16,0},{1,17},{17,1},{2,18},{18,2},{3,19},{19,3},{4,20},{20... | collective-permute-start | bytes 294920 | tf_op jit(solution)/shard_map/ppermute | solution.py:456
  17.7 0.3 maximum_bitcast_fusion
  18.2 1.4 %collective-permute-start.9 = (bf16[4,64,256]{2,1,0:T(8,128)(2,1)S(1)}, bf16[4,64,256]{2,1,0:T(8,128)(2,1)S(1)}, u32[]{:S(2)}, u32[]{:S(2)}) collective-permute-start(bf16[4,64,256]{2,1,0:T(8,128)(2,1)S(1)} %dynamic-slice_bitcast_fusion), channel_id=1, source_target_pairs={{0,3},{1,0},{2,1},{3,2},{4,7},{5,4},{6,5},{7,6},{8,11},{9,8},{10,9... | collective-permute-start | bytes 393224 | tf_op jit(solution)/shard_map/ppermute | solution.py:456
  19.6 1.7 %collective-permute-start.11 = (bf16[4,64,256]{2,1,0:T(8,128)(2,1)S(1)}, bf16[4,64,256]{2,1,0:T(8,128)(2,1)S(1)}, u32[]{:S(2)}, u32[]{:S(2)}) collective-permute-start(bf16[4,64,256]{2,1,0:T(8,128)(2,1)S(1)} %dynamic-slice_bitcast_fusion), channel_id=1, source_target_pairs={{0,2},{1,3},{2,0},{3,1},{4,6},{5,7},{6,4},{7,5},{8,10},{9,11},{10,... | collective-permute-start | bytes 393224 | tf_op jit(solution)/shard_map/ppermute | solution.py:456
  21.3 1.1 %collective-permute-start.7 = (bf16[4,64,256]{2,1,0:T(8,128)(2,1)S(1)}, bf16[4,64,256]{2,1,0:T(8,128)(2,1)S(1)}, u32[]{:S(2)}, u32[]{:S(2)}) collective-permute-start(bf16[4,64,256]{2,1,0:T(8,128)(2,1)S(1)} %dynamic-slice_bitcast_fusion), channel_id=1, source_target_pairs={{0,1},{1,2},{2,3},{3,0},{4,5},{5,6},{6,7},{7,4},{8,9},{9,10},{10,1... | collective-permute-start | bytes 393224 | tf_op jit(solution)/shard_map/ppermute | solution.py:456
  22.4 1.5 %collective-permute-start.1 = (bf16[4,64,256]{2,1,0:T(8,128)(2,1)S(1)}, bf16[4,64,256]{2,1,0:T(8,128)(2,1)S(1)}, u32[]{:S(2)}, u32[]{:S(2)}) collective-permute-start(bf16[4,64,256]{2,1,0:T(8,128)(2,1)S(1)} %collective-permute-done.refs_0_), channel_id=1, source_target_pairs={{0,8},{8,0},{1,9},{9,1},{2,10},{10,2},{3,11},{11,3},{4,12},{12,4},... | collective-permute-start | bytes 393224 | tf_op jit(solution)/shard_map/ppermute | solution.py:456
  23.9 0.6 collective-permute-start.3
  24.5 1.5 %collective-permute-start.5 = (bf16[4,64,256]{2,1,0:T(8,128)(2,1)S(1)}, bf16[4,64,256]{2,1,0:T(8,128)(2,1)S(1)}, u32[]{:S(2)}, u32[]{:S(2)}) collective-permute-start(bf16[4,64,256]{2,1,0:T(8,128)(2,1)S(1)} %collective-permute-done.4.refs_4_), channel_id=1, source_target_pairs={{0,8},{8,0},{1,9},{9,1},{2,10},{10,2},{3,11},{11,3},{4,12},{12,4},... | collective-permute-start | bytes 393224 | tf_op jit(solution)/shard_map/ppermute | solution.py:456
  26.0 6.4 %collective-permute-done.11.refs_4_ = bf16[4,64,256]{2,1,0:T(8,128)(2,1)S(1)} collective-permute-done((bf16[4,64,256]{2,1,0:T(8,128)(2,1)S(1)}, bf16[4,64,256]{2,1,0:T(8,128)(2,1)S(1)}, u32[]{:S(2)}, u32[]{:S(2)}) %collective-permute-start.11) | collective-permute-done | bytes 131104 | tf_op jit(solution)/shard_map/ppermute | solution.py:456
  32.4 1.5 %collective-permute-start.10 = (bf16[4,64,256]{2,1,0:T(8,128)(2,1)S(1)}, bf16[4,64,256]{2,1,0:T(8,128)(2,1)S(1)}, u32[]{:S(2)}, u32[]{:S(2)}) collective-permute-start(bf16[4,64,256]{2,1,0:T(8,128)(2,1)S(1)} %collective-permute-done.9.refs_2_), channel_id=1, source_target_pairs={{0,8},{8,0},{1,9},{9,1},{2,10},{10,2},{3,11},{11,3},{4,12},{12,4},... | collective-permute-start | bytes 393224 | tf_op jit(solution)/shard_map/ppermute | solution.py:456
  33.9 0.5 collective-permute-start.12
  34.4 1.5 %collective-permute-start.8 = (bf16[4,64,256]{2,1,0:T(8,128)(2,1)S(1)}, bf16[4,64,256]{2,1,0:T(8,128)(2,1)S(1)}, u32[]{:S(2)}, u32[]{:S(2)}) collective-permute-start(bf16[4,64,256]{2,1,0:T(8,128)(2,1)S(1)} %collective-permute-done.7.refs_0_), channel_id=1, source_target_pairs={{0,8},{8,0},{1,9},{9,1},{2,10},{10,2},{3,11},{11,3},{4,12},{12,4},... | collective-permute-start | bytes 393224 | tf_op jit(solution)/shard_map/ppermute | solution.py:456
  36.0 2.4 %shard_map.156 = (bf16[4,256,256]{2,1,0:T(8,128)(2,1)S(1)}, bf16[4,192,320]{2,1,0:T(8,128)(2,1)S(1)}, f32[2,256,256]{2,1,0:T(8,128)S(1)}) custom-call(s32[3]{0:T(128)S(1)} %pad_add_fusion.place_ref, f32[4,96,128]{2,1,0:T(8,128)S(1)} %bitcast.39, s32[2,256,9]{2,1,0:T(8,128)S(1)} %copy.29.bits_ref, s32[2,256]{1,0:T(2,128)S(1)} %copy-done.7, ...), custom_call_target="tpu_custom_call" | custom-call | tf_op jit(solution)/shard_map/pallas_call | solution.py:560
  38.5 0.6 shard_map.154
  39.1 1.1 %collective-permute-done.12.refs_5_ = bf16[4,64,256]{2,1,0:T(8,128)(2,1)S(1)} collective-permute-done((bf16[4,64,256]{2,1,0:T(8,128)(2,1)S(1)}, bf16[4,64,256]{2,1,0:T(8,128)(2,1)S(1)}, u32[]{:S(2)}, u32[]{:S(2)}) %collective-permute-start.12) | collective-permute-done | bytes 131104 | tf_op jit(solution)/shard_map/ppermute | solution.py:456
  40.2 1.4 %collective-permute-done.8.refs_1_ = bf16[4,64,256]{2,1,0:T(8,128)(2,1)S(1)} collective-permute-done((bf16[4,64,256]{2,1,0:T(8,128)(2,1)S(1)}, bf16[4,64,256]{2,1,0:T(8,128)(2,1)S(1)}, u32[]{:S(2)}, u32[]{:S(2)}) %collective-permute-start.8) | collective-permute-done | bytes 131104 | tf_op jit(solution)/shard_map/ppermute | solution.py:456
  41.6 0.7 shard_map.155.refs_0_.refs_1_
  42.4 5.5 %shard_map.157 = (f32[4,64,256]{2,1,0:T(8,128)}, f32[4,256,256]{2,1,0:T(8,128)S(1)}, bf16[4,256,256]{2,1,0:T(8,128)(2,1)S(1)}) custom-call(s32[3]{0:T(128)S(1)} %pad_add_fusion.place_ref, bf16[4,256,256]{2,1,0:T(8,128)(2,1)S(1)} %get-tuple-element.29.base_ref, f32[8,256,256]{2,1,0:T(8,128)S(1)} %shard_map.155.refs_0_.refs_1_, ...), custom_call_target="tpu_custom_call" | custom-call | tf_op jit(solution)/shard_map/pallas_call | solution.py:575
  47.8 0.1 collective-permute-start.15
  47.9 1.9 %collective-permute-done.15.refs_0_ = bf16[4,256,256]{2,1,0:T(8,128)(2,1)S(1)} collective-permute-done((bf16[4,256,256]{2,1,0:T(8,128)(2,1)S(1)}, bf16[4,256,256]{2,1,0:T(8,128)(2,1)S(1)}, u32[]{:S(2)}, u32[]{:S(2)}) %collective-permute-start.15) | collective-permute-done | bytes 524320 | tf_op jit(solution)/shard_map/ppermute | solution.py:611
  49.8 6.9 %shard_map.158 = (f32[4,256,256]{2,1,0:T(8,128)S(1)}, bf16[4,256,256]{2,1,0:T(8,128)(2,1)S(1)}) custom-call(s32[3]{0:T(128)S(1)} %pad_add_fusion.place_ref, bf16[4,256,256]{2,1,0:T(8,128)(2,1)S(1)} %get-tuple-element.32.v_ref, bf16[4,256,256]{2,1,0:T(8,128)(2,1)S(1)} %collective-permute-done.15.refs_0_, f32[4,256,256]{2,1,0:T(8,128)S(1)} %get-tuple-element.33.refs_1_, ...), custom_call_target="tpu_custom_call" | custom-call | tf_op jit(solution)/shard_map/pallas_call | solution.py:590
  56.8 0.2 collective-permute-start.16
  56.9 1.8 %collective-permute-done.16.refs_0_ = bf16[4,256,256]{2,1,0:T(8,128)(2,1)S(1)} collective-permute-done((bf16[4,256,256]{2,1,0:T(8,128)(2,1)S(1)}, bf16[4,256,256]{2,1,0:T(8,128)(2,1)S(1)}, u32[]{:S(2)}, u32[]{:S(2)}) %collective-permute-start.16) | collective-permute-done | bytes 524320 | tf_op jit(solution)/shard_map/ppermute | solution.py:611
  58.7 5.3 %shard_map.159 = (f32[4,64,256]{2,1,0:T(8,128)S(1)}, f32[4,256,256]{2,1,0:T(8,128)S(1)}, bf16[4,256,256]{2,1,0:T(8,128)(2,1)S(1)}) custom-call(s32[3]{0:T(128)S(1)} %pad_add_fusion.place_ref, f32[4,256,256]{2,1,0:T(8,128)S(1)} %get-tuple-element.36.base_ref, bf16[4,256,256]{2,1,0:T(8,128)(2,1)S(1)} %collective-permute-done.16.refs_0_, ...), custom_call_target="tpu_custom_call" | custom-call | tf_op jit(solution)/shard_map/pallas_call | solution.py:575
  64.1 0.2 collective-permute-start.17
  64.3 1.8 %collective-permute-done.17.refs_0_ = bf16[4,256,256]{2,1,0:T(8,128)(2,1)S(1)} collective-permute-done((bf16[4,256,256]{2,1,0:T(8,128)(2,1)S(1)}, bf16[4,256,256]{2,1,0:T(8,128)(2,1)S(1)}, u32[]{:S(2)}, u32[]{:S(2)}) %collective-permute-start.17) | collective-permute-done | bytes 524320 | tf_op jit(solution)/shard_map/ppermute | solution.py:611
  66.0 6.9 %shard_map.160 = (f32[4,256,256]{2,1,0:T(8,128)S(1)}, bf16[4,256,256]{2,1,0:T(8,128)(2,1)S(1)}) custom-call(s32[3]{0:T(128)S(1)} %pad_add_fusion.place_ref, bf16[4,256,256]{2,1,0:T(8,128)(2,1)S(1)} %get-tuple-element.38.v_ref, bf16[4,256,256]{2,1,0:T(8,128)(2,1)S(1)} %collective-permute-done.17.refs_0_, f32[4,256,256]{2,1,0:T(8,128)S(1)} %get-tuple-element.39.refs_1_, ...), custom_call_target="tpu_custom_call" | custom-call | tf_op jit(solution)/shard_map/pallas_call | solution.py:590
  73.0 0.2 collective-permute-start.18
  73.2 1.8 %collective-permute-done.18.refs_0_ = bf16[4,256,256]{2,1,0:T(8,128)(2,1)S(1)} collective-permute-done((bf16[4,256,256]{2,1,0:T(8,128)(2,1)S(1)}, bf16[4,256,256]{2,1,0:T(8,128)(2,1)S(1)}, u32[]{:S(2)}, u32[]{:S(2)}) %collective-permute-start.18) | collective-permute-done | bytes 524320 | tf_op jit(solution)/shard_map/ppermute | solution.py:611
  75.0 5.3 %shard_map.161 = (f32[4,64,256]{2,1,0:T(8,128)S(1)}, f32[4,256,256]{2,1,0:T(8,128)S(1)}, bf16[4,256,256]{2,1,0:T(8,128)(2,1)S(1)}) custom-call(s32[3]{0:T(128)S(1)} %pad_add_fusion.place_ref, f32[4,256,256]{2,1,0:T(8,128)S(1)} %get-tuple-element.40.base_ref, bf16[4,256,256]{2,1,0:T(8,128)(2,1)S(1)} %collective-permute-done.18.refs_0_, ...), custom_call_target="tpu_custom_call" | custom-call | tf_op jit(solution)/shard_map/pallas_call | solution.py:575
  80.3 0.2 collective-permute-start.19
  80.5 1.8 %collective-permute-done.19.refs_0_ = bf16[4,256,256]{2,1,0:T(8,128)(2,1)S(1)} collective-permute-done((bf16[4,256,256]{2,1,0:T(8,128)(2,1)S(1)}, bf16[4,256,256]{2,1,0:T(8,128)(2,1)S(1)}, u32[]{:S(2)}, u32[]{:S(2)}) %collective-permute-start.19) | collective-permute-done | bytes 524320 | tf_op jit(solution)/shard_map/ppermute | solution.py:611
  82.3 6.9 %shard_map.162 = (f32[4,256,256]{2,1,0:T(8,128)S(1)}, bf16[4,256,256]{2,1,0:T(8,128)(2,1)S(1)}) custom-call(s32[3]{0:T(128)S(1)} %pad_add_fusion.place_ref, bf16[4,256,256]{2,1,0:T(8,128)(2,1)S(1)} %get-tuple-element.42.v_ref, bf16[4,256,256]{2,1,0:T(8,128)(2,1)S(1)} %collective-permute-done.19.refs_0_, f32[4,256,256]{2,1,0:T(8,128)S(1)} %get-tuple-element.43.refs_1_, ...), custom_call_target="tpu_custom_call" | custom-call | tf_op jit(solution)/shard_map/pallas_call | solution.py:590
  89.2 0.2 collective-permute-start.20
  89.4 1.8 %collective-permute-done.20.refs_0_ = bf16[4,256,256]{2,1,0:T(8,128)(2,1)S(1)} collective-permute-done((bf16[4,256,256]{2,1,0:T(8,128)(2,1)S(1)}, bf16[4,256,256]{2,1,0:T(8,128)(2,1)S(1)}, u32[]{:S(2)}, u32[]{:S(2)}) %collective-permute-start.20) | collective-permute-done | bytes 524320 | tf_op jit(solution)/shard_map/ppermute | solution.py:611
  91.2 5.3 %shard_map.163 = (f32[4,64,256]{2,1,0:T(8,128)S(1)}, f32[4,256,256]{2,1,0:T(8,128)S(1)}, bf16[4,256,256]{2,1,0:T(8,128)(2,1)S(1)}) custom-call(s32[3]{0:T(128)S(1)} %pad_add_fusion.place_ref, f32[4,256,256]{2,1,0:T(8,128)S(1)} %get-tuple-element.44.base_ref, bf16[4,256,256]{2,1,0:T(8,128)(2,1)S(1)} %collective-permute-done.20.refs_0_, ...), custom_call_target="tpu_custom_call" | custom-call | tf_op jit(solution)/shard_map/pallas_call | solution.py:575
  96.5 0.2 collective-permute-start.21
  96.7 1.8 %collective-permute-done.21.refs_0_ = bf16[4,256,256]{2,1,0:T(8,128)(2,1)S(1)} collective-permute-done((bf16[4,256,256]{2,1,0:T(8,128)(2,1)S(1)}, bf16[4,256,256]{2,1,0:T(8,128)(2,1)S(1)}, u32[]{:S(2)}, u32[]{:S(2)}) %collective-permute-start.21) | collective-permute-done | bytes 524320 | tf_op jit(solution)/shard_map/ppermute | solution.py:611
  98.5 3.8 %shard_map.164 = (f32[4,64,256]{2,1,0:T(8,128)S(1)}, bf16[4,64,256]{2,1,0:T(8,128)(2,1)S(1)}) custom-call(s32[3]{0:T(128)S(1)} %pad_add_fusion.place_ref, bf16[4,256,256]{2,1,0:T(8,128)(2,1)S(1)} %get-tuple-element.46.v_ref, bf16[4,256,256]{2,1,0:T(8,128)(2,1)S(1)} %collective-permute-done.21.refs_0_, f32[4,256,256]{2,1,0:T(8,128)S(1)} %get-tuple-element.47.refs_1_, ...), custom_call_target="tpu_custom_call" | custom-call | tf_op jit(solution)/shard_map/pallas_call | solution.py:590
  102.3 0.2 collective-permute-start.22
  102.5 1.2 %collective-permute-done.22 = bf16[4,64,256]{2,1,0:T(8,128)(2,1)S(1)} collective-permute-done((bf16[4,64,256]{2,1,0:T(8,128)(2,1)S(1)}, bf16[4,64,256]{2,1,0:T(8,128)(2,1)S(1)}, u32[]{:S(2)}, u32[]{:S(2)}) %collective-permute-start.22) | collective-permute-done | bytes 131104 | tf_op jit(solution)/shard_map/ppermute | solution.py:611
  103.7 0.1 select_convert_fusion
  103.8 0.6 collective-permute-start.23
  104.4 0.1 bitcast_dynamic-update-slice_fusion
  104.5 4.9 %collective-permute-done.23 = bf16[4,64,256]{2,1,0:T(8,128)(2,1)S(1)} collective-permute-done((bf16[4,64,256]{2,1,0:T(8,128)(2,1)S(1)}, bf16[4,64,256]{2,1,0:T(8,128)(2,1)S(1)}, u32[]{:S(2)}, u32[]{:S(2)}) %collective-permute-start.23) | collective-permute-done | bytes 131104 | tf_op jit(solution)/shard_map/ppermute | solution.py:649
  109.4 0.7 convert_dynamic-update-slice_fusion
  (44 shorter events, 0.4 us)
Async XLA Ops:
  0.0 13.4 %copy-start.9 = (s32[2,256,9]{1,0,2:T(2,128)S(1)}, s32[2,256,9]{1,0,2:T(2,128)}, u32[]{:S(2)}) copy-start(s32[2,256,9]{1,0,2:T(2,128)} %param.19) | copy-start | bytes 55300
  1.1 18.5 %collective-permute-start = (bf16[4,64,256]{2,1,0:T(8,128)(2,1)S(1)}, bf16[4,64,256]{2,1,0:T(8,128)(2,1)S(1)}, u32[]{:S(2)}, u32[]{:S(2)}) collective-permute-start(bf16[4,64,256]{2,1,0:T(8,128)(2,1)S(1)} %fusion.1), channel_id=1, source_target_pairs={{0,1},{1,2},{2,3},{3,0},{4,5},{5,6},{6,7},{7,4},{8,9},{9,10},{10,1... | collective-permute-start | bytes 393224 | tf_op jit(solution)/shard_map/ppermute | solution.py:456
  4.2 17.0 %collective-permute-start.2 = (bf16[4,64,256]{2,1,0:T(8,128)(2,1)S(1)}, bf16[4,64,256]{2,1,0:T(8,128)(2,1)S(1)}, u32[]{:S(2)}, u32[]{:S(2)}) collective-permute-start(bf16[4,64,256]{2,1,0:T(8,128)(2,1)S(1)} %fusion.1), channel_id=1, source_target_pairs={{0,3},{1,0},{2,1},{3,2},{4,7},{5,4},{6,5},{7,6},{8,11},{9,8},{10,9... | collective-permute-start | bytes 393224 | tf_op jit(solution)/shard_map/ppermute | solution.py:456
  6.3 16.1 %collective-permute-start.4 = (bf16[4,64,256]{2,1,0:T(8,128)(2,1)S(1)}, bf16[4,64,256]{2,1,0:T(8,128)(2,1)S(1)}, u32[]{:S(2)}, u32[]{:S(2)}) collective-permute-start(bf16[4,64,256]{2,1,0:T(8,128)(2,1)S(1)} %fusion.1), channel_id=1, source_target_pairs={{0,2},{1,3},{2,0},{3,1},{4,6},{5,7},{6,4},{7,5},{8,10},{9,11},{10,... | collective-permute-start | bytes 393224 | tf_op jit(solution)/shard_map/ppermute | solution.py:456
  8.2 9.5 %collective-permute-start.6 = (bf16[2,64,512]{2,1,0:T(8,128)(2,1)S(1)}, bf16[2,64,512]{2,1,0:T(8,128)(2,1)S(1)}, u32[]{:S(2)}, u32[]{:S(2)}) collective-permute-start(bf16[2,64,512]{2,1,0:T(8,128)(2,1)S(1)} %get-tuple-element.54), channel_id=1, source_target_pairs={{0,4},{4,0},{1,5},{5,1},{2,6},{6,2},{3,7},{7,3},{8,12},{12,8},{9,1... | collective-permute-start | bytes 393224 | tf_op jit(solution)/shard_map/ppermute | solution.py:456
  11.4 24.5 %copy-start.4 = (bf16[2,3,192,108]{3,2,1,0:T(8,128)(2,1)S(1)}, bf16[2,3,192,108]{3,2,1,0:T(8,128)(2,1)}, u32[]{:S(2)}) copy-start(bf16[2,3,192,108]{3,2,1,0:T(8,128)(2,1)} %constant.173.clone.select2_ref) | copy-start | bytes 746500
  11.4 24.5 %copy-start.5 = (bf16[256,256]{1,0:T(8,128)(2,1)S(1)}, bf16[256,256]{1,0:T(8,128)(2,1)}, u32[]{:S(2)}) copy-start(bf16[256,256]{1,0:T(8,128)(2,1)} %constant.175.clone.order_ref) | copy-start | bytes 393220
  11.4 24.5 %copy-start.6 = (bf16[2,108,256]{2,1,0:T(8,128)(2,1)S(1)}, bf16[2,108,256]{2,1,0:T(8,128)(2,1)}, u32[]{:S(2)}) copy-start(bf16[2,108,256]{2,1,0:T(8,128)(2,1)} %constant.172.clone.select1_ref) | copy-start | bytes 331780
  11.4 24.5 %copy-start.7 = (s32[2,256]{1,0:T(2,128)S(1)}, s32[2,256]{1,0:T(2,128)}, u32[]{:S(2)}) copy-start(s32[2,256]{1,0:T(2,128)} %constant.174.clone.columns_ref) | copy-start | bytes 6148
  11.5 4.6 %collective-permute-start.13 = (f32[96,128]{0,1:T(8,128)S(1)}, f32[96,128]{0,1:T(8,128)S(1)}, u32[]{:S(2)}, u32[]{:S(2)}) collective-permute-start(f32[96,128]{0,1:T(8,128)S(1)} %pad_maximum_fusion.1), channel_id=1, source_target_pairs={{0,8},{8,0},{1,9},{9,1},{2,10},{10,2},{3,11},{11,3},{4,12},{12,4},... | collective-permute-start | bytes 147464 | tf_op jit(solution)/shard_map/ppermute | solution.py:456
  16.1 7.8 %collective-permute-start.14 = (f32[2,96,128]{2,1,0:T(8,128)S(1)}, f32[2,96,128]{2,1,0:T(8,128)S(1)}, u32[]{:S(2)}, u32[]{:S(2)}) collective-permute-start(f32[2,96,128]{2,1,0:T(8,128)S(1)} %constant_dynamic-update-slice_fusion), channel_id=1, source_target_pairs={{0,16},{16,0},{1,17},{17,1},{2,18},{18,2},{3,19},{19,3},{4,20},{20... | collective-permute-start | bytes 294920 | tf_op jit(solution)/shard_map/ppermute | solution.py:456
  18.2 6.4 %collective-permute-start.9 = (bf16[4,64,256]{2,1,0:T(8,128)(2,1)S(1)}, bf16[4,64,256]{2,1,0:T(8,128)(2,1)S(1)}, u32[]{:S(2)}, u32[]{:S(2)}) collective-permute-start(bf16[4,64,256]{2,1,0:T(8,128)(2,1)S(1)} %dynamic-slice_bitcast_fusion), channel_id=1, source_target_pairs={{0,3},{1,0},{2,1},{3,2},{4,7},{5,4},{6,5},{7,6},{8,11},{9,8},{10,9... | collective-permute-start | bytes 393224 | tf_op jit(solution)/shard_map/ppermute | solution.py:456
  19.6 12.8 %collective-permute-start.11 = (bf16[4,64,256]{2,1,0:T(8,128)(2,1)S(1)}, bf16[4,64,256]{2,1,0:T(8,128)(2,1)S(1)}, u32[]{:S(2)}, u32[]{:S(2)}) collective-permute-start(bf16[4,64,256]{2,1,0:T(8,128)(2,1)S(1)} %dynamic-slice_bitcast_fusion), channel_id=1, source_target_pairs={{0,2},{1,3},{2,0},{3,1},{4,6},{5,7},{6,4},{7,5},{8,10},{9,11},{10,... | collective-permute-start | bytes 393224 | tf_op jit(solution)/shard_map/ppermute | solution.py:456
  21.3 12.6 %collective-permute-start.7 = (bf16[4,64,256]{2,1,0:T(8,128)(2,1)S(1)}, bf16[4,64,256]{2,1,0:T(8,128)(2,1)S(1)}, u32[]{:S(2)}, u32[]{:S(2)}) collective-permute-start(bf16[4,64,256]{2,1,0:T(8,128)(2,1)S(1)} %dynamic-slice_bitcast_fusion), channel_id=1, source_target_pairs={{0,1},{1,2},{2,3},{3,0},{4,5},{5,6},{6,7},{7,4},{8,9},{9,10},{10,1... | collective-permute-start | bytes 393224 | tf_op jit(solution)/shard_map/ppermute | solution.py:456
  22.4 12.1 %collective-permute-start.1 = (bf16[4,64,256]{2,1,0:T(8,128)(2,1)S(1)}, bf16[4,64,256]{2,1,0:T(8,128)(2,1)S(1)}, u32[]{:S(2)}, u32[]{:S(2)}) collective-permute-start(bf16[4,64,256]{2,1,0:T(8,128)(2,1)S(1)} %collective-permute-done.refs_0_), channel_id=1, source_target_pairs={{0,8},{8,0},{1,9},{9,1},{2,10},{10,2},{3,11},{11,3},{4,12},{12,4},... | collective-permute-start | bytes 393224 | tf_op jit(solution)/shard_map/ppermute | solution.py:456
  23.9 14.5 %collective-permute-start.3 = (bf16[4,64,256]{2,1,0:T(8,128)(2,1)S(1)}, bf16[4,64,256]{2,1,0:T(8,128)(2,1)S(1)}, u32[]{:S(2)}, u32[]{:S(2)}) collective-permute-start(bf16[4,64,256]{2,1,0:T(8,128)(2,1)S(1)} %collective-permute-done.2.refs_2_), channel_id=1, source_target_pairs={{0,8},{8,0},{1,9},{9,1},{2,10},{10,2},{3,11},{11,3},{4,12},{12,4},... | collective-permute-start | bytes 393224 | tf_op jit(solution)/shard_map/ppermute | solution.py:456
  24.5 13.9 %collective-permute-start.5 = (bf16[4,64,256]{2,1,0:T(8,128)(2,1)S(1)}, bf16[4,64,256]{2,1,0:T(8,128)(2,1)S(1)}, u32[]{:S(2)}, u32[]{:S(2)}) collective-permute-start(bf16[4,64,256]{2,1,0:T(8,128)(2,1)S(1)} %collective-permute-done.4.refs_4_), channel_id=1, source_target_pairs={{0,8},{8,0},{1,9},{9,1},{2,10},{10,2},{3,11},{11,3},{4,12},{12,4},... | collective-permute-start | bytes 393224 | tf_op jit(solution)/shard_map/ppermute | solution.py:456
  32.4 6.7 %collective-permute-start.10 = (bf16[4,64,256]{2,1,0:T(8,128)(2,1)S(1)}, bf16[4,64,256]{2,1,0:T(8,128)(2,1)S(1)}, u32[]{:S(2)}, u32[]{:S(2)}) collective-permute-start(bf16[4,64,256]{2,1,0:T(8,128)(2,1)S(1)} %collective-permute-done.9.refs_2_), channel_id=1, source_target_pairs={{0,8},{8,0},{1,9},{9,1},{2,10},{10,2},{3,11},{11,3},{4,12},{12,4},... | collective-permute-start | bytes 393224 | tf_op jit(solution)/shard_map/ppermute | solution.py:456
  33.9 6.3 %collective-permute-start.12 = (bf16[4,64,256]{2,1,0:T(8,128)(2,1)S(1)}, bf16[4,64,256]{2,1,0:T(8,128)(2,1)S(1)}, u32[]{:S(2)}, u32[]{:S(2)}) collective-permute-start(bf16[4,64,256]{2,1,0:T(8,128)(2,1)S(1)} %collective-permute-done.11.refs_4_), channel_id=1, source_target_pairs={{0,8},{8,0},{1,9},{9,1},{2,10},{10,2},{3,11},{11,3},{4,12},{12,4},... | collective-permute-start | bytes 393224 | tf_op jit(solution)/shard_map/ppermute | solution.py:456
  34.4 7.2 %collective-permute-start.8 = (bf16[4,64,256]{2,1,0:T(8,128)(2,1)S(1)}, bf16[4,64,256]{2,1,0:T(8,128)(2,1)S(1)}, u32[]{:S(2)}, u32[]{:S(2)}) collective-permute-start(bf16[4,64,256]{2,1,0:T(8,128)(2,1)S(1)} %collective-permute-done.7.refs_0_), channel_id=1, source_target_pairs={{0,8},{8,0},{1,9},{9,1},{2,10},{10,2},{3,11},{11,3},{4,12},{12,4},... | collective-permute-start | bytes 393224 | tf_op jit(solution)/shard_map/ppermute | solution.py:456
  38.4 3.9 %copy-start = (bf16[256,256]{1,0:T(8,128)(2,1)S(1)}, bf16[256,256]{1,0:T(8,128)(2,1)}, u32[]{:S(2)}) copy-start(bf16[256,256]{1,0:T(8,128)(2,1)} %constant.168.clone.refs_4_.refs_5_) | copy-start | bytes 393220
  38.4 3.9 %copy-start.1 = (bf16[256,256]{1,0:T(8,128)(2,1)S(1)}, bf16[256,256]{1,0:T(8,128)(2,1)}, u32[]{:S(2)}) copy-start(bf16[256,256]{1,0:T(8,128)(2,1)} %constant.169.clone.refs_5_.refs_6_) | copy-start | bytes 393220
  38.4 3.9 %copy-start.2 = (bf16[256,256]{1,0:T(8,128)(2,1)S(1)}, bf16[256,256]{1,0:T(8,128)(2,1)}, u32[]{:S(2)}) copy-start(bf16[256,256]{1,0:T(8,128)(2,1)} %constant.170.clone.refs_6_.refs_7_) | copy-start | bytes 393220
  38.4 3.9 %copy-start.3 = (bf16[256,256]{1,0:T(8,128)(2,1)S(1)}, bf16[256,256]{1,0:T(8,128)(2,1)}, u32[]{:S(2)}) copy-start(bf16[256,256]{1,0:T(8,128)(2,1)} %constant.171.clone.refs_7_.refs_8_) | copy-start | bytes 393220
  47.8 2.0 %collective-permute-start.15 = (bf16[4,256,256]{2,1,0:T(8,128)(2,1)S(1)}, bf16[4,256,256]{2,1,0:T(8,128)(2,1)S(1)}, u32[]{:S(2)}, u32[]{:S(2)}) collective-permute-start(bf16[4,256,256]{2,1,0:T(8,128)(2,1)S(1)} %get-tuple-element.32.v_ref), channel_id=1, source_target_pairs={{0,4},{4,0},{1,5},{5,1},{2,6},{6,2},{3,7},{7,3},{8,12},{12,8},{9,1... | collective-permute-start | bytes 1572872 | tf_op jit(solution)/shard_map/ppermute | solution.py:611
  56.8 2.0 %collective-permute-start.16 = (bf16[4,256,256]{2,1,0:T(8,128)(2,1)S(1)}, bf16[4,256,256]{2,1,0:T(8,128)(2,1)S(1)}, u32[]{:S(2)}, u32[]{:S(2)}) collective-permute-start(bf16[4,256,256]{2,1,0:T(8,128)(2,1)S(1)} %get-tuple-element.37), channel_id=1, source_target_pairs={{0,4},{4,0},{1,5},{5,1},{2,6},{6,2},{3,7},{7,3},{8,12},{12,8},{9,1... | collective-permute-start | bytes 1572872 | tf_op jit(solution)/shard_map/ppermute | solution.py:611
  64.1 2.0 %collective-permute-start.17 = (bf16[4,256,256]{2,1,0:T(8,128)(2,1)S(1)}, bf16[4,256,256]{2,1,0:T(8,128)(2,1)S(1)}, u32[]{:S(2)}, u32[]{:S(2)}) collective-permute-start(bf16[4,256,256]{2,1,0:T(8,128)(2,1)S(1)} %get-tuple-element.38.v_ref), channel_id=1, source_target_pairs={{0,4},{4,0},{1,5},{5,1},{2,6},{6,2},{3,7},{7,3},{8,12},{12,8},{9,1... | collective-permute-start | bytes 1572872 | tf_op jit(solution)/shard_map/ppermute | solution.py:611
  73.0 2.0 %collective-permute-start.18 = (bf16[4,256,256]{2,1,0:T(8,128)(2,1)S(1)}, bf16[4,256,256]{2,1,0:T(8,128)(2,1)S(1)}, u32[]{:S(2)}, u32[]{:S(2)}) collective-permute-start(bf16[4,256,256]{2,1,0:T(8,128)(2,1)S(1)} %get-tuple-element.41), channel_id=1, source_target_pairs={{0,4},{4,0},{1,5},{5,1},{2,6},{6,2},{3,7},{7,3},{8,12},{12,8},{9,1... | collective-permute-start | bytes 1572872 | tf_op jit(solution)/shard_map/ppermute | solution.py:611
  80.3 2.0 %collective-permute-start.19 = (bf16[4,256,256]{2,1,0:T(8,128)(2,1)S(1)}, bf16[4,256,256]{2,1,0:T(8,128)(2,1)S(1)}, u32[]{:S(2)}, u32[]{:S(2)}) collective-permute-start(bf16[4,256,256]{2,1,0:T(8,128)(2,1)S(1)} %get-tuple-element.42.v_ref), channel_id=1, source_target_pairs={{0,4},{4,0},{1,5},{5,1},{2,6},{6,2},{3,7},{7,3},{8,12},{12,8},{9,1... | collective-permute-start | bytes 1572872 | tf_op jit(solution)/shard_map/ppermute | solution.py:611
  89.2 2.0 %collective-permute-start.20 = (bf16[4,256,256]{2,1,0:T(8,128)(2,1)S(1)}, bf16[4,256,256]{2,1,0:T(8,128)(2,1)S(1)}, u32[]{:S(2)}, u32[]{:S(2)}) collective-permute-start(bf16[4,256,256]{2,1,0:T(8,128)(2,1)S(1)} %get-tuple-element.45), channel_id=1, source_target_pairs={{0,4},{4,0},{1,5},{5,1},{2,6},{6,2},{3,7},{7,3},{8,12},{12,8},{9,1... | collective-permute-start | bytes 1572872 | tf_op jit(solution)/shard_map/ppermute | solution.py:611
  96.5 2.0 %collective-permute-start.21 = (bf16[4,256,256]{2,1,0:T(8,128)(2,1)S(1)}, bf16[4,256,256]{2,1,0:T(8,128)(2,1)S(1)}, u32[]{:S(2)}, u32[]{:S(2)}) collective-permute-start(bf16[4,256,256]{2,1,0:T(8,128)(2,1)S(1)} %get-tuple-element.46.v_ref), channel_id=1, source_target_pairs={{0,4},{4,0},{1,5},{5,1},{2,6},{6,2},{3,7},{7,3},{8,12},{12,8},{9,1... | collective-permute-start | bytes 1572872 | tf_op jit(solution)/shard_map/ppermute | solution.py:611
  102.3 1.4 %collective-permute-start.22 = (bf16[4,64,256]{2,1,0:T(8,128)(2,1)S(1)}, bf16[4,64,256]{2,1,0:T(8,128)(2,1)S(1)}, u32[]{:S(2)}, u32[]{:S(2)}) collective-permute-start(bf16[4,64,256]{2,1,0:T(8,128)(2,1)S(1)} %get-tuple-element.49), channel_id=1, source_target_pairs={{0,4},{4,0},{1,5},{5,1},{2,6},{6,2},{3,7},{7,3},{8,12},{12,8},{9,1... | collective-permute-start | bytes 393224 | tf_op jit(solution)/shard_map/ppermute | solution.py:611
  103.8 5.6 %collective-permute-start.23 = (bf16[4,64,256]{2,1,0:T(8,128)(2,1)S(1)}, bf16[4,64,256]{2,1,0:T(8,128)(2,1)S(1)}, u32[]{:S(2)}, u32[]{:S(2)}) collective-permute-start(bf16[4,64,256]{2,1,0:T(8,128)(2,1)S(1)} %select_convert_fusion), channel_id=1, source_target_pairs={{0,16},{16,0},{1,17},{17,1},{2,18},{18,2},{3,19},{19,3},{4,20},{20... | collective-permute-start | bytes 393224 | tf_op jit(solution)/shard_map/ppermute | solution.py:649
  104.5 4.9 %copy-start.8 = (f32[1,4,2,1,64,256]{5,4,3,2,1,0:T(8,128)}, f32[1,4,2,1,64,256]{5,4,3,2,1,0:T(8,128)S(1)}, u32[]{:S(2)}) copy-start(f32[1,4,2,1,64,256]{5,4,3,2,1,0:T(8,128)S(1)} %bitcast_dynamic-update-slice_fusion) | copy-start | bytes 1572868
